TPU v7x, 32 devices: a whole 2x2x4 slice. The times are simulated.
32 devices in a mesh: grp: 2 (over x), ctx: 16 (over z, y, core).
Axes of the slice: x: 2, y: 2, z: 4, core: 2. Of those that a mesh axis runs over, the one named last changes fastest.
Arguments:
- cache_keys: bfloat16 [2048, 512], P(('grp', 'ctx')), parts along dimension 0, may hold values from -4 to 4
- cache_values: bfloat16 [2048, 512], P(('grp', 'ctx')), parts along dimension 0, may hold values from -4 to 4
- new_queries: bfloat16 [2048, 4096], P(('grp', 'ctx')), parts along dimension 0, may hold values from -600 to 600
- new_keys: bfloat16 [2048, 512], P(('grp', 'ctx')), parts along dimension 0, may hold values from -4 to 4
- new_values: bfloat16 [2048, 512], P(('grp', 'ctx')), parts along dimension 0, may hold values from -4 to 4
- cont_queries: bfloat16 [64, 4096], P(('grp', 'ctx')), parts along dimension 0, may hold values from -600 to 600
- suffix_keys: bfloat16 [64, 128, 512], P(('grp', 'ctx')), parts along dimension 0, may hold values from -4 to 4
- suffix_values: bfloat16 [64, 128, 512], P(('grp', 'ctx')), parts along dimension 0, may hold values from -4 to 4
- window_start: int32 [2], P('grp'), parts along dimension 0, may hold values from 0 to 255
- prefix_length: int32 [2], P('grp'), parts along dimension 0, may hold values from 512 to 1024
- suffix_length: int32 [64], P(('grp', 'ctx')), parts along dimension 0, may hold values from 2 to 128
Outputs:
- prompt_out: bfloat16 [2048, 4096], P(('grp', 'ctx')), parts along dimension 0
- cont_out: bfloat16 [64, 4096], P(('grp', 'ctx')), parts along dimension 0
There are 2 independent parts, one for each index of `grp`. A program takes and returns all parts, laid end to end along the dimension named above; each array names one. Nothing has to cross between parts.
All inputs are finite; a program needn't handle non-finite values.
Results may differ from a plain program's by a relative error of at most 0.009.
Values may be sent and summed in bfloat16 or wider, within the bound.
No kernel may reach another device: no remote copies, remote signals or barrier semaphores. Data moves between devices by JAX's collectives and lax.ppermute only.
A program may use at most 192 MiB of HBM per device.

v0:
```python
import jax
import jax.numpy as jnp
from jax import lax
from jax.sharding import PartitionSpec as P

KVH = 4
HD = 128
GROUP = 8


def empty_running(row_count):
    return (
        jnp.full((row_count, KVH, GROUP), -1e30, jnp.float32),
        jnp.zeros((row_count, KVH, GROUP), jnp.float32),
        jnp.zeros((row_count, KVH, GROUP, HD), jnp.float32),
    )


def key_places(begin_row, row_count, cache_rows, prompt_rows, window_first, prefix_last):
    position = begin_row + jnp.arange(row_count, dtype=jnp.int32)
    stride = cache_rows + prompt_rows
    shard_index = position // stride
    within = position % stride
    in_cache = within < cache_rows
    cache_index = shard_index * cache_rows + within
    prompt_index = shard_index * prompt_rows + within - cache_rows
    cache_ok = in_cache & (cache_index >= window_first) & (cache_index < prefix_last)
    return (in_cache, cache_ok, prompt_index)


def attend_piece(running, queries, visible, key_piece, value_piece):
    row_max, row_sum, numerator = running
    count = key_piece.shape[0]
    key_heads = key_piece.reshape(count, KVH, HD)
    value_heads = value_piece.reshape(count, KVH, HD)
    scores = jnp.einsum(
        "rkgd,lkd->rkgl", queries, key_heads, preferred_element_type=jnp.float32
    ) * HD ** (-0.5)
    mask = visible[:, None, None, :]
    scores = jnp.where(mask, scores, -1e30)
    new_max = jnp.maximum(row_max, jnp.max(scores, axis=-1))
    probs = jnp.where(mask, jnp.exp(scores - new_max[..., None]), 0.0)
    row_sum = jnp.sum(probs, axis=-1)
    numerator = jnp.einsum(
        "rkgl,lkd->rkgd",
        probs.astype(jnp.bfloat16),
        value_heads,
        preferred_element_type=jnp.float32,
    )
    return (new_max, row_sum, numerator)


def combine_states(stacked, suffix_state):
    stack_max, stack_sum, stack_numer = stacked
    suffix_max, suffix_sum, suffix_numer = suffix_state
    highest = jnp.maximum(jnp.max(stack_max, axis=0), suffix_max)
    stack_weight = jnp.exp(stack_max - highest)
    suffix_weight = jnp.exp(suffix_max - highest)
    numerator = (
        jnp.sum(stack_numer * stack_weight[..., None], axis=0)
        + suffix_numer * suffix_weight[..., None]
    )
    denominator = jnp.sum(stack_sum * stack_weight, axis=0) + suffix_sum * suffix_weight
    return numerator / denominator[..., None]


def body(
    cache_keys,
    cache_values,
    new_queries,
    new_keys,
    new_values,
    cont_queries,
    suffix_keys,
    suffix_values,
    window_start,
    prefix_length,
    suffix_length,
):
    cache_rows = cache_keys.shape[0]
    prompt_rows = new_keys.shape[0]
    window_first = window_start[0]
    prefix_last = prefix_length[0]
    device_place = lax.axis_index("ctx")
    query_index = device_place * prompt_rows + jnp.arange(prompt_rows, dtype=jnp.int32)
    prompt_heads = new_queries.reshape(prompt_rows, KVH, GROUP, HD)
    local_keys = jnp.concatenate([cache_keys, new_keys], axis=0)
    local_values = jnp.concatenate([cache_values, new_values], axis=0)
    cont_count = cont_queries.shape[0]
    cont_heads = cont_queries.reshape(cont_count, KVH, GROUP, HD)
    suffix_rows = suffix_keys.shape[1]
    own_keys = suffix_keys.reshape(cont_count, suffix_rows, KVH, HD)
    own_values = suffix_values.reshape(cont_count, suffix_rows, KVH, HD)
    suffix_scores = jnp.einsum(
        "ckgd,cskd->ckgs", cont_heads, own_keys, preferred_element_type=jnp.float32
    ) * HD ** (-0.5)
    suffix_mask = (jnp.arange(suffix_rows, dtype=jnp.int32)[None, :] < suffix_length[:, None])[
        :, None, None, :
    ]
    suffix_scores = jnp.where(suffix_mask, suffix_scores, -1e30)
    suffix_max = jnp.max(suffix_scores, axis=-1)
    suffix_probs = jnp.where(suffix_mask, jnp.exp(suffix_scores - suffix_max[..., None]), 0.0)
    suffix_sum = jnp.sum(suffix_probs, axis=-1)
    suffix_numer = jnp.einsum(
        "ckgs,cskd->ckgd",
        suffix_probs.astype(jnp.bfloat16),
        own_values,
        preferred_element_type=jnp.float32,
    )
    suffix_state = (suffix_max, suffix_sum, suffix_numer)
    key_piece = lax.all_gather(local_keys, "ctx", axis=0, tiled=True)
    in_cache, cache_ok, prompt_index = key_places(
        jnp.int32(0), key_piece.shape[0], cache_rows, prompt_rows, window_first, prefix_last
    )
    visible = cache_ok[None, :] | (~in_cache)[None, :] & (
        prompt_index[None, :] <= query_index[:, None]
    )
    prompt_state = attend_piece(
        empty_running(prompt_rows),
        prompt_heads,
        visible,
        key_piece,
        lax.all_gather(local_values, "ctx", axis=0, tiled=True),
    )
    every_query = lax.all_gather(cont_queries, "ctx", axis=0, tiled=True)
    every_count = every_query.shape[0]
    every_heads = every_query.reshape(every_count, KVH, GROUP, HD)
    in_cache, cache_ok, prompt_index = key_places(
        device_place * (cache_rows + prompt_rows),
        local_keys.shape[0],
        cache_rows,
        prompt_rows,
        window_first,
        prefix_last,
    )
    visible = (cache_ok | ~in_cache)[None, :]
    local_max, local_sum, local_numer = attend_piece(
        empty_running(every_count), every_heads, visible, local_keys, local_values
    )
    exchanged = (
        lax.all_to_all(local_numer[None], "ctx", split_axis=1, concat_axis=0, tiled=True),
        lax.all_to_all(local_max[None], "ctx", split_axis=1, concat_axis=0, tiled=True),
        lax.all_to_all(local_sum[None], "ctx", split_axis=1, concat_axis=0, tiled=True),
    )
    stacked = (exchanged[1], exchanged[2], exchanged[0])
    prompt_max, prompt_sum, prompt_numer = prompt_state
    prompt_out = (
        (prompt_numer / prompt_sum[..., None])
        .reshape(prompt_rows, new_queries.shape[1])
        .astype(jnp.bfloat16)
    )
    cont_out = (
        combine_states(stacked, suffix_state)
        .reshape(cont_count, cont_queries.shape[1])
        .astype(jnp.bfloat16)
    )
    return (prompt_out, cont_out)


def solution(mesh):
    in_specs = (
        P(("grp", "ctx"), None),
        P(("grp", "ctx"), None),
        P(("grp", "ctx"), None),
        P(("grp", "ctx"), None),
        P(("grp", "ctx"), None),
        P(("grp", "ctx"), None),
        P(("grp", "ctx"), None, None),
        P(("grp", "ctx"), None, None),
        P("grp"),
        P("grp"),
        P(("grp", "ctx")),
    )
    out_specs = (P(("grp", "ctx"), None), P(("grp", "ctx"), None))
    return jax.shard_map(body, mesh=mesh, in_specs=in_specs, out_specs=out_specs, check_vma=False)
```

profile of v0, /device:TPU:0, one launch (start us, length us, event | category | flops | bytes accessed | tf_op | source)
XLA Modules:
  0.0 118.5 jit_solution(2128454379710857456)
XLA Ops:
  7.2 0.0 copy-start
  7.2 0.0 all-gather.6.cloned.1.call-start
  7.2 1.0 copy.85
  8.2 1.0 copy.86
  9.2 0.8 pad_maximum_fusion.1
  10.0 0.0 all-gather.6.cloned.1.call-update
  11.3 24.1 %all-gather = bf16[16,2,4096]{2,1,0:T(2,128)(2,1)S(1)} all-gather(bf16[1,2,4096]{2,1,0:T(2,128)(2,1)} %bitcast.110), channel_id=1, replica_groups=mesh['grp'=2,'ctx'=16] {'ctx'}, dimensions={0}, use_global_device_ids=true | all-gather | bytes 278528 | tf_op jit(solution)/shard_map/all_gather | solution.py:125
  35.4 0.2 reshape.240
  35.7 1.3 %fusion.56 = (f32[32,4,8]{0,2,1:T(8,128)S(1)}, f32[32,4,8,128]{3,0,2,1:T(8,128)S(1)}) fusion(bf16[128,4,128,1]{0,2,3,1:T(8,128)(2,1)} %bitcast.103, bf16[32,4,8,128]{3,2,1,0:T(8,128)(2,1)S(1)} %reshape.240, pred[128]{0:T(512)(128)(4,1)S(1)} %not_or_fusion), kind=kOutput, calls=%fused_computation.85 | convolution fusion | flops 33946624 | bytes 921728 | tf_op jit(solution)/shard_map/rkgd,lkd->rkgl/dot_general | solution.py:36
  37.0 0.4 fusion.21
  37.3 0.7 copy.104
  38.1 3.5 %all-to-all-start.2 = ((f32[1,32,4,8]{3,2,0,1:T(4,128)}), f32[1,32,4,8]{3,2,0,1:T(4,128)S(1)}, u32[]{:S(2)}, u32[]{:S(2)}) async-start(f32[1,32,4,8]{3,2,0,1:T(4,128)} %copy.104), calls=%async_computation.2 | async-start | bytes 131072 | tf_op jit(solution)/shard_map/all_to_all | solution.py:143
  41.6 0.0 all-gather.4.cloned.1.call-start
  41.6 1.0 copy.83
  42.6 1.0 copy.84
  43.5 0.8 pad_maximum_fusion
  44.3 0.0 all-gather.4.cloned.1.call-update
  44.3 0.7 iota_compare_fusion
  45.1 1.2 %convolution_bitcast_fusion = f32[1,32,4,8,128]{4,1,3,2,0:T(8,128)S(1)} fusion(bf16[128,4,128,1]{0,2,3,1:T(8,128)(2,1)} %bitcast.104, f32[32,4,8,128]{3,0,2,1:T(8,128)S(1)} %get-tuple-element.11, f32[32,4,8]{0,2,1:T(8,128)S(1)} %get-tuple-element.7, pred[128]{0:T(512)(128)(4,1)S(1)} %not_or_fusion), kind=kOutput, calls=%fused_computation.8 | convolution fusion | flops 33947648 | bytes 1183872 | tf_op jit(solution)/shard_map/rkgl,lkd->rkgd/dot_general | solution.py:44
  46.3 0.0 copy-done
  46.3 1.1 fusion.57
  47.4 0.2 fusion.32
  47.6 0.7 copy.95
  48.3 1.3 %all-to-all-done.2 = f32[1,32,4,8]{3,2,0,1:T(4,128)S(1)} async-done(((f32[1,32,4,8]{3,2,0,1:T(4,128)}), f32[1,32,4,8]{3,2,0,1:T(4,128)S(1)}, u32[]{:S(2)}, u32[]{:S(2)}) %all-to-all-start.2) | async-done | bytes 4128 | tf_op jit(solution)/shard_map/all_to_all | solution.py:143
  49.5 4.7 %all-to-all-start.1 = ((f32[1,32,4,8]{3,2,0,1:T(4,128)}), f32[1,32,4,8]{3,2,0,1:T(4,128)S(1)}, u32[]{:S(2)}, u32[]{:S(2)}) async-start(f32[1,32,4,8]{3,2,0,1:T(4,128)} %copy.95), calls=%async_computation.1 | async-start | bytes 131072 | tf_op jit(solution)/shard_map/all_to_all | solution.py:142
  54.2 1.1 copy.94
  55.3 1.1 copy.121
  56.5 4.6 %all-to-all-done.1 = f32[1,32,4,8]{3,2,0,1:T(4,128)S(1)} async-done(((f32[1,32,4,8]{3,2,0,1:T(4,128)}), f32[1,32,4,8]{3,2,0,1:T(4,128)S(1)}, u32[]{:S(2)}, u32[]{:S(2)}) %all-to-all-start.1) | async-done | bytes 4128 | tf_op jit(solution)/shard_map/all_to_all | solution.py:142
  61.1 3.6 %all-to-all-start = ((f32[1,32,4,8,128]{4,3,2,0,1:T(8,128)}), f32[1,32,4,8,128]{4,3,2,0,1:T(8,128)S(1)}, u32[]{:S(2)}, u32[]{:S(2)}) async-start(f32[1,32,4,8,128]{4,3,2,0,1:T(8,128)} %copy.94), calls=%async_computation | async-start | bytes 1048576 | tf_op jit(solution)/shard_map/all_to_all | solution.py:141
  64.7 0.2 and_or_fusion
  65.0 0.1 multiply_reduce_fusion
  65.1 0.5 copy.100
  65.5 16.9 %all-to-all-done = f32[1,32,4,8,128]{4,3,2,0,1:T(8,128)S(1)} async-done(((f32[1,32,4,8,128]{4,3,2,0,1:T(8,128)}), f32[1,32,4,8,128]{4,3,2,0,1:T(8,128)S(1)}, u32[]{:S(2)}, u32[]{:S(2)}) %all-to-all-start) | async-done | bytes 524320 | tf_op jit(solution)/shard_map/all_to_all | solution.py:141
  82.4 0.7 fusion.18
  83.1 1.2 %fusion.15 = bf16[1,2,32,128]{3,2,1,0:T(8,128)(2,1)S(1)} fusion(f32[2,4,8,128]{3,0,2,1:T(2,128)S(1)} %fusion.18, f32[2,4,8,128]{3,2,1,0:T(8,128)S(1)} %get-tuple-element.13, f32[2,4,8]{2,1,0:T(4,128)S(1)} %get-tuple-element.2, f32[2,4,8]{2,1,0:T(4,128)S(1)} %get-tuple-element.3, f32[2,4,8]{2,1,0:T(4,128)S(1)} %get-tuple-element.12, ...), kind=kOutput, calls=%fused_computation.18 | convolution fusion | flops 2154496 | bytes 345088 | tf_op jit(solution)/shard_map/ckgs,cskd->ckgd/dot_general | solution.py:104
  84.3 0.6 copy.161
  85.0 0.0 all-gather.6.cloned.1.call-done
  85.0 4.6 %fusion = (f32[64,4,8]{0,2,1:T(8,128)S(1)}, f32[4,2048,64,8]{1,2,3,0:T(8,128)S(1)}) fusion(pred[64,2048]{1,0:T(8,128)(4,1)S(1)} %and_or_fusion, bf16[2048,4,128,1]{0,2,3,1:T(8,128)(2,1)} %bitcast.102, bf16[64,4,8,128]{3,2,1,0:T(8,128)(2,1)S(1)} %bitcast.99), kind=kOutput, calls=%fused_computation.2 | convolution fusion | flops 1086322688 | bytes 19537920 | tf_op jit(solution)/shard_map/rkgd,lkd->rkgl/dot_general | solution.py:36
  89.6 0.0 copy-start.1
  89.6 5.7 %copy-done.1 = f32[4,2048,64,8]{1,2,3,0:T(8,128)} copy-done((f32[4,2048,64,8]{1,2,3,0:T(8,128)}, f32[4,2048,64,8]{1,2,3,0:T(8,128)S(1)}, u32[]{:S(2)}) %copy-start.1) | copy-done | bytes 16777240
  95.3 5.1 %fusion.1 = f32[64,4,8]{0,2,1:T(8,128)S(1)} fusion(f32[4,2048,64,8]{1,2,3,0:T(8,128)S(1)} %get-tuple-element.9, f32[64,4,8]{0,2,1:T(8,128)S(1)} %broadcast_maximum_fusion.1, pred[64,2048]{1,0:T(8,128)(4,1)S(1)} %and_or_fusion), kind=kLoop, calls=%fused_computation.3 | loop fusion | flops 20969472 | bytes 16924672 | tf_op jit(solution)/shard_map/reduce_sum | solution.py:43
  100.4 1.6 %all-gather.4.cloned.1.call-done = bf16[2048,512]{0,1:T(8,128)(2,1)} async-done(((bf16[128,512]{0,1:T(8,128)(2,1)}), bf16[2048,512]{0,1:T(8,128)(2,1)}) %all-gather.4.cloned.1.call-update) | async-done | bytes 2097168 | tf_op jit(solution)/shard_map/all_gather | solution.py:123
  102.0 8.3 %divide_convert_fusion = bf16[64,4,8,128]{3,0,2,1:T(8,128)(2,1)S(1)} fusion(bf16[2048,4,128,1]{0,2,3,1:T(8,128)(2,1)} %bitcast.114, f32[4,2048,64,8]{1,2,3,0:T(8,128)} %copy-done.1, f32[64,4,8]{0,2,1:T(8,128)S(1)} %broadcast_maximum_fusion.1, pred[64,2048]{1,0:T(8,128)(4,1)S(1)} %and_or_fusion, f32[64,4,8]{0,2,1:T(8,128)S(1)} %fusion.1), kind=kOutput, calls=%fused_computation.19 | convolution fusion | flops 1095237632 | bytes 19546112 | tf_op jit(solution)/shard_map/rkgl,lkd->rkgd/dot_general | solution.py:44
  110.3 0.3 copy.90
  110.7 1.0 copy.160
  (12 shorter events, 0.1 us)
Async XLA Ops:
  7.2 39.1 %copy-start = (bf16[2,128,512]{2,1,0:T(8,128)(2,1)S(1)}, bf16[2,128,512]{2,1,0:T(8,128)(2,1)}, u32[]{:S(2)}) copy-start(bf16[2,128,512]{2,1,0:T(8,128)(2,1)} %param.17) | copy-start | bytes 786436
  7.2 77.8 %all-gather.6.cloned.1.call-start = ((), (), s32[]{:S(2)}) async-start(), calls=%async_computation.4 | async-start | bytes 2228224 | tf_op jit(solution)/shard_map/all_gather | solution.py:111
  38.1 11.5 %all-to-all-start.2 = ((f32[1,32,4,8]{3,2,0,1:T(4,128)}), f32[1,32,4,8]{3,2,0,1:T(4,128)S(1)}, u32[]{:S(2)}, u32[]{:S(2)}) async-start(f32[1,32,4,8]{3,2,0,1:T(4,128)} %copy.104), calls=%async_computation.2 | async-start | bytes 131072 | tf_op jit(solution)/shard_map/all_to_all | solution.py:143
  41.6 60.4 %all-gather.4.cloned.1.call-start = ((), (), s32[]{:S(2)}) async-start(), calls=%async_computation.3 | async-start | bytes 2228224 | tf_op jit(solution)/shard_map/all_gather | solution.py:123
  49.5 11.6 %all-to-all-start.1 = ((f32[1,32,4,8]{3,2,0,1:T(4,128)}), f32[1,32,4,8]{3,2,0,1:T(4,128)S(1)}, u32[]{:S(2)}, u32[]{:S(2)}) async-start(f32[1,32,4,8]{3,2,0,1:T(4,128)} %copy.95), calls=%async_computation.1 | async-start | bytes 131072 | tf_op jit(solution)/shard_map/all_to_all | solution.py:142
  61.1 21.3 %all-to-all-start = ((f32[1,32,4,8,128]{4,3,2,0,1:T(8,128)}), f32[1,32,4,8,128]{4,3,2,0,1:T(8,128)S(1)}, u32[]{:S(2)}, u32[]{:S(2)}) async-start(f32[1,32,4,8,128]{4,3,2,0,1:T(8,128)} %copy.94), calls=%async_computation | async-start | bytes 1048576 | tf_op jit(solution)/shard_map/all_to_all | solution.py:141
  89.6 5.7 %copy-start.1 = (f32[4,2048,64,8]{1,2,3,0:T(8,128)}, f32[4,2048,64,8]{1,2,3,0:T(8,128)S(1)}, u32[]{:S(2)}) copy-start(f32[4,2048,64,8]{1,2,3,0:T(8,128)S(1)} %get-tuple-element.9) | copy-start | bytes 50331652
Sparse Core Ops, SparseCore 0:
  10.1 44.8 all-gather.5
  57.2 44.6 all-gather.3
where the time goes:
time: 119 us
  waiting for transfers between devices  24.4 us (21%)
  blocking collectives  24.1 us (20%)
  matrix products  17.7 us (15%)
  local copies, waits for them, and re-layouts  15.9 us (13%)
  between operations  15.6 us (13%)
  starting transfers between devices  11.8 us (10%)
  other arithmetic  8.98 us (8%)
    all_gather x1, blocking collectives, body(): every_query = lax.all_gather(cont_queries, 'ctx', axis=0, tiled=True)  24.1 us
    all_to_all x1, waiting for transfers between devices, body(): lax.all_to_all(local_numer[None], 'ctx', split_axis=1, concat_axis=0, til...  16.9 us
    unnamed x11, local copies, waits for them, and re-layouts  12.3 us
    dot_general x2, matrix products, attend_piece(): jnp.einsum('rkgl,lkd->rkgd', probs.astype(jnp.bfloat16), value_heads, pre...  9.58 us
    dot_general x2, matrix products, attend_piece(): jnp.einsum('rkgd,lkd->rkgl', queries, key_heads, preferred_element_type=j...  5.89 us
    reduce_sum x2, other arithmetic, attend_piece(): row_sum = jnp.sum(probs, axis=-1)  5.49 us
    all_to_all x1, starting transfers between devices, body(): lax.all_to_all(local_max[None], 'ctx', split_axis=1, concat_axis=0, tiled...  4.68 us
    all_to_all x1, waiting for transfers between devices, body(): lax.all_to_all(local_max[None], 'ctx', split_axis=1, concat_axis=0, tiled...  4.64 us
  transfers between devices with their start and end apart: 5, of which 4 were waited for; matrix products, arithmetic and copies ran while one was open for 21% of the time, Pallas kernels for 0%

commit v1 on v0

v1 whole, which is shorter than its diff:
```python
import functools

import jax
import jax.numpy as jnp
from jax import lax
from jax.experimental import pallas as pl
from jax.experimental.pallas import tpu as pltpu
from jax.sharding import PartitionSpec as P

KVH = 4
HD = 128
GROUP = 8
SCALE = HD ** (-0.5)
MASKED = -1e30
FLOOR = -1e20
FAR = 1 << 29

VMEM = pl.BlockSpec(memory_space=pltpu.VMEM)
SMEM = pl.BlockSpec(memory_space=pltpu.SMEM)


def ring_chip(place, chips):
    return jnp.where(place < chips // 2, 2 * place, 2 * (chips - 1 - place) + 1)


def ring_place(chip, chips):
    return jnp.where(chip % 2 == 0, chip // 2, chips - 1 - chip // 2)


def ring_pairs(size):
    chips = size // 2
    order = list(range(0, chips, 2)) + list(range(chips - 1, 0, -2))
    place = {chip: index for index, chip in enumerate(order)}
    pairs = []
    for device in range(size):
        chip, core = divmod(device, 2)
        step = 1 if core == 0 else -1
        pairs.append((device, 2 * order[(place[chip] + step) % chips] + core))
    return pairs


def block_origin(device, hop, swapped, partner, size):
    chips = size // 2
    chip, core = device // 2, device % 2
    via = 1 - core if swapped else core
    held = 1 - via if partner else via
    place = ring_place(chip, chips) + jnp.where(via == 0, -hop, hop)
    place = lax.rem(place + 2 * chips, chips)
    return 2 * ring_chip(place, chips) + held


def attend(device, origins, blocks, limits, window, cache_rows, prompt_rows, g, q, state):
    row_max, row_sum, total = state
    keys = cache_rows + prompt_rows
    cols = slice(g * HD, (g + 1) * HD)
    lane = lax.broadcasted_iota(jnp.int32, (1, keys), 1)
    first, last = window
    scores = []
    for origin, block in zip(origins, blocks):
        s = lax.dot_general(
            q, block[:keys, cols], (((1,), (1,)), ((), ())), preferred_element_type=jnp.float32
        )
        at = origin * cache_rows + lane
        cached = jnp.where((at >= first) & (at < last), -1, FAR)
        column = jnp.where(lane < cache_rows, cached, origin * prompt_rows + lane - cache_rows)
        scores.append(jnp.where(column <= limits, s, MASKED))
    high = functools.reduce(jnp.maximum, scores)
    new_max = jnp.maximum(row_max, jnp.max(high, axis=1, keepdims=True))
    weights = [jnp.exp((s - new_max) * SCALE) for s in scores]
    scale_old = jnp.exp((row_max - new_max) * SCALE)
    row_sum = row_sum * scale_old + jnp.sum(
        functools.reduce(jnp.add, weights), axis=1, keepdims=True
    )
    p = jnp.concatenate([w.astype(jnp.bfloat16) for w in weights], axis=1)
    v = jnp.concatenate([block[keys:, cols] for block in blocks], axis=0)
    total = total * scale_old + jnp.dot(p, v, preferred_element_type=jnp.float32)
    return new_max, row_sum, total


def row_limits(device, prompt_rows, cont_rows):
    row = lax.broadcasted_iota(jnp.int32, (GROUP * prompt_rows + cont_rows, 1), 0)
    own = device * prompt_rows + lax.rem(row, prompt_rows)
    return jnp.where(row < GROUP * prompt_rows, own, FAR - 1)


def first_kernel(
    size, cache_rows, prompt_rows, cont_count,
    first_ref, last_ref, length_ref, query_ref, cont_ref, suffix_key_ref, suffix_value_ref, *refs
):
    blocks, (q_ref, max_ref, sum_ref, total_ref) = refs[:-4], refs[-4:]
    device = lax.axis_index("ctx")
    window = (first_ref[0], last_ref[0])
    rows = GROUP * prompt_rows
    suffix_rows = suffix_key_ref.shape[1]
    lane = lax.broadcasted_iota(jnp.int32, (1, suffix_rows), 1)
    limits = row_limits(device, prompt_rows, GROUP * cont_count)
    cont = cont_ref[...].astype(jnp.float32)
    for g in range(KVH):
        heads = [slice((g * GROUP + h) * HD, (g * GROUP + h + 1) * HD) for h in range(GROUP)]
        cont_q = jnp.concatenate(
            [cont[c : c + 1, head] for c in range(cont_count) for head in heads], axis=0
        ).astype(jnp.bfloat16)
        q = jnp.concatenate([query_ref[:, head] for head in heads] + [cont_q], axis=0)
        q_ref[g] = q
        cols = slice(g * HD, (g + 1) * HD)
        maxes, sums, totals = [], [], []
        for c in range(cont_count):
            s = lax.dot_general(
                cont_q, suffix_key_ref[c, :, cols], (((1,), (1,)), ((), ())),
                preferred_element_type=jnp.float32,
            )[c * GROUP : (c + 1) * GROUP]
            s = jnp.where(lane < length_ref[c], s, MASKED)
            high = jnp.maximum(jnp.max(s, axis=1, keepdims=True), FLOOR)
            w = jnp.exp((s - high) * SCALE)
            maxes.append(high)
            sums.append(jnp.sum(w, axis=1, keepdims=True))
            totals.append(
                jnp.dot(
                    w.astype(jnp.bfloat16), suffix_value_ref[c, :, cols],
                    preferred_element_type=jnp.float32,
                )
            )
        state = (
            jnp.concatenate([jnp.full((rows, 1), FLOOR, jnp.float32)] + maxes, axis=0),
            jnp.concatenate([jnp.zeros((rows, 1), jnp.float32)] + sums, axis=0),
            jnp.concatenate([jnp.zeros((rows, HD), jnp.float32)] + totals, axis=0),
        )
        origins = [block_origin(device, 0, False, partner, size) for partner in (False, True)]
        state = attend(
            device, origins, blocks, limits, window, cache_rows, prompt_rows, g, q, state
        )
        max_ref[g] = jnp.broadcast_to(state[0], max_ref.shape[1:])
        sum_ref[g] = jnp.broadcast_to(state[1], sum_ref.shape[1:])
        total_ref[g] = state[2]


def step_kernel(
    size, cache_rows, prompt_rows, cont_count, sources, last_step,
    first_ref, last_ref, q_ref, max_in, sum_in, total_in, *refs
):
    outs = 2 if last_step else 3
    blocks, outs = refs[:-outs], refs[-outs:]
    device = lax.axis_index("ctx")
    window = (first_ref[0], last_ref[0])
    rows = GROUP * prompt_rows
    limits = row_limits(device, prompt_rows, GROUP * cont_count)
    origins = [block_origin(device, *source, size) for source in sources]
    for g in range(KVH):
        state = (max_in[g][:, :1], sum_in[g][:, :1], total_in[g])
        state = attend(
            device, origins, blocks, limits, window, cache_rows, prompt_rows, g, q_ref[g], state
        )
        if not last_step:
            outs[0][g] = jnp.broadcast_to(state[0], outs[0].shape[1:])
            outs[1][g] = jnp.broadcast_to(state[1], outs[1].shape[1:])
            outs[2][g] = state[2]
            continue
        result = state[2] / state[1]
        for h in range(GROUP):
            cols = slice((g * GROUP + h) * HD, (g * GROUP + h + 1) * HD)
            piece = result[h * prompt_rows : (h + 1) * prompt_rows]
            outs[0][:, cols] = piece.astype(jnp.bfloat16)
            rest = [result[rows + c * GROUP + h :][:1] for c in range(cont_count)]
            outs[1][:, cols] = jnp.concatenate(rest, axis=0).astype(jnp.bfloat16)


def cost(rows, keys):
    work = KVH * rows * keys
    return pl.CostEstimate(flops=4 * work * HD, transcendentals=work, bytes_accessed=4 << 20)


def body(
    size,
    cache_keys,
    cache_values,
    new_queries,
    new_keys,
    new_values,
    cont_queries,
    suffix_keys,
    suffix_values,
    window_start,
    prefix_length,
    suffix_length,
):
    cache_rows, prompt_rows, cont_count = (
        cache_keys.shape[0], new_keys.shape[0], cont_queries.shape[0],
    )
    chips = size // 2
    ring = ring_pairs(size)
    pair = [(device, device ^ 1) for device in range(size)]
    send = lambda block, pairs: lax.ppermute(block, "ctx", pairs)

    own = jnp.concatenate([cache_keys, new_keys, cache_values, new_values], axis=0)
    other = send(own, pair)
    rows = GROUP * (prompt_rows + cont_count)
    keys = cache_rows + prompt_rows
    params = pltpu.CompilerParams(vmem_limit_bytes=24 << 20)
    state_shape = [
        jax.ShapeDtypeStruct((KVH, rows, HD), jnp.float32),
        jax.ShapeDtypeStruct((KVH, rows, HD), jnp.float32),
        jax.ShapeDtypeStruct((KVH, rows, HD), jnp.float32),
    ]
    sizes = (size, cache_rows, prompt_rows, cont_count)
    queries, *state = pl.pallas_call(
        functools.partial(first_kernel, *sizes),
        out_shape=[jax.ShapeDtypeStruct((KVH, rows, HD), jnp.bfloat16)] + state_shape,
        in_specs=[SMEM] * 3 + [VMEM] * 6,
        out_specs=[VMEM] * 4,
        compiler_params=params,
        cost_estimate=cost(rows, 3 * keys),
    )(
        window_start, prefix_length, suffix_length, new_queries, cont_queries,
        suffix_keys, suffix_values, own, other,
    )

    def step(state, sources, blocks, last_step=False):
        outs = (
            [jax.ShapeDtypeStruct(new_queries.shape, jnp.bfloat16),
             jax.ShapeDtypeStruct(cont_queries.shape, jnp.bfloat16)]
            if last_step else state_shape
        )
        return pl.pallas_call(
            functools.partial(step_kernel, *sizes, sources, last_step),
            out_shape=outs,
            in_specs=[SMEM] * 2 + [VMEM] * (4 + len(blocks)),
            out_specs=[VMEM] * len(outs),
            input_output_aliases={} if last_step else {3: 0, 4: 1, 5: 2},
            compiler_params=params,
            cost_estimate=cost(rows, len(blocks) * keys),
        )(window_start, prefix_length, queries, *state, *blocks)

    for hop in range(1, chips // 2):
        own, other = send(own, ring), send(other, ring)
        blocks = [own, other, send(own, pair), send(other, pair)]
        sources = [(hop, False, False), (hop, False, True), (hop, True, False), (hop, True, True)]
        state = step(state, sources, blocks)
    own = send(own, ring)
    hop = chips // 2
    sources = [(hop, False, False), (hop, True, False)]
    return tuple(step(state, sources, [own, send(own, pair)], last_step=True))


def solution(mesh):
    in_specs = (
        P(("grp", "ctx"), None),
        P(("grp", "ctx"), None),
        P(("grp", "ctx"), None),
        P(("grp", "ctx"), None),
        P(("grp", "ctx"), None),
        P(("grp", "ctx"), None),
        P(("grp", "ctx"), None, None),
        P(("grp", "ctx"), None, None),
        P("grp"),
        P("grp"),
        P(("grp", "ctx")),
    )
    out_specs = (P(("grp", "ctx"), None), P(("grp", "ctx"), None))
    run = functools.partial(body, mesh.shape["ctx"])
    return jax.shard_map(run, mesh=mesh, in_specs=in_specs, out_specs=out_specs, check_vma=False)
```

time: 119 us -> 72.2 us (0.61)
  Pallas kernels: 0 us -> 35.6 us
  blocking collectives: 24.1 us -> 0 us
  matrix products: 17.7 us -> 0 us
  waiting for transfers between devices: 24.4 us -> 10 us
  between operations: 15.6 us -> 1.96 us
  other arithmetic: 8.98 us -> 0 us
  local copies, waits for them, and re-layouts: 15.9 us -> 7.68 us
  starting transfers between devices: 11.8 us -> 16.4 us
    pallas_call x0 -> x5, Pallas kernels: none -> 35.6 us  [the longest x4 27.8 us: step(): pl.pallas_call(functools.partial(step_kernel, *sizes, sources, last_step)...]
    all_gather x1 -> x0, blocking collectives: 24.1 us -> none  [body(): every_query = lax.all_gather(cont_queries, 'ctx', axis=0, tiled=True)]
    all_to_all x3 -> x0, waiting for transfers between devices: 22.8 us -> none  [the longest x1 16.9 us: body(): lax.all_to_all(local_numer[None], 'ctx', split_axis=1, concat_axis=0, til...]
    dot_general x6 -> x0, matrix products: 17.7 us -> none  [the longest x2 9.58 us: attend_piece(): jnp.einsum('rkgl,lkd->rkgd', probs.astype(jnp.bfloat16), value_heads, pre...]
    ppermute x0 -> x15, starting transfers between devices: none -> 16.4 us  [body(): send = lambda block, pairs: lax.ppermute(block, 'ctx', pairs)]
    all_to_all x3 -> x0, starting transfers between devices: 11.8 us -> none  [the longest x1 4.68 us: body(): lax.all_to_all(local_max[None], 'ctx', split_axis=1, concat_axis=0, tiled...]
    ppermute x0 -> x15, waiting for transfers between devices: none -> 10 us  [body(): send = lambda block, pairs: lax.ppermute(block, 'ctx', pairs)]
    reduce_sum x5 -> x0, other arithmetic: 6.44 us -> none  [the longest x2 5.49 us: attend_piece(): row_sum = jnp.sum(probs, axis=-1)]
  transfers between devices with their start and end apart: 5 -> 15, of which waited for: 4 -> 7; matrix products, arithmetic and copies ran while one was open for 21% -> 0% of each run, Pallas kernels for 0% -> 39%
where the time goes in v1:
time: 72.2 us; the launch traced here: 71.7 us
  Pallas kernels  35.6 us (49%)
  starting transfers between devices  16.4 us (23%)
  waiting for transfers between devices  10 us (14%)
  local copies, waits for them, and re-layouts  7.68 us (11%)
  between operations  1.96 us (3%)
    pallas_call x4, Pallas kernels, step(): pl.pallas_call(functools.partial(step_kernel, *sizes, sources, last_step)...  27.8 us
    ppermute x15, starting transfers between devices, body(): send = lambda block, pairs: lax.ppermute(block, 'ctx', pairs)  16.4 us
    ppermute x15, waiting for transfers between devices, body(): send = lambda block, pairs: lax.ppermute(block, 'ctx', pairs)  10 us
    pallas_call x1, Pallas kernels, body(): pl.pallas_call(functools.partial(first_kernel, *sizes), out_shape=[jax.Sh...  7.76 us
    unnamed x13, local copies, waits for them, and re-layouts  6.84 us
  transfers between devices with their start and end apart: 15, of which 7 were waited for; matrix products, arithmetic and copies ran while one was open for 0% of the time, Pallas kernels for 39%

profile of v1, /device:TPU:0, one launch (start us, length us, event | category | flops | bytes accessed | tf_op | source)
XLA Modules:
  0.0 71.7 jit_solution(17301199310894090655)
XLA Ops:
  0.6 0.8 %constant_dynamic-update-slice_fusion.3 = bf16[256,512]{1,0:T(8,128)(2,1)S(1)} fusion(bf16[64,512]{1,0:T(8,128)(2,1)} %param.11), kind=kLoop, calls=%fused_computation.3 | loop fusion | bytes 131072
  1.5 0.8 %constant_dynamic-update-slice_fusion.2 = bf16[256,512]{1,0:T(8,128)(2,1)S(1)} fusion(bf16[256,512]{1,0:T(8,128)(2,1)S(1)} %constant_dynamic-update-slice_fusion.3, bf16[64,512]{1,0:T(8,128)(2,1)} %param.14), kind=kLoop, calls=%fused_computation.2 | loop fusion | bytes 131072
  2.3 0.8 %constant_dynamic-update-slice_fusion.1 = bf16[256,512]{1,0:T(8,128)(2,1)S(1)} fusion(bf16[256,512]{1,0:T(8,128)(2,1)S(1)} %constant_dynamic-update-slice_fusion.2, bf16[64,512]{1,0:T(8,128)(2,1)} %param.12), kind=kLoop, calls=%fused_computation.1 | loop fusion | bytes 131072
  3.2 0.8 %constant_dynamic-update-slice_fusion.refs_0_ = bf16[256,512]{1,0:T(8,128)(2,1)S(1)} fusion(bf16[256,512]{1,0:T(8,128)(2,1)S(1)} %constant_dynamic-update-slice_fusion.1, bf16[64,512]{1,0:T(8,128)(2,1)} %param.15), kind=kLoop, calls=%fused_computation | loop fusion | bytes 131072 | tf_op jit(solution)/shard_map/concatenate | solution.py:194
  4.0 0.5 collective-permute-start
  4.5 2.6 %collective-permute-start.1 = (bf16[256,512]{1,0:T(8,128)(2,1)S(1)}, bf16[256,512]{1,0:T(8,128)(2,1)S(1)}, u32[]{:S(2)}, u32[]{:S(2)}) collective-permute-start(bf16[256,512]{1,0:T(8,128)(2,1)S(1)} %constant_dynamic-update-slice_fusion.refs_0_), channel_id=1, source_target_pairs={{0,4},{1,3},{2,0},{3,7},{4,8},{5,1},{6,2},{7,11},{8,12},{9,5},{10,... | collective-permute-start | bytes 786440 | tf_op jit(solution)/shard_map/ppermute | solution.py:192
  7.1 0.0 collective-permute-done.refs_1_
  7.1 1.6 %collective-permute-start.2 = (bf16[256,512]{1,0:T(8,128)(2,1)S(1)}, bf16[256,512]{1,0:T(8,128)(2,1)S(1)}, u32[]{:S(2)}, u32[]{:S(2)}) collective-permute-start(bf16[256,512]{1,0:T(8,128)(2,1)S(1)} %collective-permute-done.refs_1_), channel_id=1, source_target_pairs={{0,4},{1,3},{2,0},{3,7},{4,8},{5,1},{6,2},{7,11},{8,12},{9,5},{10,... | collective-permute-start | bytes 786440 | tf_op jit(solution)/shard_map/ppermute | solution.py:192
  8.6 2.7 %collective-permute-done.1.refs_0_ = bf16[256,512]{1,0:T(8,128)(2,1)S(1)} collective-permute-done((bf16[256,512]{1,0:T(8,128)(2,1)S(1)}, bf16[256,512]{1,0:T(8,128)(2,1)S(1)}, u32[]{:S(2)}, u32[]{:S(2)}) %collective-permute-start.1) | collective-permute-done | bytes 262176 | tf_op jit(solution)/shard_map/ppermute | solution.py:192
  11.4 2.1 %collective-permute-start.5 = (bf16[256,512]{1,0:T(8,128)(2,1)S(1)}, bf16[256,512]{1,0:T(8,128)(2,1)S(1)}, u32[]{:S(2)}, u32[]{:S(2)}) collective-permute-start(bf16[256,512]{1,0:T(8,128)(2,1)S(1)} %collective-permute-done.1.refs_0_), channel_id=1, source_target_pairs={{0,4},{1,3},{2,0},{3,7},{4,8},{5,1},{6,2},{7,11},{8,12},{9,5},{10,... | collective-permute-start | bytes 786440 | tf_op jit(solution)/shard_map/ppermute | solution.py:192
  13.4 0.7 %collective-permute-done.2.refs_1_ = bf16[256,512]{1,0:T(8,128)(2,1)S(1)} collective-permute-done((bf16[256,512]{1,0:T(8,128)(2,1)S(1)}, bf16[256,512]{1,0:T(8,128)(2,1)S(1)}, u32[]{:S(2)}, u32[]{:S(2)}) %collective-permute-start.2) | collective-permute-done | bytes 262176 | tf_op jit(solution)/shard_map/ppermute | solution.py:192
  14.2 2.1 %collective-permute-start.6 = (bf16[256,512]{1,0:T(8,128)(2,1)S(1)}, bf16[256,512]{1,0:T(8,128)(2,1)S(1)}, u32[]{:S(2)}, u32[]{:S(2)}) collective-permute-start(bf16[256,512]{1,0:T(8,128)(2,1)S(1)} %collective-permute-done.2.refs_1_), channel_id=1, source_target_pairs={{0,4},{1,3},{2,0},{3,7},{4,8},{5,1},{6,2},{7,11},{8,12},{9,5},{10,... | collective-permute-start | bytes 786440 | tf_op jit(solution)/shard_map/ppermute | solution.py:192
  16.2 1.5 %collective-permute-done.5.refs_0_ = bf16[256,512]{1,0:T(8,128)(2,1)S(1)} collective-permute-done((bf16[256,512]{1,0:T(8,128)(2,1)S(1)}, bf16[256,512]{1,0:T(8,128)(2,1)S(1)}, u32[]{:S(2)}, u32[]{:S(2)}) %collective-permute-start.5) | collective-permute-done | bytes 262176 | tf_op jit(solution)/shard_map/ppermute | solution.py:192
  17.7 2.1 %collective-permute-start.9 = (bf16[256,512]{1,0:T(8,128)(2,1)S(1)}, bf16[256,512]{1,0:T(8,128)(2,1)S(1)}, u32[]{:S(2)}, u32[]{:S(2)}) collective-permute-start(bf16[256,512]{1,0:T(8,128)(2,1)S(1)} %collective-permute-done.5.refs_0_), channel_id=1, source_target_pairs={{0,4},{1,3},{2,0},{3,7},{4,8},{5,1},{6,2},{7,11},{8,12},{9,5},{10,... | collective-permute-start | bytes 786440 | tf_op jit(solution)/shard_map/ppermute | solution.py:192
  19.8 0.0 collective-permute-start.3
  19.8 0.5 collective-permute-start.4
  20.3 0.2 collective-permute-done.6.refs_1_
  20.5 2.1 %collective-permute-start.10 = (bf16[256,512]{1,0:T(8,128)(2,1)S(1)}, bf16[256,512]{1,0:T(8,128)(2,1)S(1)}, u32[]{:S(2)}, u32[]{:S(2)}) collective-permute-start(bf16[256,512]{1,0:T(8,128)(2,1)S(1)} %collective-permute-done.6.refs_1_), channel_id=1, source_target_pairs={{0,4},{1,3},{2,0},{3,7},{4,8},{5,1},{6,2},{7,11},{8,12},{9,5},{10,... | collective-permute-start | bytes 786440 | tf_op jit(solution)/shard_map/ppermute | solution.py:192
  22.6 1.5 %collective-permute-done.9.refs_0_ = bf16[256,512]{1,0:T(8,128)(2,1)S(1)} collective-permute-done((bf16[256,512]{1,0:T(8,128)(2,1)S(1)}, bf16[256,512]{1,0:T(8,128)(2,1)S(1)}, u32[]{:S(2)}, u32[]{:S(2)}) %collective-permute-start.9) | collective-permute-done | bytes 262176 | tf_op jit(solution)/shard_map/ppermute | solution.py:192
  24.1 2.1 %collective-permute-start.13 = (bf16[256,512]{1,0:T(8,128)(2,1)S(1)}, bf16[256,512]{1,0:T(8,128)(2,1)S(1)}, u32[]{:S(2)}, u32[]{:S(2)}) collective-permute-start(bf16[256,512]{1,0:T(8,128)(2,1)S(1)} %collective-permute-done.9.refs_0_), channel_id=1, source_target_pairs={{0,4},{1,3},{2,0},{3,7},{4,8},{5,1},{6,2},{7,11},{8,12},{9,5},{10,... | collective-permute-start | bytes 786440 | tf_op jit(solution)/shard_map/ppermute | solution.py:192
  26.2 0.0 collective-permute-start.7
  26.2 0.0 collective-permute-done.3.refs_2_
  26.2 0.5 collective-permute-start.8
  26.7 0.0 collective-permute-done.4.refs_3_
  26.7 0.1 collective-permute-start.11
  26.8 0.1 collective-permute-done.10.refs_1_
  26.9 0.3 collective-permute-start.12
  27.2 3.3 %collective-permute-done.13.refs_0_ = bf16[256,512]{1,0:T(8,128)(2,1)S(1)} collective-permute-done((bf16[256,512]{1,0:T(8,128)(2,1)S(1)}, bf16[256,512]{1,0:T(8,128)(2,1)S(1)}, u32[]{:S(2)}, u32[]{:S(2)}) %collective-permute-start.13) | collective-permute-done | bytes 262176 | tf_op jit(solution)/shard_map/ppermute | solution.py:192
  30.5 0.0 collective-permute-start.14
  31.8 0.0 copy-start
  31.8 1.0 %copy-done = bf16[64,4096]{1,0:T(8,128)(2,1)S(1)} copy-done((bf16[64,4096]{1,0:T(8,128)(2,1)S(1)}, bf16[64,4096]{1,0:T(8,128)(2,1)}, u32[]{:S(2)}) %copy-start) | copy-done | bytes 524312
  32.8 0.0 copy-start.1
  32.8 0.9 %copy-done.1 = bf16[2,128,512]{2,1,0:T(8,128)(2,1)S(1)} copy-done((bf16[2,128,512]{2,1,0:T(8,128)(2,1)S(1)}, bf16[2,128,512]{2,1,0:T(8,128)(2,1)}, u32[]{:S(2)}) %copy-start.1) | copy-done | bytes 262168
  33.8 0.0 copy-start.2
  33.8 0.9 %copy-done.2 = bf16[2,128,512]{2,1,0:T(8,128)(2,1)S(1)} copy-done((bf16[2,128,512]{2,1,0:T(8,128)(2,1)S(1)}, bf16[2,128,512]{2,1,0:T(8,128)(2,1)}, u32[]{:S(2)}) %copy-start.2) | copy-done | bytes 262168
  34.7 0.0 copy-start.3
  34.7 0.7 copy-done.3
  35.4 0.0 copy-start.4
  35.4 0.7 copy-done.4
  36.1 7.8 %shard_map.122 = (bf16[4,528,128]{2,1,0:T(8,128)(2,1)S(1)}, f32[4,528,128]{2,1,0:T(8,128)S(1)}, f32[4,528,128]{2,1,0:T(8,128)S(1)}, f32[4,528,128]{2,1,0:T(8,128)S(1)}) custom-call(s32[1]{0:T(128)S(6)} %copy.34.first_ref, s32[1]{0:T(128)S(6)} %copy.35.last_ref, s32[2]{0:T(128)S(1)} %copy-done.4, bf16[64,4096]{1,0:T(8,128)(2,1)S(1)} %copy-done, ...), custom_call_target="tpu_custom_call" | custom-call | flops 415236096 | bytes 4194304 | tf_op jit(solution)/shard_map/pallas_call | solution.py:205
  43.9 6.8 %shard_map.123 = (f32[4,528,128]{2,1,0:T(8,128)S(1)}, f32[4,528,128]{2,1,0:T(8,128)S(1)}, f32[4,528,128]{2,1,0:T(8,128)S(1)}) custom-call(s32[1]{0:T(128)S(6)} %copy.34.first_ref, s32[1]{0:T(128)S(6)} %copy.35.last_ref, bf16[4,528,128]{2,1,0:T(8,128)(2,1)S(1)} %get-tuple-element.15.q_ref, ...), custom_call_target="tpu_custom_call", output_to_operand_aliasing={{0}: (3, {}), {1}: (4, {}), {2}: (5, {})} | custom-call | flops 553648128 | bytes 4194304 | tf_op jit(solution)/shard_map/pallas_call | solution.py:223
  50.6 0.0 collective-permute-done.7.refs_2_
  50.6 0.0 collective-permute-done.8.refs_3_
  50.6 7.0 %shard_map.124 = (f32[4,528,128]{2,1,0:T(8,128)S(1)}, f32[4,528,128]{2,1,0:T(8,128)S(1)}, f32[4,528,128]{2,1,0:T(8,128)S(1)}) custom-call(s32[1]{0:T(128)S(6)} %copy.34.first_ref, s32[1]{0:T(128)S(6)} %copy.35.last_ref, bf16[4,528,128]{2,1,0:T(8,128)(2,1)S(1)} %get-tuple-element.15.q_ref, ...), custom_call_target="tpu_custom_call", output_to_operand_aliasing={{0}: (3, {}), {1}: (4, {}), {2}: (5, {})} | custom-call | flops 553648128 | bytes 4194304 | tf_op jit(solution)/shard_map/pallas_call | solution.py:223
  57.6 0.0 collective-permute-done.11.refs_2_
  57.6 0.0 collective-permute-done.12.refs_3_
  57.6 6.8 %shard_map.125 = (f32[4,528,128]{2,1,0:T(8,128)S(1)}, f32[4,528,128]{2,1,0:T(8,128)S(1)}, f32[4,528,128]{2,1,0:T(8,128)S(1)}) custom-call(s32[1]{0:T(128)S(6)} %copy.34.first_ref, s32[1]{0:T(128)S(6)} %copy.35.last_ref, bf16[4,528,128]{2,1,0:T(8,128)(2,1)S(1)} %get-tuple-element.15.q_ref, ...), custom_call_target="tpu_custom_call", output_to_operand_aliasing={{0}: (3, {}), {1}: (4, {}), {2}: (5, {})} | custom-call | flops 553648128 | bytes 4194304 | tf_op jit(solution)/shard_map/pallas_call | solution.py:223
  64.4 0.0 collective-permute-done.14.refs_1_
  64.4 7.3 %shard_map.126 = (bf16[64,4096]{1,0:T(8,128)(2,1)}, bf16[2,4096]{1,0:T(2,128)(2,1)}) custom-call(s32[1]{0:T(128)S(6)} %copy.34.first_ref, s32[1]{0:T(128)S(6)} %copy.35.last_ref, bf16[4,528,128]{2,1,0:T(8,128)(2,1)S(1)} %get-tuple-element.15.q_ref, f32[4,528,128]{2,1,0:T(8,128)S(1)} %get-tuple-element.25.max_in, ...), custom_call_target="tpu_custom_call" | custom-call | flops 276824064 | bytes 4194304 | tf_op jit(solution)/shard_map/pallas_call | solution.py:223
Async XLA Ops:
  4.0 3.1 %collective-permute-start = (bf16[256,512]{1,0:T(8,128)(2,1)S(1)}, bf16[256,512]{1,0:T(8,128)(2,1)S(1)}, u32[]{:S(2)}, u32[]{:S(2)}) collective-permute-start(bf16[256,512]{1,0:T(8,128)(2,1)S(1)} %constant_dynamic-update-slice_fusion.refs_0_), channel_id=1, source_target_pairs={{0,1},{1,0},{2,3},{3,2},{4,5},{5,4},{6,7},{7,6},{8,9},{9,8},{10,11... | collective-permute-start | bytes 786440 | tf_op jit(solution)/shard_map/ppermute | solution.py:192
  4.5 6.9 %collective-permute-start.1 = (bf16[256,512]{1,0:T(8,128)(2,1)S(1)}, bf16[256,512]{1,0:T(8,128)(2,1)S(1)}, u32[]{:S(2)}, u32[]{:S(2)}) collective-permute-start(bf16[256,512]{1,0:T(8,128)(2,1)S(1)} %constant_dynamic-update-slice_fusion.refs_0_), channel_id=1, source_target_pairs={{0,4},{1,3},{2,0},{3,7},{4,8},{5,1},{6,2},{7,11},{8,12},{9,5},{10,... | collective-permute-start | bytes 786440 | tf_op jit(solution)/shard_map/ppermute | solution.py:192
  7.1 7.1 %collective-permute-start.2 = (bf16[256,512]{1,0:T(8,128)(2,1)S(1)}, bf16[256,512]{1,0:T(8,128)(2,1)S(1)}, u32[]{:S(2)}, u32[]{:S(2)}) collective-permute-start(bf16[256,512]{1,0:T(8,128)(2,1)S(1)} %collective-permute-done.refs_1_), channel_id=1, source_target_pairs={{0,4},{1,3},{2,0},{3,7},{4,8},{5,1},{6,2},{7,11},{8,12},{9,5},{10,... | collective-permute-start | bytes 786440 | tf_op jit(solution)/shard_map/ppermute | solution.py:192
  11.4 6.4 %collective-permute-start.5 = (bf16[256,512]{1,0:T(8,128)(2,1)S(1)}, bf16[256,512]{1,0:T(8,128)(2,1)S(1)}, u32[]{:S(2)}, u32[]{:S(2)}) collective-permute-start(bf16[256,512]{1,0:T(8,128)(2,1)S(1)} %collective-permute-done.1.refs_0_), channel_id=1, source_target_pairs={{0,4},{1,3},{2,0},{3,7},{4,8},{5,1},{6,2},{7,11},{8,12},{9,5},{10,... | collective-permute-start | bytes 786440 | tf_op jit(solution)/shard_map/ppermute | solution.py:192
  14.2 6.4 %collective-permute-start.6 = (bf16[256,512]{1,0:T(8,128)(2,1)S(1)}, bf16[256,512]{1,0:T(8,128)(2,1)S(1)}, u32[]{:S(2)}, u32[]{:S(2)}) collective-permute-start(bf16[256,512]{1,0:T(8,128)(2,1)S(1)} %collective-permute-done.2.refs_1_), channel_id=1, source_target_pairs={{0,4},{1,3},{2,0},{3,7},{4,8},{5,1},{6,2},{7,11},{8,12},{9,5},{10,... | collective-permute-start | bytes 786440 | tf_op jit(solution)/shard_map/ppermute | solution.py:192
  17.7 6.4 %collective-permute-start.9 = (bf16[256,512]{1,0:T(8,128)(2,1)S(1)}, bf16[256,512]{1,0:T(8,128)(2,1)S(1)}, u32[]{:S(2)}, u32[]{:S(2)}) collective-permute-start(bf16[256,512]{1,0:T(8,128)(2,1)S(1)} %collective-permute-done.5.refs_0_), channel_id=1, source_target_pairs={{0,4},{1,3},{2,0},{3,7},{4,8},{5,1},{6,2},{7,11},{8,12},{9,5},{10,... | collective-permute-start | bytes 786440 | tf_op jit(solution)/shard_map/ppermute | solution.py:192
  19.8 6.4 %collective-permute-start.3 = (bf16[256,512]{1,0:T(8,128)(2,1)S(1)}, bf16[256,512]{1,0:T(8,128)(2,1)S(1)}, u32[]{:S(2)}, u32[]{:S(2)}) collective-permute-start(bf16[256,512]{1,0:T(8,128)(2,1)S(1)} %collective-permute-done.1.refs_0_), channel_id=1, source_target_pairs={{0,1},{1,0},{2,3},{3,2},{4,5},{5,4},{6,7},{7,6},{8,9},{9,8},{10,11... | collective-permute-start | bytes 786440 | tf_op jit(solution)/shard_map/ppermute | solution.py:192
  19.8 6.9 %collective-permute-start.4 = (bf16[256,512]{1,0:T(8,128)(2,1)S(1)}, bf16[256,512]{1,0:T(8,128)(2,1)S(1)}, u32[]{:S(2)}, u32[]{:S(2)}) collective-permute-start(bf16[256,512]{1,0:T(8,128)(2,1)S(1)} %collective-permute-done.2.refs_1_), channel_id=1, source_target_pairs={{0,1},{1,0},{2,3},{3,2},{4,5},{5,4},{6,7},{7,6},{8,9},{9,8},{10,11... | collective-permute-start | bytes 786440 | tf_op jit(solution)/shard_map/ppermute | solution.py:192
  20.5 6.4 %collective-permute-start.10 = (bf16[256,512]{1,0:T(8,128)(2,1)S(1)}, bf16[256,512]{1,0:T(8,128)(2,1)S(1)}, u32[]{:S(2)}, u32[]{:S(2)}) collective-permute-start(bf16[256,512]{1,0:T(8,128)(2,1)S(1)} %collective-permute-done.6.refs_1_), channel_id=1, source_target_pairs={{0,4},{1,3},{2,0},{3,7},{4,8},{5,1},{6,2},{7,11},{8,12},{9,5},{10,... | collective-permute-start | bytes 786440 | tf_op jit(solution)/shard_map/ppermute | solution.py:192
  24.1 6.4 %collective-permute-start.13 = (bf16[256,512]{1,0:T(8,128)(2,1)S(1)}, bf16[256,512]{1,0:T(8,128)(2,1)S(1)}, u32[]{:S(2)}, u32[]{:S(2)}) collective-permute-start(bf16[256,512]{1,0:T(8,128)(2,1)S(1)} %collective-permute-done.9.refs_0_), channel_id=1, source_target_pairs={{0,4},{1,3},{2,0},{3,7},{4,8},{5,1},{6,2},{7,11},{8,12},{9,5},{10,... | collective-permute-start | bytes 786440 | tf_op jit(solution)/shard_map/ppermute | solution.py:192
  26.2 24.4 %collective-permute-start.7 = (bf16[256,512]{1,0:T(8,128)(2,1)S(1)}, bf16[256,512]{1,0:T(8,128)(2,1)S(1)}, u32[]{:S(2)}, u32[]{:S(2)}) collective-permute-start(bf16[256,512]{1,0:T(8,128)(2,1)S(1)} %collective-permute-done.5.refs_0_), channel_id=1, source_target_pairs={{0,1},{1,0},{2,3},{3,2},{4,5},{5,4},{6,7},{7,6},{8,9},{9,8},{10,11... | collective-permute-start | bytes 786440 | tf_op jit(solution)/shard_map/ppermute | solution.py:192
  26.2 24.4 %collective-permute-start.8 = (bf16[256,512]{1,0:T(8,128)(2,1)S(1)}, bf16[256,512]{1,0:T(8,128)(2,1)S(1)}, u32[]{:S(2)}, u32[]{:S(2)}) collective-permute-start(bf16[256,512]{1,0:T(8,128)(2,1)S(1)} %collective-permute-done.6.refs_1_), channel_id=1, source_target_pairs={{0,1},{1,0},{2,3},{3,2},{4,5},{5,4},{6,7},{7,6},{8,9},{9,8},{10,11... | collective-permute-start | bytes 786440 | tf_op jit(solution)/shard_map/ppermute | solution.py:192
  26.7 30.9 %collective-permute-start.11 = (bf16[256,512]{1,0:T(8,128)(2,1)S(1)}, bf16[256,512]{1,0:T(8,128)(2,1)S(1)}, u32[]{:S(2)}, u32[]{:S(2)}) collective-permute-start(bf16[256,512]{1,0:T(8,128)(2,1)S(1)} %collective-permute-done.9.refs_0_), channel_id=1, source_target_pairs={{0,1},{1,0},{2,3},{3,2},{4,5},{5,4},{6,7},{7,6},{8,9},{9,8},{10,11... | collective-permute-start | bytes 786440 | tf_op jit(solution)/shard_map/ppermute | solution.py:192
  26.9 30.7 %collective-permute-start.12 = (bf16[256,512]{1,0:T(8,128)(2,1)S(1)}, bf16[256,512]{1,0:T(8,128)(2,1)S(1)}, u32[]{:S(2)}, u32[]{:S(2)}) collective-permute-start(bf16[256,512]{1,0:T(8,128)(2,1)S(1)} %collective-permute-done.10.refs_1_), channel_id=1, source_target_pairs={{0,1},{1,0},{2,3},{3,2},{4,5},{5,4},{6,7},{7,6},{8,9},{9,8},{10,11... | collective-permute-start | bytes 786440 | tf_op jit(solution)/shard_map/ppermute | solution.py:192
  30.5 33.9 %collective-permute-start.14 = (bf16[256,512]{1,0:T(8,128)(2,1)S(1)}, bf16[256,512]{1,0:T(8,128)(2,1)S(1)}, u32[]{:S(2)}, u32[]{:S(2)}) collective-permute-start(bf16[256,512]{1,0:T(8,128)(2,1)S(1)} %collective-permute-done.13.refs_0_), channel_id=1, source_target_pairs={{0,1},{1,0},{2,3},{3,2},{4,5},{5,4},{6,7},{7,6},{8,9},{9,8},{10,11... | collective-permute-start | bytes 786440 | tf_op jit(solution)/shard_map/ppermute | solution.py:192
  31.8 1.0 %copy-start = (bf16[64,4096]{1,0:T(8,128)(2,1)S(1)}, bf16[64,4096]{1,0:T(8,128)(2,1)}, u32[]{:S(2)}) copy-start(bf16[64,4096]{1,0:T(8,128)(2,1)} %query_ref.1) | copy-start | bytes 1572868
  32.8 0.9 %copy-start.1 = (bf16[2,128,512]{2,1,0:T(8,128)(2,1)S(1)}, bf16[2,128,512]{2,1,0:T(8,128)(2,1)}, u32[]{:S(2)}) copy-start(bf16[2,128,512]{2,1,0:T(8,128)(2,1)} %suffix_key_ref.1) | copy-start | bytes 786436
  33.8 0.9 %copy-start.2 = (bf16[2,128,512]{2,1,0:T(8,128)(2,1)S(1)}, bf16[2,128,512]{2,1,0:T(8,128)(2,1)}, u32[]{:S(2)}) copy-start(bf16[2,128,512]{2,1,0:T(8,128)(2,1)} %suffix_value_ref.1) | copy-start | bytes 786436
  34.7 0.7 %copy-start.3 = (bf16[2,4096]{1,0:T(2,128)(2,1)S(1)}, bf16[2,4096]{1,0:T(2,128)(2,1)}, u32[]{:S(2)}) copy-start(bf16[2,4096]{1,0:T(2,128)(2,1)} %cont_ref.1) | copy-start | bytes 49156
  35.4 0.7 copy-start.4

commit v2 on v1

v2 whole, which is shorter than its diff:
```python
import functools
import math

import jax
import jax.numpy as jnp
from jax import lax
from jax.experimental import pallas as pl
from jax.experimental.pallas import tpu as pltpu
from jax.sharding import PartitionSpec as P

KVH = 4
HD = 128
GROUP = 8
SCALE = HD ** (-0.5) * math.log2(math.e)
MASKED = -1e30
FLOOR = -1e20
ONES = 16

VMEM = pl.BlockSpec(memory_space=pltpu.VMEM)
SMEM = pl.BlockSpec(memory_space=pltpu.SMEM)
HBM = pl.BlockSpec(memory_space=pltpu.HBM)
BF16 = jnp.bfloat16
F32 = jnp.float32


def ring_chip(place, chips):
    return jnp.where(place < chips // 2, 2 * place, 2 * (chips - 1 - place) + 1)


def ring_place(chip, chips):
    return jnp.where(chip % 2 == 0, chip // 2, chips - 1 - chip // 2)


def ring_pairs(size):
    chips = size // 2
    order = list(range(0, chips, 2)) + list(range(chips - 1, 0, -2))
    place = {chip: index for index, chip in enumerate(order)}
    pairs = []
    for device in range(size):
        chip, core = divmod(device, 2)
        step = 1 if core == 0 else -1
        pairs.append((device, 2 * order[(place[chip] + step) % chips] + core))
    return pairs


def block_origin(device, hop, swapped, partner, size):
    chips = size // 2
    chip, core = device // 2, device % 2
    via = 1 - core if swapped else core
    held = 1 - via if partner else via
    place = ring_place(chip, chips) + jnp.where(via == 0, -hop, hop)
    place = lax.rem(place + 2 * chips, chips)
    return 2 * ring_chip(place, chips) + held


def pack_kernel(ck_ref, nk_ref, cv_ref, nv_ref, out_ref, value_ref, sems):
    cache_rows, keys = ck_ref.shape[0], value_ref.shape[0]
    copies = [
        pltpu.make_async_copy(source, target, sems.at[index])
        for index, (source, target) in enumerate(
            [
                (cv_ref, value_ref.at[:cache_rows]),
                (nv_ref, value_ref.at[cache_rows:]),
                (ck_ref, out_ref.at[:cache_rows]),
                (nk_ref, out_ref.at[cache_rows:keys]),
            ]
        )
    ]
    for copy in copies:
        copy.start()
    for copy in copies[:2]:
        copy.wait()
    for g in range(KVH):
        out_ref[keys:, g * keys : (g + 1) * keys] = value_ref[:, g * HD : (g + 1) * HD].T
    for copy in copies[2:]:
        copy.wait()


def mask_columns(device, origin, window, cache_rows, prompt_rows):
    keys = cache_rows + prompt_rows
    key = lax.broadcasted_iota(jnp.int32, (keys, HD), 0)
    feature = lax.broadcasted_iota(jnp.int32, (keys, HD), 1)
    first, last = window
    at = origin * cache_rows + key
    outside = (key < cache_rows) & ((at < first) | (at >= last)) & (feature == prompt_rows)
    reach = jnp.where(origin == device, 0, jnp.where(origin < device, -keys, keys + HD))
    late = (key >= cache_rows) & (feature < prompt_rows) & (key - cache_rows + reach > feature)
    return jnp.where(outside | late, MASKED, 0.0).astype(BF16)


def row_features(rows, prompt_rows):
    feature = lax.broadcasted_iota(jnp.int32, (HD, rows), 0)
    row = lax.rem(lax.broadcasted_iota(jnp.int32, (HD, rows), 1), prompt_rows)
    return jnp.where((feature == row) | (feature == prompt_rows), 1.0, 0.0).astype(BF16)


def own_head(full, cont_rows):
    group = lax.broadcasted_iota(jnp.int32, (HD, KVH * cont_rows), 1) // cont_rows
    parts = [jnp.where(group == g, full[g * HD : (g + 1) * HD], 0.0) for g in range(KVH)]
    return jnp.concatenate([functools.reduce(jnp.add, parts), full[KVH * HD :]], axis=0)


def prep_kernel(
    length_ref, query_hbm, cont_hbm, key_hbm, value_hbm,
    q_ref, cont_q_ref, cont_max_ref, cont_total_ref,
    query_ref, cont_ref, key_ref, value_ref, sems,
):
    copies = [
        pltpu.make_async_copy(source, target, sems.at[index])
        for index, (source, target) in enumerate(
            [(query_hbm, query_ref), (cont_hbm, cont_ref), (key_hbm, key_ref), (value_hbm, value_ref)]
        )
    ]
    for copy in copies:
        copy.start()
    prompt_rows = query_ref.shape[0]
    cont_count, suffix_rows = key_ref.shape[:2]
    cont_rows = cont_count * GROUP
    for copy in copies[:2]:
        copy.wait()
    cont = cont_ref[...].astype(F32)
    zeros = jnp.zeros((HD, KVH * cont_rows), F32)
    column = lax.broadcasted_iota(jnp.int32, zeros.shape, 1) // cont_rows
    pieces = []
    for g in range(KVH):
        heads = [slice((g * GROUP + h) * HD, (g * GROUP + h + 1) * HD) for h in range(GROUP)]
        q = jnp.concatenate([query_ref[:, head] for head in heads], axis=0)
        q_ref[g * HD : (g + 1) * HD] = q.T
        pieces += [cont[c : c + 1, head] for c in range(cont_count) for head in heads]
    q_ref[KVH * HD :] = row_features(GROUP * prompt_rows, prompt_rows)
    cont_q = jnp.concatenate(pieces, axis=0).T
    cont_q = jnp.concatenate([jnp.where(column == g, cont_q, 0.0) for g in range(KVH)], axis=0)
    cont_q = cont_q.astype(BF16)
    cont_q_ref[...] = cont_q
    for copy in copies[2:]:
        copy.wait()
    scores = []
    for c in range(cont_count):
        s = jnp.dot(key_ref[c], cont_q, preferred_element_type=F32)
        key = lax.broadcasted_iota(jnp.int32, s.shape, 0)
        owner = lax.broadcasted_iota(jnp.int32, s.shape, 1) % cont_rows // GROUP
        scores.append(jnp.where((owner == c) & (key < length_ref[c]), s, MASKED))
    s = jnp.concatenate(scores, axis=0)
    high = jnp.maximum(jnp.max(s, axis=0, keepdims=True), FLOOR)
    p = jnp.exp2((s - high) * SCALE).astype(BF16)
    v = value_ref[...].reshape(cont_count * suffix_rows, KVH * HD)
    v = jnp.concatenate([v.T, jnp.ones((ONES, v.shape[0]), BF16)], axis=0)
    cont_max_ref[...] = high
    cont_total_ref[...] = own_head(jnp.dot(v, p, preferred_element_type=F32), cont_rows)


def step_kernel(size, cache_rows, prompt_rows, sources, first_step, last_step, *refs):
    first_ref, last_ref, q_ref, cont_q_ref = refs[:4]
    held, refs = (refs[4:6], refs[6:]) if first_step else (refs[4:8], refs[8:])
    blocks, outs = refs[: len(sources)], refs[len(sources) :]
    device = lax.axis_index("ctx")
    window = (first_ref[0], last_ref[0])
    keys = cache_rows + prompt_rows
    rows = GROUP * prompt_rows
    cont_rows = cont_q_ref.shape[1] // KVH
    masks = jnp.concatenate(
        [
            mask_columns(device, block_origin(device, *source, size), window, cache_rows, prompt_rows)
            for source in sources
        ],
        axis=0,
    )
    ones = jnp.ones((ONES, len(blocks) * keys), BF16)

    def merge(scores, old_max, old_total, values):
        new_max = jnp.maximum(old_max, jnp.max(scores, axis=0, keepdims=True))
        p = jnp.exp2((scores - new_max) * SCALE).astype(BF16)
        total = values(p)
        if old_total is not None:
            total = total + old_total * jnp.exp2((old_max - new_max) * SCALE)
        return new_max, total

    values = []
    for g in range(KVH):
        cols = slice(g * HD, (g + 1) * HD)
        k = jnp.concatenate([block[:keys, cols] for block in blocks], axis=0)
        v = jnp.concatenate([block[keys:, g * keys : (g + 1) * keys] for block in blocks], axis=1)
        values.append(v)
        v = jnp.concatenate([v, ones], axis=0)
        s = jnp.dot(
            jnp.concatenate([k, masks], axis=1),
            jnp.concatenate([q_ref[cols], q_ref[KVH * HD :]], axis=0),
            preferred_element_type=F32,
        )
        old = (jnp.full((1, rows), FLOOR, F32), None) if first_step else (held[2][g], held[3][g])
        new_max, total = merge(s, *old, lambda p: jnp.dot(v, p, preferred_element_type=F32))
        if not last_step:
            outs[2][g] = new_max
            outs[3][g] = total
            continue
        result = (total[:HD] * (1.0 / total[HD : HD + 1])).T.astype(BF16)
        for h in range(GROUP):
            cols = slice((g * GROUP + h) * HD, (g * GROUP + h + 1) * HD)
            outs[0][:, cols] = result[h * prompt_rows : (h + 1) * prompt_rows]

    s = sum(
        jnp.dot(
            jnp.concatenate([block[:keys, half * 2 * HD : (half + 1) * 2 * HD] for block in blocks], axis=0),
            cont_q_ref[half * 2 * HD : (half + 1) * 2 * HD],
            preferred_element_type=F32,
        )
        for half in range(KVH // 2)
    )
    hidden = masks[:, prompt_rows : prompt_rows + 1].astype(F32)
    v = jnp.concatenate(values + [ones], axis=0)
    new_max, total = merge(
        s + hidden, held[0][...], held[1][...],
        lambda p: own_head(jnp.dot(v, p, preferred_element_type=F32), cont_rows),
    )
    if not last_step:
        outs[0][...] = new_max
        outs[1][...] = total
        return
    result = (total[:HD] * (1.0 / total[HD : HD + 1])).T
    for row in range(KVH * cont_rows):
        g, c, h = row // cont_rows, row % cont_rows // GROUP, row % GROUP
        cols = slice((g * GROUP + h) * HD, (g * GROUP + h + 1) * HD)
        outs[1][c : c + 1, cols] = result[row : row + 1].astype(BF16)


def in_hbm(array):
    return pltpu.with_memory_space_constraint(array, pltpu.HBM)


def cost(rows, keys):
    work = rows * keys
    return pl.CostEstimate(flops=8 * work * HD, transcendentals=work, bytes_accessed=1 << 20)


def body(
    size,
    cache_keys,
    cache_values,
    new_queries,
    new_keys,
    new_values,
    cont_queries,
    suffix_keys,
    suffix_values,
    window_start,
    prefix_length,
    suffix_length,
):
    cache_rows, prompt_rows, cont_count = (
        cache_keys.shape[0], new_keys.shape[0], cont_queries.shape[0],
    )
    keys = cache_rows + prompt_rows
    chips = size // 2
    ring = ring_pairs(size)
    pair = [(device, device ^ 1) for device in range(size)]
    params = pltpu.CompilerParams(vmem_limit_bytes=24 << 20)
    rows, cont_rows = GROUP * prompt_rows, KVH * GROUP * cont_count
    shape = jax.ShapeDtypeStruct

    def send(block, pairs):
        return lax.ppermute(block, "ctx", pairs)

    own = pl.pallas_call(
        pack_kernel,
        out_shape=shape((keys + HD, KVH * HD), BF16),
        in_specs=[HBM] * 4,
        out_specs=VMEM,
        scratch_shapes=[pltpu.VMEM((keys, KVH * HD), BF16), pltpu.SemaphoreType.DMA((4,))],
        compiler_params=params,
    )(*[in_hbm(x) for x in (cache_keys, new_keys, cache_values, new_values)])
    other = send(own, pair)

    state_shape = [
        shape((1, cont_rows), F32),
        shape((HD + ONES, cont_rows), F32),
        shape((KVH, 1, rows), F32),
        shape((KVH, HD + ONES, rows), F32),
    ]
    queries, cont_q, *state = pl.pallas_call(
        prep_kernel,
        out_shape=[
            shape(((KVH + 1) * HD, rows), BF16),
            shape((KVH * HD, cont_rows), BF16),
        ] + state_shape[:2],
        in_specs=[SMEM] + [HBM] * 4,
        out_specs=[VMEM] * 4,
        scratch_shapes=[
            pltpu.VMEM(new_queries.shape, BF16),
            pltpu.VMEM(cont_queries.shape, BF16),
            pltpu.VMEM(suffix_keys.shape, BF16),
            pltpu.VMEM(suffix_values.shape, BF16),
            pltpu.SemaphoreType.DMA((4,)),
        ],
        compiler_params=params,
        cost_estimate=cost(rows, keys),
    )(suffix_length, *[in_hbm(x) for x in (new_queries, cont_queries, suffix_keys, suffix_values)])

    def step(state, sources, blocks, last_step=False):
        first_step = len(state) == 2
        outs = [shape(new_queries.shape, BF16), shape(cont_queries.shape, BF16)]
        outs = outs if last_step else state_shape
        aliases = {} if last_step else {4 + index: index for index in range(len(state))}
        return pl.pallas_call(
            functools.partial(
                step_kernel, size, cache_rows, prompt_rows, sources, first_step, last_step
            ),
            out_shape=outs,
            in_specs=[SMEM] * 2 + [VMEM] * (2 + len(state) + len(blocks)),
            out_specs=[VMEM] * len(outs),
            input_output_aliases=aliases,
            compiler_params=params,
            cost_estimate=cost(rows, len(blocks) * keys),
        )(window_start, prefix_length, queries, cont_q, *state, *blocks)

    state = step(state, [(0, False, False), (0, False, True)], [own, other])
    for hop in range(1, chips // 2):
        own = send(own, ring)
        other = send(other, ring)
        blocks = [own, other, send(own, pair), send(other, pair)]
        sources = [(hop, False, False), (hop, False, True), (hop, True, False), (hop, True, True)]
        state = step(state, sources, blocks)
    hop = chips // 2
    own = send(own, ring)
    sources = [(hop, False, False), (hop, True, False)]
    blocks = [own, send(own, pair)]
    return tuple(step(state, sources, blocks, last_step=True))


def solution(mesh):
    in_specs = (
        P(("grp", "ctx"), None),
        P(("grp", "ctx"), None),
        P(("grp", "ctx"), None),
        P(("grp", "ctx"), None),
        P(("grp", "ctx"), None),
        P(("grp", "ctx"), None),
        P(("grp", "ctx"), None, None),
        P(("grp", "ctx"), None, None),
        P("grp"),
        P("grp"),
        P(("grp", "ctx")),
    )
    out_specs = (P(("grp", "ctx"), None), P(("grp", "ctx"), None))
    size = mesh.shape["ctx"]

    def run(*arrays):
        return body(size, *arrays)

    return jax.shard_map(run, mesh=mesh, in_specs=in_specs, out_specs=out_specs, check_vma=False)
```

time: 72.2 us -> 45.5 us (0.63)
  Pallas kernels: 35.6 us -> 16 us
  local copies, waits for them, and re-layouts: 7.68 us -> 0.65 us
    pallas_call x5 -> x7, Pallas kernels: 35.6 us -> 16 us  [the longest x5 12.7 us: step(): pl.pallas_call(functools.partial(step_kernel, size, cache_rows, prompt_ro...]
    unnamed x13 -> x2, local copies, waits for them, and re-layouts: 6.84 us -> 0.65 us
    concatenate x1 -> x0, local copies, waits for them, and re-layouts: 0.84 us -> none  [body(): jnp.concatenate([cache_keys, new_keys, cache_values, new_values], axis=0)]
  transfers between devices with their start and end apart: 15 -> 15, of which waited for: 7 -> 7; matrix products, arithmetic and copies ran while one was open for 0% -> 0% of each run, Pallas kernels for 39% -> 27%
where the time goes in v2:
time: 45.5 us; the launch traced here: 45.3 us
  starting transfers between devices  16.5 us (36%)
  Pallas kernels  16 us (35%)
  waiting for transfers between devices  10.1 us (22%)
  between operations  2.03 us (4%)
  local copies, waits for them, and re-layouts  0.65 us (1%)
    ppermute x15, starting transfers between devices, send(): return lax.ppermute(block, 'ctx', pairs)  16.5 us
    pallas_call x5, Pallas kernels, step(): pl.pallas_call(functools.partial(step_kernel, size, cache_rows, prompt_ro...  12.7 us
    ppermute x15, waiting for transfers between devices, send(): return lax.ppermute(block, 'ctx', pairs)  10.1 us
    pallas_call x1, Pallas kernels, body(): pl.pallas_call(prep_kernel, out_shape=[shape(((KVH + 1) * HD, rows), BF16...  2.32 us
    pallas_call x1, Pallas kernels, body(): pl.pallas_call(pack_kernel, out_shape=shape((keys + HD, KVH * HD), BF16),...  1 us
  transfers between devices with their start and end apart: 15, of which 7 were waited for; matrix products, arithmetic and copies ran while one was open for 0% of the time, Pallas kernels for 27%

profile of v2, /device:TPU:0, one launch (start us, length us, event | category | flops | bytes accessed | tf_op | source)
XLA Modules:
  0.0 45.3 jit_solution(10784323838174046770)
XLA Ops:
  0.6 1.0 %shard_map.123.refs_6_ = bf16[256,512]{1,0:T(8,128)(2,1)S(1)} custom-call(bf16[64,512]{1,0:T(8,128)(2,1)} %ck_ref.1, bf16[64,512]{1,0:T(8,128)(2,1)} %nk_ref.1, bf16[64,512]{1,0:T(8,128)(2,1)} %cv_ref.1, bf16[64,512]{1,0:T(8,128)(2,1)} %nv_ref.1), custom_call_target="tpu_custom_call" | custom-call | tf_op jit(solution)/shard_map/pallas_call | solution.py:263
  1.6 0.6 %collective-permute-start = (bf16[256,512]{1,0:T(8,128)(2,1)S(1)}, bf16[256,512]{1,0:T(8,128)(2,1)S(1)}, u32[]{:S(2)}, u32[]{:S(2)}) collective-permute-start(bf16[256,512]{1,0:T(8,128)(2,1)S(1)} %shard_map.123.refs_6_), channel_id=1, source_target_pairs={{0,1},{1,0},{2,3},{3,2},{4,5},{5,4},{6,7},{7,6},{8,9},{9,8},{10,11... | collective-permute-start | bytes 786440 | tf_op jit(solution)/shard_map/ppermute | solution.py:261
  2.2 2.6 %collective-permute-start.1 = (bf16[256,512]{1,0:T(8,128)(2,1)S(1)}, bf16[256,512]{1,0:T(8,128)(2,1)S(1)}, u32[]{:S(2)}, u32[]{:S(2)}) collective-permute-start(bf16[256,512]{1,0:T(8,128)(2,1)S(1)} %shard_map.123.refs_6_), channel_id=1, source_target_pairs={{0,4},{1,3},{2,0},{3,7},{4,8},{5,1},{6,2},{7,11},{8,12},{9,5},{10,... | collective-permute-start | bytes 786440 | tf_op jit(solution)/shard_map/ppermute | solution.py:261
  4.8 0.0 collective-permute-done.refs_7_
  4.8 1.6 %collective-permute-start.2 = (bf16[256,512]{1,0:T(8,128)(2,1)S(1)}, bf16[256,512]{1,0:T(8,128)(2,1)S(1)}, u32[]{:S(2)}, u32[]{:S(2)}) collective-permute-start(bf16[256,512]{1,0:T(8,128)(2,1)S(1)} %collective-permute-done.refs_7_), channel_id=1, source_target_pairs={{0,4},{1,3},{2,0},{3,7},{4,8},{5,1},{6,2},{7,11},{8,12},{9,5},{10,... | collective-permute-start | bytes 786440 | tf_op jit(solution)/shard_map/ppermute | solution.py:261
  6.4 2.7 %collective-permute-done.1.refs_8_ = bf16[256,512]{1,0:T(8,128)(2,1)S(1)} collective-permute-done((bf16[256,512]{1,0:T(8,128)(2,1)S(1)}, bf16[256,512]{1,0:T(8,128)(2,1)S(1)}, u32[]{:S(2)}, u32[]{:S(2)}) %collective-permute-start.1) | collective-permute-done | bytes 262176 | tf_op jit(solution)/shard_map/ppermute | solution.py:261
  9.1 2.1 %collective-permute-start.5 = (bf16[256,512]{1,0:T(8,128)(2,1)S(1)}, bf16[256,512]{1,0:T(8,128)(2,1)S(1)}, u32[]{:S(2)}, u32[]{:S(2)}) collective-permute-start(bf16[256,512]{1,0:T(8,128)(2,1)S(1)} %collective-permute-done.1.refs_8_), channel_id=1, source_target_pairs={{0,4},{1,3},{2,0},{3,7},{4,8},{5,1},{6,2},{7,11},{8,12},{9,5},{10,... | collective-permute-start | bytes 786440 | tf_op jit(solution)/shard_map/ppermute | solution.py:261
  11.2 0.7 %collective-permute-done.2.refs_9_ = bf16[256,512]{1,0:T(8,128)(2,1)S(1)} collective-permute-done((bf16[256,512]{1,0:T(8,128)(2,1)S(1)}, bf16[256,512]{1,0:T(8,128)(2,1)S(1)}, u32[]{:S(2)}, u32[]{:S(2)}) %collective-permute-start.2) | collective-permute-done | bytes 262176 | tf_op jit(solution)/shard_map/ppermute | solution.py:261
  11.9 2.1 %collective-permute-start.6 = (bf16[256,512]{1,0:T(8,128)(2,1)S(1)}, bf16[256,512]{1,0:T(8,128)(2,1)S(1)}, u32[]{:S(2)}, u32[]{:S(2)}) collective-permute-start(bf16[256,512]{1,0:T(8,128)(2,1)S(1)} %collective-permute-done.2.refs_9_), channel_id=1, source_target_pairs={{0,4},{1,3},{2,0},{3,7},{4,8},{5,1},{6,2},{7,11},{8,12},{9,5},{10,... | collective-permute-start | bytes 786440 | tf_op jit(solution)/shard_map/ppermute | solution.py:261
  14.0 1.5 %collective-permute-done.5.refs_8_ = bf16[256,512]{1,0:T(8,128)(2,1)S(1)} collective-permute-done((bf16[256,512]{1,0:T(8,128)(2,1)S(1)}, bf16[256,512]{1,0:T(8,128)(2,1)S(1)}, u32[]{:S(2)}, u32[]{:S(2)}) %collective-permute-start.5) | collective-permute-done | bytes 262176 | tf_op jit(solution)/shard_map/ppermute | solution.py:261
  15.5 2.1 %collective-permute-start.9 = (bf16[256,512]{1,0:T(8,128)(2,1)S(1)}, bf16[256,512]{1,0:T(8,128)(2,1)S(1)}, u32[]{:S(2)}, u32[]{:S(2)}) collective-permute-start(bf16[256,512]{1,0:T(8,128)(2,1)S(1)} %collective-permute-done.5.refs_8_), channel_id=1, source_target_pairs={{0,4},{1,3},{2,0},{3,7},{4,8},{5,1},{6,2},{7,11},{8,12},{9,5},{10,... | collective-permute-start | bytes 786440 | tf_op jit(solution)/shard_map/ppermute | solution.py:261
  17.6 0.0 collective-permute-start.3
  17.6 0.5 %collective-permute-start.4 = (bf16[256,512]{1,0:T(8,128)(2,1)S(1)}, bf16[256,512]{1,0:T(8,128)(2,1)S(1)}, u32[]{:S(2)}, u32[]{:S(2)}) collective-permute-start(bf16[256,512]{1,0:T(8,128)(2,1)S(1)} %collective-permute-done.2.refs_9_), channel_id=1, source_target_pairs={{0,1},{1,0},{2,3},{3,2},{4,5},{5,4},{6,7},{7,6},{8,9},{9,8},{10,11... | collective-permute-start | bytes 786440 | tf_op jit(solution)/shard_map/ppermute | solution.py:261
  18.1 0.2 collective-permute-done.6.refs_9_
  18.3 2.1 %collective-permute-start.10 = (bf16[256,512]{1,0:T(8,128)(2,1)S(1)}, bf16[256,512]{1,0:T(8,128)(2,1)S(1)}, u32[]{:S(2)}, u32[]{:S(2)}) collective-permute-start(bf16[256,512]{1,0:T(8,128)(2,1)S(1)} %collective-permute-done.6.refs_9_), channel_id=1, source_target_pairs={{0,4},{1,3},{2,0},{3,7},{4,8},{5,1},{6,2},{7,11},{8,12},{9,5},{10,... | collective-permute-start | bytes 786440 | tf_op jit(solution)/shard_map/ppermute | solution.py:261
  20.4 1.5 %collective-permute-done.9.refs_8_ = bf16[256,512]{1,0:T(8,128)(2,1)S(1)} collective-permute-done((bf16[256,512]{1,0:T(8,128)(2,1)S(1)}, bf16[256,512]{1,0:T(8,128)(2,1)S(1)}, u32[]{:S(2)}, u32[]{:S(2)}) %collective-permute-start.9) | collective-permute-done | bytes 262176 | tf_op jit(solution)/shard_map/ppermute | solution.py:261
  21.9 2.1 %collective-permute-start.13 = (bf16[256,512]{1,0:T(8,128)(2,1)S(1)}, bf16[256,512]{1,0:T(8,128)(2,1)S(1)}, u32[]{:S(2)}, u32[]{:S(2)}) collective-permute-start(bf16[256,512]{1,0:T(8,128)(2,1)S(1)} %collective-permute-done.9.refs_8_), channel_id=1, source_target_pairs={{0,4},{1,3},{2,0},{3,7},{4,8},{5,1},{6,2},{7,11},{8,12},{9,5},{10,... | collective-permute-start | bytes 786440 | tf_op jit(solution)/shard_map/ppermute | solution.py:261
  23.9 0.0 collective-permute-start.7
  23.9 0.0 collective-permute-done.3.refs_10_
  23.9 0.5 %collective-permute-start.8 = (bf16[256,512]{1,0:T(8,128)(2,1)S(1)}, bf16[256,512]{1,0:T(8,128)(2,1)S(1)}, u32[]{:S(2)}, u32[]{:S(2)}) collective-permute-start(bf16[256,512]{1,0:T(8,128)(2,1)S(1)} %collective-permute-done.6.refs_9_), channel_id=1, source_target_pairs={{0,1},{1,0},{2,3},{3,2},{4,5},{5,4},{6,7},{7,6},{8,9},{9,8},{10,11... | collective-permute-start | bytes 786440 | tf_op jit(solution)/shard_map/ppermute | solution.py:261
  24.5 0.0 collective-permute-done.4.refs_11_
  24.5 0.1 collective-permute-start.11
  24.5 0.1 collective-permute-done.10.refs_9_
  24.7 0.3 collective-permute-start.12
  25.0 3.3 %collective-permute-done.13.refs_8_ = bf16[256,512]{1,0:T(8,128)(2,1)S(1)} collective-permute-done((bf16[256,512]{1,0:T(8,128)(2,1)S(1)}, bf16[256,512]{1,0:T(8,128)(2,1)S(1)}, u32[]{:S(2)}, u32[]{:S(2)}) %collective-permute-start.13) | collective-permute-done | bytes 262176 | tf_op jit(solution)/shard_map/ppermute | solution.py:261
  28.2 0.0 collective-permute-start.14
  29.5 0.0 copy-start
  29.5 0.6 %copy-done = s32[2]{0:T(128)S(1)} copy-done((s32[2]{0:T(128)S(1)}, s32[2]{0:T(128)}, u32[]{:S(2)}) %copy-start) | copy-done | bytes 32
  30.2 2.3 %shard_map.122 = (bf16[640,512]{1,0:T(8,128)(2,1)S(1)}, bf16[512,64]{1,0:T(8,128)(2,1)S(1)}, f32[1,64]{1,0:T(1,128)S(1)}, f32[144,64]{1,0:T(8,128)S(1)}) custom-call(s32[2]{0:T(128)S(1)} %copy-done, bf16[64,4096]{1,0:T(8,128)(2,1)} %query_hbm.1, bf16[2,4096]{1,0:T(2,128)(2,1)} %cont_hbm.1, bf16[2,128,512]{2,1,0:T(8,128)(2,1)} %key_hbm.1, ...), custom_call_target="tpu_custom_call" | custom-call | flops 67108864 | bytes 1048576 | tf_op jit(solution)/shard_map/pallas_call | solution.py:279
  32.5 1.9 %shard_map.124 = (f32[1,64]{1,0:T(1,128)S(1)}, f32[144,64]{1,0:T(8,128)S(1)}, f32[4,1,512]{2,1,0:T(1,128)S(1)}, f32[4,144,512]{2,1,0:T(8,128)S(1)}) custom-call(s32[1]{0:T(128)S(6)} %copy.41.refs_0_, s32[1]{0:T(128)S(6)} %copy.42.refs_1_, bf16[640,512]{1,0:T(8,128)(2,1)S(1)} %get-tuple-element.22.refs_2_, ...), custom_call_target="tpu_custom_call", output_to_operand_aliasing={{0}: (4, {}), {1}: (5, {})} | custom-call | flops 134217728 | bytes 1048576 | tf_op jit(solution)/shard_map/pallas_call | solution.py:303
  34.4 2.7 %shard_map.125 = (f32[1,64]{1,0:T(1,128)S(1)}, f32[144,64]{1,0:T(8,128)S(1)}, f32[4,1,512]{2,1,0:T(1,128)S(1)}, f32[4,144,512]{2,1,0:T(8,128)S(1)}) custom-call(s32[1]{0:T(128)S(6)} %copy.41.refs_0_, s32[1]{0:T(128)S(6)} %copy.42.refs_1_, ...), custom_call_target="tpu_custom_call", output_to_operand_aliasing={{0}: (4, {}), {1}: (5, {}), {2}: (6, {}), {3}: (7, {})} | custom-call | flops 268435456 | bytes 1048576 | tf_op jit(solution)/shard_map/pallas_call | solution.py:303
  37.1 0.0 collective-permute-done.7.refs_10_
  37.1 0.0 collective-permute-done.8.refs_11_
  37.1 2.7 %shard_map.126 = (f32[1,64]{1,0:T(1,128)S(1)}, f32[144,64]{1,0:T(8,128)S(1)}, f32[4,1,512]{2,1,0:T(1,128)S(1)}, f32[4,144,512]{2,1,0:T(8,128)S(1)}) custom-call(s32[1]{0:T(128)S(6)} %copy.41.refs_0_, s32[1]{0:T(128)S(6)} %copy.42.refs_1_, ...), custom_call_target="tpu_custom_call", output_to_operand_aliasing={{0}: (4, {}), {1}: (5, {}), {2}: (6, {}), {3}: (7, {})} | custom-call | flops 268435456 | bytes 1048576 | tf_op jit(solution)/shard_map/pallas_call | solution.py:303
  39.8 0.0 collective-permute-done.11.refs_10_
  39.8 0.0 collective-permute-done.12.refs_11_
  39.8 2.7 %shard_map.127 = (f32[1,64]{1,0:T(1,128)S(1)}, f32[144,64]{1,0:T(8,128)S(1)}, f32[4,1,512]{2,1,0:T(1,128)S(1)}, f32[4,144,512]{2,1,0:T(8,128)S(1)}) custom-call(s32[1]{0:T(128)S(6)} %copy.41.refs_0_, s32[1]{0:T(128)S(6)} %copy.42.refs_1_, ...), custom_call_target="tpu_custom_call", output_to_operand_aliasing={{0}: (4, {}), {1}: (5, {}), {2}: (6, {}), {3}: (7, {})} | custom-call | flops 268435456 | bytes 1048576 | tf_op jit(solution)/shard_map/pallas_call | solution.py:303
  42.5 0.0 collective-permute-done.14.refs_9_
  42.5 2.8 %shard_map.128 = (bf16[64,4096]{1,0:T(8,128)(2,1)}, bf16[2,4096]{1,0:T(2,128)(2,1)}) custom-call(s32[1]{0:T(128)S(6)} %copy.41.refs_0_, s32[1]{0:T(128)S(6)} %copy.42.refs_1_, bf16[640,512]{1,0:T(8,128)(2,1)S(1)} %get-tuple-element.22.refs_2_, bf16[512,64]{1,0:T(8,128)(2,1)S(1)} %get-tuple-element.23.refs_3_, f32[1,64]{1,0:T(1,128)S(1)} %get-tuple-element.38.refs_4_, ...), custom_call_target="tpu_custom_call" | custom-call | flops 134217728 | bytes 1048576 | tf_op jit(solution)/shard_map/pallas_call | solution.py:303
Async XLA Ops:
  1.6 3.2 %collective-permute-start = (bf16[256,512]{1,0:T(8,128)(2,1)S(1)}, bf16[256,512]{1,0:T(8,128)(2,1)S(1)}, u32[]{:S(2)}, u32[]{:S(2)}) collective-permute-start(bf16[256,512]{1,0:T(8,128)(2,1)S(1)} %shard_map.123.refs_6_), channel_id=1, source_target_pairs={{0,1},{1,0},{2,3},{3,2},{4,5},{5,4},{6,7},{7,6},{8,9},{9,8},{10,11... | collective-permute-start | bytes 786440 | tf_op jit(solution)/shard_map/ppermute | solution.py:261
  2.2 6.9 %collective-permute-start.1 = (bf16[256,512]{1,0:T(8,128)(2,1)S(1)}, bf16[256,512]{1,0:T(8,128)(2,1)S(1)}, u32[]{:S(2)}, u32[]{:S(2)}) collective-permute-start(bf16[256,512]{1,0:T(8,128)(2,1)S(1)} %shard_map.123.refs_6_), channel_id=1, source_target_pairs={{0,4},{1,3},{2,0},{3,7},{4,8},{5,1},{6,2},{7,11},{8,12},{9,5},{10,... | collective-permute-start | bytes 786440 | tf_op jit(solution)/shard_map/ppermute | solution.py:261
  4.8 7.1 %collective-permute-start.2 = (bf16[256,512]{1,0:T(8,128)(2,1)S(1)}, bf16[256,512]{1,0:T(8,128)(2,1)S(1)}, u32[]{:S(2)}, u32[]{:S(2)}) collective-permute-start(bf16[256,512]{1,0:T(8,128)(2,1)S(1)} %collective-permute-done.refs_7_), channel_id=1, source_target_pairs={{0,4},{1,3},{2,0},{3,7},{4,8},{5,1},{6,2},{7,11},{8,12},{9,5},{10,... | collective-permute-start | bytes 786440 | tf_op jit(solution)/shard_map/ppermute | solution.py:261
  9.1 6.4 %collective-permute-start.5 = (bf16[256,512]{1,0:T(8,128)(2,1)S(1)}, bf16[256,512]{1,0:T(8,128)(2,1)S(1)}, u32[]{:S(2)}, u32[]{:S(2)}) collective-permute-start(bf16[256,512]{1,0:T(8,128)(2,1)S(1)} %collective-permute-done.1.refs_8_), channel_id=1, source_target_pairs={{0,4},{1,3},{2,0},{3,7},{4,8},{5,1},{6,2},{7,11},{8,12},{9,5},{10,... | collective-permute-start | bytes 786440 | tf_op jit(solution)/shard_map/ppermute | solution.py:261
  11.9 6.4 %collective-permute-start.6 = (bf16[256,512]{1,0:T(8,128)(2,1)S(1)}, bf16[256,512]{1,0:T(8,128)(2,1)S(1)}, u32[]{:S(2)}, u32[]{:S(2)}) collective-permute-start(bf16[256,512]{1,0:T(8,128)(2,1)S(1)} %collective-permute-done.2.refs_9_), channel_id=1, source_target_pairs={{0,4},{1,3},{2,0},{3,7},{4,8},{5,1},{6,2},{7,11},{8,12},{9,5},{10,... | collective-permute-start | bytes 786440 | tf_op jit(solution)/shard_map/ppermute | solution.py:261
  15.5 6.4 %collective-permute-start.9 = (bf16[256,512]{1,0:T(8,128)(2,1)S(1)}, bf16[256,512]{1,0:T(8,128)(2,1)S(1)}, u32[]{:S(2)}, u32[]{:S(2)}) collective-permute-start(bf16[256,512]{1,0:T(8,128)(2,1)S(1)} %collective-permute-done.5.refs_8_), channel_id=1, source_target_pairs={{0,4},{1,3},{2,0},{3,7},{4,8},{5,1},{6,2},{7,11},{8,12},{9,5},{10,... | collective-permute-start | bytes 786440 | tf_op jit(solution)/shard_map/ppermute | solution.py:261
  17.6 6.4 %collective-permute-start.3 = (bf16[256,512]{1,0:T(8,128)(2,1)S(1)}, bf16[256,512]{1,0:T(8,128)(2,1)S(1)}, u32[]{:S(2)}, u32[]{:S(2)}) collective-permute-start(bf16[256,512]{1,0:T(8,128)(2,1)S(1)} %collective-permute-done.1.refs_8_), channel_id=1, source_target_pairs={{0,1},{1,0},{2,3},{3,2},{4,5},{5,4},{6,7},{7,6},{8,9},{9,8},{10,11... | collective-permute-start | bytes 786440 | tf_op jit(solution)/shard_map/ppermute | solution.py:261
  17.6 6.9 %collective-permute-start.4 = (bf16[256,512]{1,0:T(8,128)(2,1)S(1)}, bf16[256,512]{1,0:T(8,128)(2,1)S(1)}, u32[]{:S(2)}, u32[]{:S(2)}) collective-permute-start(bf16[256,512]{1,0:T(8,128)(2,1)S(1)} %collective-permute-done.2.refs_9_), channel_id=1, source_target_pairs={{0,1},{1,0},{2,3},{3,2},{4,5},{5,4},{6,7},{7,6},{8,9},{9,8},{10,11... | collective-permute-start | bytes 786440 | tf_op jit(solution)/shard_map/ppermute | solution.py:261
  18.3 6.4 %collective-permute-start.10 = (bf16[256,512]{1,0:T(8,128)(2,1)S(1)}, bf16[256,512]{1,0:T(8,128)(2,1)S(1)}, u32[]{:S(2)}, u32[]{:S(2)}) collective-permute-start(bf16[256,512]{1,0:T(8,128)(2,1)S(1)} %collective-permute-done.6.refs_9_), channel_id=1, source_target_pairs={{0,4},{1,3},{2,0},{3,7},{4,8},{5,1},{6,2},{7,11},{8,12},{9,5},{10,... | collective-permute-start | bytes 786440 | tf_op jit(solution)/shard_map/ppermute | solution.py:261
  21.9 6.4 %collective-permute-start.13 = (bf16[256,512]{1,0:T(8,128)(2,1)S(1)}, bf16[256,512]{1,0:T(8,128)(2,1)S(1)}, u32[]{:S(2)}, u32[]{:S(2)}) collective-permute-start(bf16[256,512]{1,0:T(8,128)(2,1)S(1)} %collective-permute-done.9.refs_8_), channel_id=1, source_target_pairs={{0,4},{1,3},{2,0},{3,7},{4,8},{5,1},{6,2},{7,11},{8,12},{9,5},{10,... | collective-permute-start | bytes 786440 | tf_op jit(solution)/shard_map/ppermute | solution.py:261
  23.9 13.1 %collective-permute-start.7 = (bf16[256,512]{1,0:T(8,128)(2,1)S(1)}, bf16[256,512]{1,0:T(8,128)(2,1)S(1)}, u32[]{:S(2)}, u32[]{:S(2)}) collective-permute-start(bf16[256,512]{1,0:T(8,128)(2,1)S(1)} %collective-permute-done.5.refs_8_), channel_id=1, source_target_pairs={{0,1},{1,0},{2,3},{3,2},{4,5},{5,4},{6,7},{7,6},{8,9},{9,8},{10,11... | collective-permute-start | bytes 786440 | tf_op jit(solution)/shard_map/ppermute | solution.py:261
  23.9 13.1 %collective-permute-start.8 = (bf16[256,512]{1,0:T(8,128)(2,1)S(1)}, bf16[256,512]{1,0:T(8,128)(2,1)S(1)}, u32[]{:S(2)}, u32[]{:S(2)}) collective-permute-start(bf16[256,512]{1,0:T(8,128)(2,1)S(1)} %collective-permute-done.6.refs_9_), channel_id=1, source_target_pairs={{0,1},{1,0},{2,3},{3,2},{4,5},{5,4},{6,7},{7,6},{8,9},{9,8},{10,11... | collective-permute-start | bytes 786440 | tf_op jit(solution)/shard_map/ppermute | solution.py:261
  24.5 15.3 %collective-permute-start.11 = (bf16[256,512]{1,0:T(8,128)(2,1)S(1)}, bf16[256,512]{1,0:T(8,128)(2,1)S(1)}, u32[]{:S(2)}, u32[]{:S(2)}) collective-permute-start(bf16[256,512]{1,0:T(8,128)(2,1)S(1)} %collective-permute-done.9.refs_8_), channel_id=1, source_target_pairs={{0,1},{1,0},{2,3},{3,2},{4,5},{5,4},{6,7},{7,6},{8,9},{9,8},{10,11... | collective-permute-start | bytes 786440 | tf_op jit(solution)/shard_map/ppermute | solution.py:261
  24.7 15.1 %collective-permute-start.12 = (bf16[256,512]{1,0:T(8,128)(2,1)S(1)}, bf16[256,512]{1,0:T(8,128)(2,1)S(1)}, u32[]{:S(2)}, u32[]{:S(2)}) collective-permute-start(bf16[256,512]{1,0:T(8,128)(2,1)S(1)} %collective-permute-done.10.refs_9_), channel_id=1, source_target_pairs={{0,1},{1,0},{2,3},{3,2},{4,5},{5,4},{6,7},{7,6},{8,9},{9,8},{10,11... | collective-permute-start | bytes 786440 | tf_op jit(solution)/shard_map/ppermute | solution.py:261
  28.2 14.3 %collective-permute-start.14 = (bf16[256,512]{1,0:T(8,128)(2,1)S(1)}, bf16[256,512]{1,0:T(8,128)(2,1)S(1)}, u32[]{:S(2)}, u32[]{:S(2)}) collective-permute-start(bf16[256,512]{1,0:T(8,128)(2,1)S(1)} %collective-permute-done.13.refs_8_), channel_id=1, source_target_pairs={{0,1},{1,0},{2,3},{3,2},{4,5},{5,4},{6,7},{7,6},{8,9},{9,8},{10,11... | collective-permute-start | bytes 786440 | tf_op jit(solution)/shard_map/ppermute | solution.py:261
  29.5 0.7 %copy-start = (s32[2]{0:T(128)S(1)}, s32[2]{0:T(128)}, u32[]{:S(2)}) copy-start(s32[2]{0:T(128)} %length_ref.1) | copy-start | bytes 28

commit v3 on v2

--- a/solution.py
+++ b/solution.py
@@ -17,7 +17,6 @@
 ONES = 16
 
 VMEM = pl.BlockSpec(memory_space=pltpu.VMEM)
-SMEM = pl.BlockSpec(memory_space=pltpu.SMEM)
 HBM = pl.BlockSpec(memory_space=pltpu.HBM)
 BF16 = jnp.bfloat16
 F32 = jnp.float32
@@ -76,16 +75,22 @@
         copy.wait()
 
 
-def mask_columns(device, origin, window, cache_rows, prompt_rows):
+def mask_columns(device, origin, window, cache_rows, prompt_rows, near):
     keys = cache_rows + prompt_rows
     key = lax.broadcasted_iota(jnp.int32, (keys, HD), 0)
     feature = lax.broadcasted_iota(jnp.int32, (keys, HD), 1)
-    first, last = window
-    at = origin * cache_rows + key
-    outside = (key < cache_rows) & ((at < first) | (at >= last)) & (feature == prompt_rows)
-    reach = jnp.where(origin == device, 0, jnp.where(origin < device, -keys, keys + HD))
-    late = (key >= cache_rows) & (feature < prompt_rows) & (key - cache_rows + reach > feature)
-    return jnp.where(outside | late, MASKED, 0.0).astype(BF16)
+    low = window[0] - origin * cache_rows
+    high = jnp.minimum(window[1] - origin * cache_rows, cache_rows)
+    top = jnp.where(origin > device, cache_rows, keys)
+    cached = (key >= low) & (key < high)
+    new = key >= cache_rows
+    hidden = jnp.where(cached | new, 0.0, MASKED)
+    shown = cached | (new & (key < top))
+    masks = jnp.where(shown | (feature != prompt_rows), 0.0, MASKED)
+    if near:
+        late = (origin == device) & (feature < prompt_rows) & (key - cache_rows > feature)
+        masks = jnp.where(late, MASKED, masks)
+    return masks.astype(BF16), hidden
 
 
 def row_features(rows, prompt_rows):
@@ -101,14 +106,16 @@
 
 
 def prep_kernel(
-    length_ref, query_hbm, cont_hbm, key_hbm, value_hbm,
+    limit_ref, query_hbm, cont_hbm, key_hbm, value_hbm,
     q_ref, cont_q_ref, cont_max_ref, cont_total_ref,
     query_ref, cont_ref, key_ref, value_ref, sems,
 ):
     copies = [
         pltpu.make_async_copy(source, target, sems.at[index])
         for index, (source, target) in enumerate(
-            [(query_hbm, query_ref), (cont_hbm, cont_ref), (key_hbm, key_ref), (value_hbm, value_ref)]
+            [
+                (query_hbm, query_ref), (cont_hbm, cont_ref), (key_hbm, key_ref), (value_hbm, value_ref),
+            ]
         )
     ]
     for copy in copies:
@@ -139,7 +146,7 @@
         s = jnp.dot(key_ref[c], cont_q, preferred_element_type=F32)
         key = lax.broadcasted_iota(jnp.int32, s.shape, 0)
         owner = lax.broadcasted_iota(jnp.int32, s.shape, 1) % cont_rows // GROUP
-        scores.append(jnp.where((owner == c) & (key < length_ref[c]), s, MASKED))
+        scores.append(jnp.where((owner == c) & (key < limit_ref[2 + c : 3 + c, : KVH * cont_rows]), s, MASKED))
     s = jnp.concatenate(scores, axis=0)
     high = jnp.maximum(jnp.max(s, axis=0, keepdims=True), FLOOR)
     p = jnp.exp2((s - high) * SCALE).astype(BF16)
@@ -150,77 +157,84 @@
 
 
 def step_kernel(size, cache_rows, prompt_rows, sources, first_step, last_step, *refs):
-    first_ref, last_ref, q_ref, cont_q_ref = refs[:4]
-    held, refs = (refs[4:6], refs[6:]) if first_step else (refs[4:8], refs[8:])
+    limit_ref, q_ref, cont_q_ref = refs[:3]
+    held, refs = (refs[3:5], refs[5:]) if first_step else (refs[3:7], refs[7:])
     blocks, outs = refs[: len(sources)], refs[len(sources) :]
     device = lax.axis_index("ctx")
-    window = (first_ref[0], last_ref[0])
+    window = (limit_ref[0:1], limit_ref[1:2])
     keys = cache_rows + prompt_rows
-    rows = GROUP * prompt_rows
     cont_rows = cont_q_ref.shape[1] // KVH
-    masks = jnp.concatenate(
-        [
-            mask_columns(device, block_origin(device, *source, size), window, cache_rows, prompt_rows)
-            for source in sources
-        ],
-        axis=0,
-    )
+    pairs = [
+        mask_columns(
+            device, block_origin(device, *source, size), window, cache_rows, prompt_rows, first_step
+        )
+        for source in sources
+    ]
+    masks = jnp.concatenate([pair[0] for pair in pairs], axis=0)
+    hidden = jnp.concatenate([pair[1][:, :1] for pair in pairs], axis=0)
     ones = jnp.ones((ONES, len(blocks) * keys), BF16)
-
-    def merge(scores, old_max, old_total, values):
+    dot = functools.partial(jnp.dot, preferred_element_type=F32)
+    values = [
+        jnp.concatenate([block[keys:, g * keys : (g + 1) * keys] for block in blocks], axis=1)
+        for g in range(KVH)
+    ]
+
+    def cont_scores():
+        s = sum(
+            dot(
+                jnp.concatenate([block[:keys, cols] for block in blocks], axis=0), cont_q_ref[cols]
+            )
+            for cols in (slice(at, at + 2 * HD) for at in range(0, KVH * HD, 2 * HD))
+        )
+        return s + hidden
+
+    def head_scores(g):
+        cols = slice(g * HD, (g + 1) * HD)
+        k = jnp.concatenate([block[:keys, cols] for block in blocks], axis=0)
+        q = jnp.concatenate([q_ref[cols], q_ref[KVH * HD :]], axis=0)
+        return dot(jnp.concatenate([k, masks], axis=1), q)
+
+    def weigh(scores, old_max):
         new_max = jnp.maximum(old_max, jnp.max(scores, axis=0, keepdims=True))
         p = jnp.exp2((scores - new_max) * SCALE).astype(BF16)
-        total = values(p)
-        if old_total is not None:
-            total = total + old_total * jnp.exp2((old_max - new_max) * SCALE)
-        return new_max, total
-
-    values = []
-    for g in range(KVH):
-        cols = slice(g * HD, (g + 1) * HD)
-        k = jnp.concatenate([block[:keys, cols] for block in blocks], axis=0)
-        v = jnp.concatenate([block[keys:, g * keys : (g + 1) * keys] for block in blocks], axis=1)
-        values.append(v)
-        v = jnp.concatenate([v, ones], axis=0)
-        s = jnp.dot(
-            jnp.concatenate([k, masks], axis=1),
-            jnp.concatenate([q_ref[cols], q_ref[KVH * HD :]], axis=0),
-            preferred_element_type=F32,
-        )
-        old = (jnp.full((1, rows), FLOOR, F32), None) if first_step else (held[2][g], held[3][g])
-        new_max, total = merge(s, *old, lambda p: jnp.dot(v, p, preferred_element_type=F32))
+        return new_max, p, jnp.exp2((old_max - new_max) * SCALE)
+
+    def finish_cont(s):
+        new_max, p, old = weigh(s, held[0][...])
+        v = jnp.concatenate(values + [ones], axis=0)
+        total = own_head(dot(v, p), cont_rows) + held[1][...] * old
+        if not last_step:
+            outs[0][...] = new_max
+            outs[1][...] = total
+            return
+        result = (total[:HD] * (1.0 / total[HD : HD + 1])).T
+        for row in range(KVH * cont_rows):
+            g, c, h = row // cont_rows, row % cont_rows // GROUP, row % GROUP
+            cols = slice((g * GROUP + h) * HD, (g * GROUP + h + 1) * HD)
+            outs[1][c : c + 1, cols] = result[row : row + 1].astype(BF16)
+
+    def finish_head(g, s):
+        new_max, p, old = weigh(s, FLOOR if first_step else held[2][g])
+        total = dot(jnp.concatenate([values[g], ones], axis=0), p)
+        if not first_step:
+            total = total + held[3][g] * old
         if not last_step:
             outs[2][g] = new_max
             outs[3][g] = total
-            continue
+            return
         result = (total[:HD] * (1.0 / total[HD : HD + 1])).T.astype(BF16)
         for h in range(GROUP):
             cols = slice((g * GROUP + h) * HD, (g * GROUP + h + 1) * HD)
             outs[0][:, cols] = result[h * prompt_rows : (h + 1) * prompt_rows]
 
-    s = sum(
-        jnp.dot(
-            jnp.concatenate([block[:keys, half * 2 * HD : (half + 1) * 2 * HD] for block in blocks], axis=0),
-            cont_q_ref[half * 2 * HD : (half + 1) * 2 * HD],
-            preferred_element_type=F32,
-        )
-        for half in range(KVH // 2)
-    )
-    hidden = masks[:, prompt_rows : prompt_rows + 1].astype(F32)
-    v = jnp.concatenate(values + [ones], axis=0)
-    new_max, total = merge(
-        s + hidden, held[0][...], held[1][...],
-        lambda p: own_head(jnp.dot(v, p, preferred_element_type=F32), cont_rows),
-    )
-    if not last_step:
-        outs[0][...] = new_max
-        outs[1][...] = total
-        return
-    result = (total[:HD] * (1.0 / total[HD : HD + 1])).T
-    for row in range(KVH * cont_rows):
-        g, c, h = row // cont_rows, row % cont_rows // GROUP, row % GROUP
-        cols = slice((g * GROUP + h) * HD, (g * GROUP + h + 1) * HD)
-        outs[1][c : c + 1, cols] = result[row : row + 1].astype(BF16)
+    work = [(cont_scores, finish_cont)] + [
+        (functools.partial(head_scores, g), functools.partial(finish_head, g)) for g in range(KVH)
+    ]
+    ready = work[0][0]()
+    for index, (_, finish) in enumerate(work):
+        following = work[index + 1][0]() if index + 1 < len(work) else None
+        finish(ready)
+        ready = following
 
 
 def in_hbm(array):
@@ -276,13 +290,15 @@
         shape((KVH, 1, rows), F32),
         shape((KVH, HD + ONES, rows), F32),
     ]
+    limits = jnp.concatenate([window_start, prefix_length, suffix_length])
+    limits = jnp.broadcast_to(limits[:, None], (limits.shape[0], HD))
     queries, cont_q, *state = pl.pallas_call(
         prep_kernel,
         out_shape=[
             shape(((KVH + 1) * HD, rows), BF16),
             shape((KVH * HD, cont_rows), BF16),
         ] + state_shape[:2],
-        in_specs=[SMEM] + [HBM] * 4,
+        in_specs=[VMEM] + [HBM] * 4,
         out_specs=[VMEM] * 4,
         scratch_shapes=[
             pltpu.VMEM(new_queries.shape, BF16),
@@ -293,37 +309,38 @@
         ],
         compiler_params=params,
         cost_estimate=cost(rows, keys),
-    )(suffix_length, *[in_hbm(x) for x in (new_queries, cont_queries, suffix_keys, suffix_values)])
-
-    def step(state, sources, blocks, last_step=False):
+    )(limits, *[in_hbm(x) for x in (new_queries, cont_queries, suffix_keys, suffix_values)])
+
+    def take(state, sources, blocks, last_step=False):
         first_step = len(state) == 2
         outs = [shape(new_queries.shape, BF16), shape(cont_queries.shape, BF16)]
         outs = outs if last_step else state_shape
-        aliases = {} if last_step else {4 + index: index for index in range(len(state))}
+        aliases = {} if last_step else {3 + index: index for index in range(len(state))}
         return pl.pallas_call(
             functools.partial(
                 step_kernel, size, cache_rows, prompt_rows, sources, first_step, last_step
             ),
             out_shape=outs,
-            in_specs=[SMEM] * 2 + [VMEM] * (2 + len(state) + len(blocks)),
+            in_specs=[VMEM] * (3 + len(state) + len(blocks)),
             out_specs=[VMEM] * len(outs),
             input_output_aliases=aliases,
             compiler_params=params,
             cost_estimate=cost(rows, len(blocks) * keys),
-        )(window_start, prefix_length, queries, cont_q, *state, *blocks)
-
-    state = step(state, [(0, False, False), (0, False, True)], [own, other])
-    for hop in range(1, chips // 2):
+        )(limits, queries, cont_q, *state, *blocks)
+
+    state = take(state, [(0, False, False), (0, False, True)], [own, other])
+    hops = chips // 2
+    for hop in range(1, hops + 1):
         own = send(own, ring)
-        other = send(other, ring)
-        blocks = [own, other, send(own, pair), send(other, pair)]
-        sources = [(hop, False, False), (hop, False, True), (hop, True, False), (hop, True, True)]
-        state = step(state, sources, blocks)
-    hop = chips // 2
-    own = send(own, ring)
-    sources = [(hop, False, False), (hop, True, False)]
-    blocks = [own, send(own, pair)]
-    return tuple(step(state, sources, blocks, last_step=True))
+        sources = [(hop, False, False), (hop, True, False)]
+        blocks = [own, send(own, pair)]
+        state = take(state, sources, blocks, last_step=hop == hops)
+        if hop < hops:
+            other = send(other, ring)
+            sources = [(hop, False, True), (hop, True, True)]
+            blocks = [other, send(other, pair)]
+            state = take(state, sources, blocks)
+    return tuple(state)
 
 
 def solution(mesh):

time: 45.5 us -> 43.3 us (0.952)
  Pallas kernels: 16 us -> 13.6 us
  other arithmetic: 0 us -> 0.73 us
  local copies, waits for them, and re-layouts: 0.65 us -> 0.07 us
    pallas_call x5 -> x8, Pallas kernels: 12.7 us -> 10.8 us  [take(): pl.pallas_call(functools.partial(step_kernel, size, cache_rows, prompt_ro...]
    concatenate x0 -> x1, other arithmetic: none -> 0.73 us  [body(): limits = jnp.concatenate([window_start, prefix_length, suffix_length])]
    unnamed x2 -> x0, local copies, waits for them, and re-layouts: 0.65 us -> none
    pallas_call x1, Pallas kernels: 2.32 us -> 1.78 us  [body(): pl.pallas_call(prep_kernel, out_shape=[shape(((KVH + 1) * HD, rows), BF16...]
  transfers between devices with their start and end apart: 15 -> 15, of which waited for: 7 -> 7; matrix products, arithmetic and copies ran while one was open for 0% -> 2% of each run, Pallas kernels for 27% -> 24%
where the time goes in v3:
time: 43.3 us; the launch traced here: 43.1 us
  starting transfers between devices  16.5 us (38%)
  Pallas kernels  13.6 us (31%)
  waiting for transfers between devices  10.1 us (23%)
  between operations  2.05 us (5%)
  other arithmetic  0.73 us (2%)
    ppermute x15, starting transfers between devices, send(): return lax.ppermute(block, 'ctx', pairs)  16.5 us
    pallas_call x8, Pallas kernels, take(): pl.pallas_call(functools.partial(step_kernel, size, cache_rows, prompt_ro...  10.8 us
    ppermute x15, waiting for transfers between devices, send(): return lax.ppermute(block, 'ctx', pairs)  10.1 us
    pallas_call x1, Pallas kernels, body(): pl.pallas_call(prep_kernel, out_shape=[shape(((KVH + 1) * HD, rows), BF16...  1.78 us
    pallas_call x1, Pallas kernels, body(): pl.pallas_call(pack_kernel, out_shape=shape((keys + HD, KVH * HD), BF16),...  1 us
  transfers between devices with their start and end apart: 15, of which 7 were waited for; matrix products, arithmetic and copies ran while one was open for 2% of the time, Pallas kernels for 24%

profile of v3, /device:TPU:0, one launch (start us, length us, event | category | flops | bytes accessed | tf_op | source)
XLA Modules:
  0.0 43.1 jit_solution(15485231465275106297)
XLA Ops:
  0.6 1.0 %shard_map.123.refs_5_ = bf16[256,512]{1,0:T(8,128)(2,1)S(1)} custom-call(bf16[64,512]{1,0:T(8,128)(2,1)} %ck_ref.1, bf16[64,512]{1,0:T(8,128)(2,1)} %nk_ref.1, bf16[64,512]{1,0:T(8,128)(2,1)} %cv_ref.1, bf16[64,512]{1,0:T(8,128)(2,1)} %nv_ref.1), custom_call_target="tpu_custom_call" | custom-call | tf_op jit(solution)/shard_map/pallas_call | solution.py:277
  1.6 0.6 %collective-permute-start = (bf16[256,512]{1,0:T(8,128)(2,1)S(1)}, bf16[256,512]{1,0:T(8,128)(2,1)S(1)}, u32[]{:S(2)}, u32[]{:S(2)}) collective-permute-start(bf16[256,512]{1,0:T(8,128)(2,1)S(1)} %shard_map.123.refs_5_), channel_id=1, source_target_pairs={{0,1},{1,0},{2,3},{3,2},{4,5},{5,4},{6,7},{7,6},{8,9},{9,8},{10,11... | collective-permute-start | bytes 786440 | tf_op jit(solution)/shard_map/ppermute | solution.py:275
  2.2 2.6 %collective-permute-start.1 = (bf16[256,512]{1,0:T(8,128)(2,1)S(1)}, bf16[256,512]{1,0:T(8,128)(2,1)S(1)}, u32[]{:S(2)}, u32[]{:S(2)}) collective-permute-start(bf16[256,512]{1,0:T(8,128)(2,1)S(1)} %shard_map.123.refs_5_), channel_id=1, source_target_pairs={{0,4},{1,3},{2,0},{3,7},{4,8},{5,1},{6,2},{7,11},{8,12},{9,5},{10,... | collective-permute-start | bytes 786440 | tf_op jit(solution)/shard_map/ppermute | solution.py:275
  4.8 0.0 collective-permute-done.refs_6_
  4.8 1.6 %collective-permute-start.3 = (bf16[256,512]{1,0:T(8,128)(2,1)S(1)}, bf16[256,512]{1,0:T(8,128)(2,1)S(1)}, u32[]{:S(2)}, u32[]{:S(2)}) collective-permute-start(bf16[256,512]{1,0:T(8,128)(2,1)S(1)} %collective-permute-done.refs_6_), channel_id=1, source_target_pairs={{0,4},{1,3},{2,0},{3,7},{4,8},{5,1},{6,2},{7,11},{8,12},{9,5},{10,... | collective-permute-start | bytes 786440 | tf_op jit(solution)/shard_map/ppermute | solution.py:275
  6.4 2.7 %collective-permute-done.1.refs_7_ = bf16[256,512]{1,0:T(8,128)(2,1)S(1)} collective-permute-done((bf16[256,512]{1,0:T(8,128)(2,1)S(1)}, bf16[256,512]{1,0:T(8,128)(2,1)S(1)}, u32[]{:S(2)}, u32[]{:S(2)}) %collective-permute-start.1) | collective-permute-done | bytes 262176 | tf_op jit(solution)/shard_map/ppermute | solution.py:275
  9.1 2.1 %collective-permute-start.5 = (bf16[256,512]{1,0:T(8,128)(2,1)S(1)}, bf16[256,512]{1,0:T(8,128)(2,1)S(1)}, u32[]{:S(2)}, u32[]{:S(2)}) collective-permute-start(bf16[256,512]{1,0:T(8,128)(2,1)S(1)} %collective-permute-done.1.refs_7_), channel_id=1, source_target_pairs={{0,4},{1,3},{2,0},{3,7},{4,8},{5,1},{6,2},{7,11},{8,12},{9,5},{10,... | collective-permute-start | bytes 786440 | tf_op jit(solution)/shard_map/ppermute | solution.py:275
  11.2 0.7 %collective-permute-done.3.refs_7_ = bf16[256,512]{1,0:T(8,128)(2,1)S(1)} collective-permute-done((bf16[256,512]{1,0:T(8,128)(2,1)S(1)}, bf16[256,512]{1,0:T(8,128)(2,1)S(1)}, u32[]{:S(2)}, u32[]{:S(2)}) %collective-permute-start.3) | collective-permute-done | bytes 262176 | tf_op jit(solution)/shard_map/ppermute | solution.py:275
  11.9 2.1 %collective-permute-start.7 = (bf16[256,512]{1,0:T(8,128)(2,1)S(1)}, bf16[256,512]{1,0:T(8,128)(2,1)S(1)}, u32[]{:S(2)}, u32[]{:S(2)}) collective-permute-start(bf16[256,512]{1,0:T(8,128)(2,1)S(1)} %collective-permute-done.3.refs_7_), channel_id=1, source_target_pairs={{0,4},{1,3},{2,0},{3,7},{4,8},{5,1},{6,2},{7,11},{8,12},{9,5},{10,... | collective-permute-start | bytes 786440 | tf_op jit(solution)/shard_map/ppermute | solution.py:275
  14.0 1.5 %collective-permute-done.5.refs_7_ = bf16[256,512]{1,0:T(8,128)(2,1)S(1)} collective-permute-done((bf16[256,512]{1,0:T(8,128)(2,1)S(1)}, bf16[256,512]{1,0:T(8,128)(2,1)S(1)}, u32[]{:S(2)}, u32[]{:S(2)}) %collective-permute-start.5) | collective-permute-done | bytes 262176 | tf_op jit(solution)/shard_map/ppermute | solution.py:275
  15.5 2.1 %collective-permute-start.9 = (bf16[256,512]{1,0:T(8,128)(2,1)S(1)}, bf16[256,512]{1,0:T(8,128)(2,1)S(1)}, u32[]{:S(2)}, u32[]{:S(2)}) collective-permute-start(bf16[256,512]{1,0:T(8,128)(2,1)S(1)} %collective-permute-done.5.refs_7_), channel_id=1, source_target_pairs={{0,4},{1,3},{2,0},{3,7},{4,8},{5,1},{6,2},{7,11},{8,12},{9,5},{10,... | collective-permute-start | bytes 786440 | tf_op jit(solution)/shard_map/ppermute | solution.py:275
  17.6 0.0 collective-permute-start.2
  17.6 0.5 %collective-permute-start.4 = (bf16[256,512]{1,0:T(8,128)(2,1)S(1)}, bf16[256,512]{1,0:T(8,128)(2,1)S(1)}, u32[]{:S(2)}, u32[]{:S(2)}) collective-permute-start(bf16[256,512]{1,0:T(8,128)(2,1)S(1)} %collective-permute-done.3.refs_7_), channel_id=1, source_target_pairs={{0,1},{1,0},{2,3},{3,2},{4,5},{5,4},{6,7},{7,6},{8,9},{9,8},{10,11... | collective-permute-start | bytes 786440 | tf_op jit(solution)/shard_map/ppermute | solution.py:275
  18.1 0.2 collective-permute-done.7.refs_7_
  18.3 2.1 %collective-permute-start.11 = (bf16[256,512]{1,0:T(8,128)(2,1)S(1)}, bf16[256,512]{1,0:T(8,128)(2,1)S(1)}, u32[]{:S(2)}, u32[]{:S(2)}) collective-permute-start(bf16[256,512]{1,0:T(8,128)(2,1)S(1)} %collective-permute-done.7.refs_7_), channel_id=1, source_target_pairs={{0,4},{1,3},{2,0},{3,7},{4,8},{5,1},{6,2},{7,11},{8,12},{9,5},{10,... | collective-permute-start | bytes 786440 | tf_op jit(solution)/shard_map/ppermute | solution.py:275
  20.4 1.5 %collective-permute-done.9.refs_7_ = bf16[256,512]{1,0:T(8,128)(2,1)S(1)} collective-permute-done((bf16[256,512]{1,0:T(8,128)(2,1)S(1)}, bf16[256,512]{1,0:T(8,128)(2,1)S(1)}, u32[]{:S(2)}, u32[]{:S(2)}) %collective-permute-start.9) | collective-permute-done | bytes 262176 | tf_op jit(solution)/shard_map/ppermute | solution.py:275
  21.9 2.1 %collective-permute-start.13 = (bf16[256,512]{1,0:T(8,128)(2,1)S(1)}, bf16[256,512]{1,0:T(8,128)(2,1)S(1)}, u32[]{:S(2)}, u32[]{:S(2)}) collective-permute-start(bf16[256,512]{1,0:T(8,128)(2,1)S(1)} %collective-permute-done.9.refs_7_), channel_id=1, source_target_pairs={{0,4},{1,3},{2,0},{3,7},{4,8},{5,1},{6,2},{7,11},{8,12},{9,5},{10,... | collective-permute-start | bytes 786440 | tf_op jit(solution)/shard_map/ppermute | solution.py:275
  23.9 0.0 collective-permute-start.6
  23.9 0.0 collective-permute-done.2.refs_8_
  23.9 0.5 %collective-permute-start.8 = (bf16[256,512]{1,0:T(8,128)(2,1)S(1)}, bf16[256,512]{1,0:T(8,128)(2,1)S(1)}, u32[]{:S(2)}, u32[]{:S(2)}) collective-permute-start(bf16[256,512]{1,0:T(8,128)(2,1)S(1)} %collective-permute-done.7.refs_7_), channel_id=1, source_target_pairs={{0,1},{1,0},{2,3},{3,2},{4,5},{5,4},{6,7},{7,6},{8,9},{9,8},{10,11... | collective-permute-start | bytes 786440 | tf_op jit(solution)/shard_map/ppermute | solution.py:275
  24.5 0.0 collective-permute-done.4.refs_8_
  24.5 0.1 collective-permute-start.10
  24.5 0.1 collective-permute-done.11.refs_7_
  24.7 0.3 collective-permute-start.12
  25.0 3.3 %collective-permute-done.13.refs_7_ = bf16[256,512]{1,0:T(8,128)(2,1)S(1)} collective-permute-done((bf16[256,512]{1,0:T(8,128)(2,1)S(1)}, bf16[256,512]{1,0:T(8,128)(2,1)S(1)}, u32[]{:S(2)}, u32[]{:S(2)}) %collective-permute-start.13) | collective-permute-done | bytes 262176 | tf_op jit(solution)/shard_map/ppermute | solution.py:275
  28.2 0.0 collective-permute-start.14
  29.5 0.7 %pad_add_fusion = s32[4]{0:T(128)S(1)} fusion(s32[2]{0:T(128)} %param.21, s32[1]{0:T(128)S(6)} %copy.66, s32[1]{0:T(128)S(6)} %copy.65), kind=kLoop, calls=%fused_computation | loop fusion | flops 8 | bytes 32 | tf_op jit(solution)/shard_map/concatenate | solution.py:293
  30.3 0.1 broadcast_in_dim.2.limit_ref.refs_0_
  30.3 1.8 %shard_map.122 = (bf16[640,512]{1,0:T(8,128)(2,1)S(1)}, bf16[512,64]{1,0:T(8,128)(2,1)S(1)}, f32[1,64]{1,0:T(1,128)S(1)}, f32[144,64]{1,0:T(8,128)S(1)}) custom-call(s32[4,128]{1,0:T(4,128)S(1)} %broadcast_in_dim.2.limit_ref.refs_0_, bf16[64,4096]{1,0:T(8,128)(2,1)} %query_hbm.1, bf16[2,4096]{1,0:T(2,128)(2,1)} %cont_hbm.1, bf16[2,128,512]{2,1,0:T(8,128)(2,1)} %key_hbm.1, ...), custom_call_target="tpu_custom_call" | custom-call | flops 67108864 | bytes 1048576 | tf_op jit(solution)/shard_map/pallas_call | solution.py:295
  32.1 1.1 %shard_map.124 = (f32[1,64]{1,0:T(1,128)S(1)}, f32[144,64]{1,0:T(8,128)S(1)}, f32[4,1,512]{2,1,0:T(1,128)S(1)}, f32[4,144,512]{2,1,0:T(8,128)S(1)}) custom-call(s32[4,128]{1,0:T(4,128)S(1)} %broadcast_in_dim.2.limit_ref.refs_0_, bf16[640,512]{1,0:T(8,128)(2,1)S(1)} %get-tuple-element.34.refs_1_, ...), custom_call_target="tpu_custom_call", output_to_operand_aliasing={{0}: (3, {}), {1}: (4, {})} | custom-call | flops 134217728 | bytes 1048576 | tf_op jit(solution)/shard_map/pallas_call | solution.py:319
  33.2 1.3 %shard_map.125 = (f32[1,64]{1,0:T(1,128)S(1)}, f32[144,64]{1,0:T(8,128)S(1)}, f32[4,1,512]{2,1,0:T(1,128)S(1)}, f32[4,144,512]{2,1,0:T(8,128)S(1)}) custom-call(s32[4,128]{1,0:T(4,128)S(1)} %broadcast_in_dim.2.limit_ref.refs_0_, ...), custom_call_target="tpu_custom_call", output_to_operand_aliasing={{0}: (3, {}), {1}: (4, {}), {2}: (5, {}), {3}: (6, {})} | custom-call | flops 134217728 | bytes 1048576 | tf_op jit(solution)/shard_map/pallas_call | solution.py:319
  34.5 1.3 %shard_map.126 = (f32[1,64]{1,0:T(1,128)S(1)}, f32[144,64]{1,0:T(8,128)S(1)}, f32[4,1,512]{2,1,0:T(1,128)S(1)}, f32[4,144,512]{2,1,0:T(8,128)S(1)}) custom-call(s32[4,128]{1,0:T(4,128)S(1)} %broadcast_in_dim.2.limit_ref.refs_0_, ...), custom_call_target="tpu_custom_call", output_to_operand_aliasing={{0}: (3, {}), {1}: (4, {}), {2}: (5, {}), {3}: (6, {})} | custom-call | flops 134217728 | bytes 1048576 | tf_op jit(solution)/shard_map/pallas_call | solution.py:319
  35.8 0.0 collective-permute-done.6.refs_8_
  35.8 1.3 %shard_map.127 = (f32[1,64]{1,0:T(1,128)S(1)}, f32[144,64]{1,0:T(8,128)S(1)}, f32[4,1,512]{2,1,0:T(1,128)S(1)}, f32[4,144,512]{2,1,0:T(8,128)S(1)}) custom-call(s32[4,128]{1,0:T(4,128)S(1)} %broadcast_in_dim.2.limit_ref.refs_0_, ...), custom_call_target="tpu_custom_call", output_to_operand_aliasing={{0}: (3, {}), {1}: (4, {}), {2}: (5, {}), {3}: (6, {})} | custom-call | flops 134217728 | bytes 1048576 | tf_op jit(solution)/shard_map/pallas_call | solution.py:319
  37.1 0.0 collective-permute-done.8.refs_8_
  37.1 1.3 %shard_map.128 = (f32[1,64]{1,0:T(1,128)S(1)}, f32[144,64]{1,0:T(8,128)S(1)}, f32[4,1,512]{2,1,0:T(1,128)S(1)}, f32[4,144,512]{2,1,0:T(8,128)S(1)}) custom-call(s32[4,128]{1,0:T(4,128)S(1)} %broadcast_in_dim.2.limit_ref.refs_0_, ...), custom_call_target="tpu_custom_call", output_to_operand_aliasing={{0}: (3, {}), {1}: (4, {}), {2}: (5, {}), {3}: (6, {})} | custom-call | flops 134217728 | bytes 1048576 | tf_op jit(solution)/shard_map/pallas_call | solution.py:319
  38.4 0.0 collective-permute-done.10.refs_8_
  38.4 1.3 %shard_map.129 = (f32[1,64]{1,0:T(1,128)S(1)}, f32[144,64]{1,0:T(8,128)S(1)}, f32[4,1,512]{2,1,0:T(1,128)S(1)}, f32[4,144,512]{2,1,0:T(8,128)S(1)}) custom-call(s32[4,128]{1,0:T(4,128)S(1)} %broadcast_in_dim.2.limit_ref.refs_0_, ...), custom_call_target="tpu_custom_call", output_to_operand_aliasing={{0}: (3, {}), {1}: (4, {}), {2}: (5, {}), {3}: (6, {})} | custom-call | flops 134217728 | bytes 1048576 | tf_op jit(solution)/shard_map/pallas_call | solution.py:319
  39.7 0.0 collective-permute-done.12.refs_8_
  39.7 1.3 %shard_map.130 = (f32[1,64]{1,0:T(1,128)S(1)}, f32[144,64]{1,0:T(8,128)S(1)}, f32[4,1,512]{2,1,0:T(1,128)S(1)}, f32[4,144,512]{2,1,0:T(8,128)S(1)}) custom-call(s32[4,128]{1,0:T(4,128)S(1)} %broadcast_in_dim.2.limit_ref.refs_0_, ...), custom_call_target="tpu_custom_call", output_to_operand_aliasing={{0}: (3, {}), {1}: (4, {}), {2}: (5, {}), {3}: (6, {})} | custom-call | flops 134217728 | bytes 1048576 | tf_op jit(solution)/shard_map/pallas_call | solution.py:319
  41.0 0.0 collective-permute-done.14.refs_8_
  41.0 2.1 %shard_map.131 = (bf16[64,4096]{1,0:T(8,128)(2,1)}, bf16[2,4096]{1,0:T(2,128)(2,1)}) custom-call(s32[4,128]{1,0:T(4,128)S(1)} %broadcast_in_dim.2.limit_ref.refs_0_, bf16[640,512]{1,0:T(8,128)(2,1)S(1)} %get-tuple-element.34.refs_1_, bf16[512,64]{1,0:T(8,128)(2,1)S(1)} %get-tuple-element.35.refs_2_, f32[1,64]{1,0:T(1,128)S(1)} %get-tuple-element.62.refs_3_, ...), custom_call_target="tpu_custom_call" | custom-call | flops 134217728 | bytes 1048576 | tf_op jit(solution)/shard_map/pallas_call | solution.py:319
Async XLA Ops:
  1.6 3.2 %collective-permute-start = (bf16[256,512]{1,0:T(8,128)(2,1)S(1)}, bf16[256,512]{1,0:T(8,128)(2,1)S(1)}, u32[]{:S(2)}, u32[]{:S(2)}) collective-permute-start(bf16[256,512]{1,0:T(8,128)(2,1)S(1)} %shard_map.123.refs_5_), channel_id=1, source_target_pairs={{0,1},{1,0},{2,3},{3,2},{4,5},{5,4},{6,7},{7,6},{8,9},{9,8},{10,11... | collective-permute-start | bytes 786440 | tf_op jit(solution)/shard_map/ppermute | solution.py:275
  2.2 6.9 %collective-permute-start.1 = (bf16[256,512]{1,0:T(8,128)(2,1)S(1)}, bf16[256,512]{1,0:T(8,128)(2,1)S(1)}, u32[]{:S(2)}, u32[]{:S(2)}) collective-permute-start(bf16[256,512]{1,0:T(8,128)(2,1)S(1)} %shard_map.123.refs_5_), channel_id=1, source_target_pairs={{0,4},{1,3},{2,0},{3,7},{4,8},{5,1},{6,2},{7,11},{8,12},{9,5},{10,... | collective-permute-start | bytes 786440 | tf_op jit(solution)/shard_map/ppermute | solution.py:275
  4.8 7.1 %collective-permute-start.3 = (bf16[256,512]{1,0:T(8,128)(2,1)S(1)}, bf16[256,512]{1,0:T(8,128)(2,1)S(1)}, u32[]{:S(2)}, u32[]{:S(2)}) collective-permute-start(bf16[256,512]{1,0:T(8,128)(2,1)S(1)} %collective-permute-done.refs_6_), channel_id=1, source_target_pairs={{0,4},{1,3},{2,0},{3,7},{4,8},{5,1},{6,2},{7,11},{8,12},{9,5},{10,... | collective-permute-start | bytes 786440 | tf_op jit(solution)/shard_map/ppermute | solution.py:275
  9.1 6.4 %collective-permute-start.5 = (bf16[256,512]{1,0:T(8,128)(2,1)S(1)}, bf16[256,512]{1,0:T(8,128)(2,1)S(1)}, u32[]{:S(2)}, u32[]{:S(2)}) collective-permute-start(bf16[256,512]{1,0:T(8,128)(2,1)S(1)} %collective-permute-done.1.refs_7_), channel_id=1, source_target_pairs={{0,4},{1,3},{2,0},{3,7},{4,8},{5,1},{6,2},{7,11},{8,12},{9,5},{10,... | collective-permute-start | bytes 786440 | tf_op jit(solution)/shard_map/ppermute | solution.py:275
  11.9 6.4 %collective-permute-start.7 = (bf16[256,512]{1,0:T(8,128)(2,1)S(1)}, bf16[256,512]{1,0:T(8,128)(2,1)S(1)}, u32[]{:S(2)}, u32[]{:S(2)}) collective-permute-start(bf16[256,512]{1,0:T(8,128)(2,1)S(1)} %collective-permute-done.3.refs_7_), channel_id=1, source_target_pairs={{0,4},{1,3},{2,0},{3,7},{4,8},{5,1},{6,2},{7,11},{8,12},{9,5},{10,... | collective-permute-start | bytes 786440 | tf_op jit(solution)/shard_map/ppermute | solution.py:275
  15.5 6.4 %collective-permute-start.9 = (bf16[256,512]{1,0:T(8,128)(2,1)S(1)}, bf16[256,512]{1,0:T(8,128)(2,1)S(1)}, u32[]{:S(2)}, u32[]{:S(2)}) collective-permute-start(bf16[256,512]{1,0:T(8,128)(2,1)S(1)} %collective-permute-done.5.refs_7_), channel_id=1, source_target_pairs={{0,4},{1,3},{2,0},{3,7},{4,8},{5,1},{6,2},{7,11},{8,12},{9,5},{10,... | collective-permute-start | bytes 786440 | tf_op jit(solution)/shard_map/ppermute | solution.py:275
  17.6 6.4 %collective-permute-start.2 = (bf16[256,512]{1,0:T(8,128)(2,1)S(1)}, bf16[256,512]{1,0:T(8,128)(2,1)S(1)}, u32[]{:S(2)}, u32[]{:S(2)}) collective-permute-start(bf16[256,512]{1,0:T(8,128)(2,1)S(1)} %collective-permute-done.1.refs_7_), channel_id=1, source_target_pairs={{0,1},{1,0},{2,3},{3,2},{4,5},{5,4},{6,7},{7,6},{8,9},{9,8},{10,11... | collective-permute-start | bytes 786440 | tf_op jit(solution)/shard_map/ppermute | solution.py:275
  17.6 6.9 %collective-permute-start.4 = (bf16[256,512]{1,0:T(8,128)(2,1)S(1)}, bf16[256,512]{1,0:T(8,128)(2,1)S(1)}, u32[]{:S(2)}, u32[]{:S(2)}) collective-permute-start(bf16[256,512]{1,0:T(8,128)(2,1)S(1)} %collective-permute-done.3.refs_7_), channel_id=1, source_target_pairs={{0,1},{1,0},{2,3},{3,2},{4,5},{5,4},{6,7},{7,6},{8,9},{9,8},{10,11... | collective-permute-start | bytes 786440 | tf_op jit(solution)/shard_map/ppermute | solution.py:275
  18.3 6.4 %collective-permute-start.11 = (bf16[256,512]{1,0:T(8,128)(2,1)S(1)}, bf16[256,512]{1,0:T(8,128)(2,1)S(1)}, u32[]{:S(2)}, u32[]{:S(2)}) collective-permute-start(bf16[256,512]{1,0:T(8,128)(2,1)S(1)} %collective-permute-done.7.refs_7_), channel_id=1, source_target_pairs={{0,4},{1,3},{2,0},{3,7},{4,8},{5,1},{6,2},{7,11},{8,12},{9,5},{10,... | collective-permute-start | bytes 786440 | tf_op jit(solution)/shard_map/ppermute | solution.py:275
  21.9 6.4 %collective-permute-start.13 = (bf16[256,512]{1,0:T(8,128)(2,1)S(1)}, bf16[256,512]{1,0:T(8,128)(2,1)S(1)}, u32[]{:S(2)}, u32[]{:S(2)}) collective-permute-start(bf16[256,512]{1,0:T(8,128)(2,1)S(1)} %collective-permute-done.9.refs_7_), channel_id=1, source_target_pairs={{0,4},{1,3},{2,0},{3,7},{4,8},{5,1},{6,2},{7,11},{8,12},{9,5},{10,... | collective-permute-start | bytes 786440 | tf_op jit(solution)/shard_map/ppermute | solution.py:275
  23.9 11.8 %collective-permute-start.6 = (bf16[256,512]{1,0:T(8,128)(2,1)S(1)}, bf16[256,512]{1,0:T(8,128)(2,1)S(1)}, u32[]{:S(2)}, u32[]{:S(2)}) collective-permute-start(bf16[256,512]{1,0:T(8,128)(2,1)S(1)} %collective-permute-done.5.refs_7_), channel_id=1, source_target_pairs={{0,1},{1,0},{2,3},{3,2},{4,5},{5,4},{6,7},{7,6},{8,9},{9,8},{10,11... | collective-permute-start | bytes 786440 | tf_op jit(solution)/shard_map/ppermute | solution.py:275
  23.9 13.1 %collective-permute-start.8 = (bf16[256,512]{1,0:T(8,128)(2,1)S(1)}, bf16[256,512]{1,0:T(8,128)(2,1)S(1)}, u32[]{:S(2)}, u32[]{:S(2)}) collective-permute-start(bf16[256,512]{1,0:T(8,128)(2,1)S(1)} %collective-permute-done.7.refs_7_), channel_id=1, source_target_pairs={{0,1},{1,0},{2,3},{3,2},{4,5},{5,4},{6,7},{7,6},{8,9},{9,8},{10,11... | collective-permute-start | bytes 786440 | tf_op jit(solution)/shard_map/ppermute | solution.py:275
  24.5 13.9 %collective-permute-start.10 = (bf16[256,512]{1,0:T(8,128)(2,1)S(1)}, bf16[256,512]{1,0:T(8,128)(2,1)S(1)}, u32[]{:S(2)}, u32[]{:S(2)}) collective-permute-start(bf16[256,512]{1,0:T(8,128)(2,1)S(1)} %collective-permute-done.9.refs_7_), channel_id=1, source_target_pairs={{0,1},{1,0},{2,3},{3,2},{4,5},{5,4},{6,7},{7,6},{8,9},{9,8},{10,11... | collective-permute-start | bytes 786440 | tf_op jit(solution)/shard_map/ppermute | solution.py:275
  24.7 15.0 %collective-permute-start.12 = (bf16[256,512]{1,0:T(8,128)(2,1)S(1)}, bf16[256,512]{1,0:T(8,128)(2,1)S(1)}, u32[]{:S(2)}, u32[]{:S(2)}) collective-permute-start(bf16[256,512]{1,0:T(8,128)(2,1)S(1)} %collective-permute-done.11.refs_7_), channel_id=1, source_target_pairs={{0,1},{1,0},{2,3},{3,2},{4,5},{5,4},{6,7},{7,6},{8,9},{9,8},{10,11... | collective-permute-start | bytes 786440 | tf_op jit(solution)/shard_map/ppermute | solution.py:275
  28.2 12.8 %collective-permute-start.14 = (bf16[256,512]{1,0:T(8,128)(2,1)S(1)}, bf16[256,512]{1,0:T(8,128)(2,1)S(1)}, u32[]{:S(2)}, u32[]{:S(2)}) collective-permute-start(bf16[256,512]{1,0:T(8,128)(2,1)S(1)} %collective-permute-done.13.refs_7_), channel_id=1, source_target_pairs={{0,1},{1,0},{2,3},{3,2},{4,5},{5,4},{6,7},{7,6},{8,9},{9,8},{10,11... | collective-permute-start | bytes 786440 | tf_op jit(solution)/shard_map/ppermute | solution.py:275

commit v4 on v3

v4 whole, which is shorter than its diff:
```python
import functools
import math

import jax
import jax.numpy as jnp
from jax import lax
from jax.experimental import pallas as pl
from jax.experimental.pallas import tpu as pltpu
from jax.sharding import PartitionSpec as P

KVH = 4
HD = 128
GROUP = 8
SCALE = HD ** (-0.5) * math.log2(math.e)
MASKED = -1e30
FLOOR = -1e20
ONES = 16
AHEAD = 3

VMEM = pl.BlockSpec(memory_space=pltpu.VMEM)
SMEM = pl.BlockSpec(memory_space=pltpu.SMEM)
HBM = pl.BlockSpec(memory_space=pltpu.HBM)
BF16 = jnp.bfloat16
F32 = jnp.float32


def ring_chip(place, chips):
    return jnp.where(place < chips // 2, 2 * place, 2 * (chips - 1 - place) + 1)


def ring_place(chip, chips):
    return jnp.where(chip % 2 == 0, chip // 2, chips - 1 - chip // 2)


def ring_pairs(size):
    chips = size // 2
    order = list(range(0, chips, 2)) + list(range(chips - 1, 0, -2))
    place = {chip: index for index, chip in enumerate(order)}
    pairs = []
    for device in range(size):
        chip, core = divmod(device, 2)
        step = 1 if core == 0 else -1
        pairs.append((device, 2 * order[(place[chip] + step) % chips] + core))
    return pairs


def block_origin(device, hop, swapped, partner, size):
    chips = size // 2
    chip, core = device // 2, device % 2
    via = 1 - core if swapped else core
    held = 1 - via if partner else via
    place = ring_place(chip, chips) + jnp.where(via == 0, -hop, hop)
    place = lax.rem(place + 2 * chips, chips)
    return 2 * ring_chip(place, chips) + held


def pack_kernel(ck_hbm, nk_hbm, cv_hbm, nv_hbm, *refs):
    others, out_ref, targets, value_ref, sems = refs[:4], refs[4], refs[5:9], refs[9], refs[10]
    cache_rows, keys = ck_hbm.shape[0], value_ref.shape[0]
    copies = [
        pltpu.make_async_copy(source, target, sems.at[index])
        for index, (source, target) in enumerate(
            [
                (cv_hbm, value_ref.at[:cache_rows]),
                (nv_hbm, value_ref.at[cache_rows:]),
                (ck_hbm, out_ref.at[:cache_rows]),
                (nk_hbm, out_ref.at[cache_rows:keys]),
                *zip(others, targets),
            ]
        )
    ]
    for copy in copies:
        copy.start()
    for copy in copies[:2]:
        copy.wait()
    for g in range(KVH):
        out_ref[keys:, g * keys : (g + 1) * keys] = value_ref[:, g * HD : (g + 1) * HD].T
    for copy in copies[2:]:
        copy.wait()


def mask_columns(device, origin, window, cache_rows, prompt_rows, near):
    keys = cache_rows + prompt_rows
    key = lax.broadcasted_iota(jnp.int32, (keys, HD), 0)
    feature = lax.broadcasted_iota(jnp.int32, (keys, HD), 1)
    low = window[0] - origin * cache_rows
    high = jnp.minimum(window[1] - origin * cache_rows, cache_rows)
    top = jnp.where(origin > device, cache_rows, keys)
    cached = (key >= low) & (key < high)
    new = key >= cache_rows
    hidden = jnp.where(cached | new, 0.0, MASKED)
    shown = cached | (new & (key < top))
    masks = jnp.where(shown | (feature != prompt_rows), 0.0, MASKED)
    if near:
        late = (origin == device) & (feature < prompt_rows) & (key - cache_rows > feature)
        masks = jnp.where(late, MASKED, masks)
    return masks.astype(BF16), hidden


def row_features(rows, prompt_rows):
    feature = lax.broadcasted_iota(jnp.int32, (HD, rows), 0)
    row = lax.rem(lax.broadcasted_iota(jnp.int32, (HD, rows), 1), prompt_rows)
    return jnp.where((feature == row) | (feature == prompt_rows), 1.0, 0.0).astype(BF16)


def own_head(full, cont_rows):
    group = lax.broadcasted_iota(jnp.int32, (HD, KVH * cont_rows), 1) // cont_rows
    parts = [jnp.where(group == g, full[g * HD : (g + 1) * HD], 0.0) for g in range(KVH)]
    return jnp.concatenate([functools.reduce(jnp.add, parts), full[KVH * HD :]], axis=0)


def prep_kernel(
    length_hbm, query_ref, cont_ref, key_ref, value_ref,
    q_ref, cont_q_ref, cont_max_ref, cont_total_ref, length_ref, sem,
):
    load = pltpu.make_async_copy(length_hbm, length_ref, sem)
    load.start()
    prompt_rows = query_ref.shape[0]
    cont_count, suffix_rows = key_ref.shape[:2]
    cont_rows = cont_count * GROUP
    dot = functools.partial(jnp.dot, preferred_element_type=F32)
    cont = cont_ref[...].astype(F32)
    heads = [slice(head * HD, (head + 1) * HD) for head in range(KVH * GROUP)]
    cont_q = jnp.concatenate(
        [
            cont[c : c + 1, head]
            for g in range(KVH)
            for c in range(cont_count)
            for head in heads[g * GROUP : (g + 1) * GROUP]
        ],
        axis=0,
    ).T
    column = lax.broadcasted_iota(jnp.int32, cont_q.shape, 1) // cont_rows
    cont_q = jnp.concatenate([jnp.where(column == g, cont_q, 0.0) for g in range(KVH)], axis=0)
    cont_q = cont_q.astype(BF16)
    cont_q_ref[...] = cont_q
    scores = [dot(key_ref[c], cont_q) for c in range(cont_count)]
    for g in range(KVH):
        q = jnp.concatenate([query_ref[:, head] for head in heads[g * GROUP : (g + 1) * GROUP]], axis=0)
        q_ref[g * HD : (g + 1) * HD] = q.T
    q_ref[KVH * HD :] = row_features(GROUP * prompt_rows, prompt_rows)
    v = value_ref[...].reshape(cont_count * suffix_rows, KVH * HD).T
    v = jnp.concatenate([v, jnp.ones((ONES, v.shape[1]), BF16)], axis=0)
    load.wait()
    key = lax.broadcasted_iota(jnp.int32, scores[0].shape, 0)
    owner = lax.broadcasted_iota(jnp.int32, scores[0].shape, 1) % cont_rows // GROUP
    s = jnp.concatenate(
        [
            jnp.where((owner == c) & (key < length_ref[c]), scores[c], MASKED)
            for c in range(cont_count)
        ],
        axis=0,
    )
    new_max, p, _ = weigh(s, FLOOR)
    cont_max_ref[...] = new_max
    cont_total_ref[...] = own_head(dot(v, p), cont_rows)


def window_kernel(first_ref, last_ref, window_ref):
    window_ref[0:1] = jnp.full((1, HD), first_ref[0], jnp.int32)
    window_ref[1:2] = jnp.full((1, HD), last_ref[0], jnp.int32)


def weigh(scores, old_max):
    new_max = jnp.maximum(old_max, jnp.max(scores, axis=0, keepdims=True))
    p = jnp.exp2((scores - new_max) * SCALE).astype(BF16)
    return new_max, p, jnp.exp2((old_max - new_max) * SCALE)


def take_kernel(size, cache_rows, prompt_rows, cont_count, sources, kind, *refs):
    first, last = kind == "first", kind == "last"
    window_ref, q_ref, cont_q_ref = refs[:3]
    held, refs = (refs[3:5], refs[5:]) if first else (refs[3:7], refs[7:])
    blocks, outs = refs[: len(sources)], refs[len(sources) :]
    device = lax.axis_index("ctx")
    keys = cache_rows + prompt_rows
    cont_rows = cont_count * GROUP
    ones = jnp.ones((ONES, len(blocks) * keys), BF16)
    dot = functools.partial(jnp.dot, preferred_element_type=F32)
    if last:
        out_hbm, cont_hbm, out_ref, cont_ref, sems = outs

    window = (window_ref[0:1], window_ref[1:2])
    terms = [
        mask_columns(
            device, block_origin(device, *source, size), window, cache_rows, prompt_rows, source[0] == 0
        )
        for source in sources
    ]
    masks = jnp.concatenate([term[0] for term in terms], axis=0)
    hidden = jnp.concatenate([term[1][:, :1] for term in terms], axis=0)
    values = [
        jnp.concatenate([block[keys:, g * keys : (g + 1) * keys] for block in blocks], axis=1)
        for g in range(KVH)
    ]
    stores = []

    def cont_scores():
        cuts = [slice(at, at + 2 * HD) for at in range(0, KVH * HD, 2 * HD)]
        parts = [
            dot(jnp.concatenate([block[:keys, cut] for block in blocks], axis=0), cont_q_ref[cut])
            for cut in cuts
        ]
        return sum(parts) + hidden

    def finish_cont(s):
        new_max, p, old = weigh(s, held[0][...])
        total = own_head(dot(jnp.concatenate(values + [ones], axis=0), p), cont_rows)
        total = total + held[1][...] * old
        if not last:
            outs[0][...] = new_max
            outs[1][...] = total
            return
        result = (total[:HD] * (1.0 / total[HD : HD + 1])).T
        for row in range(KVH * cont_rows):
            g, c, h = row // cont_rows, row % cont_rows // GROUP, row % GROUP
            cols = slice((g * GROUP + h) * HD, (g * GROUP + h + 1) * HD)
            cont_ref[c : c + 1, cols] = result[row : row + 1].astype(BF16)
        stores.append(pltpu.make_async_copy(cont_ref, cont_hbm, sems.at[KVH]))
        stores[-1].start()

    def head_scores(g):
        cols = slice(g * HD, (g + 1) * HD)
        k = jnp.concatenate([block[:keys, cols] for block in blocks], axis=0)
        q = jnp.concatenate([q_ref[cols], q_ref[KVH * HD :]], axis=0)
        return dot(jnp.concatenate([k, masks], axis=1), q)

    def finish_head(g, s):
        new_max, p, old = weigh(s, FLOOR if first else held[2][g])
        total = dot(jnp.concatenate([values[g], ones], axis=0), p)
        if not first:
            total = total + held[3][g] * old
        if not last:
            outs[2][g] = new_max
            outs[3][g] = total
            return
        result = (total[:HD] * (1.0 / total[HD : HD + 1])).T.astype(BF16)
        for h in range(GROUP):
            cols = slice((g * GROUP + h) * HD, (g * GROUP + h + 1) * HD)
            out_ref[:, cols] = result[h * prompt_rows : (h + 1) * prompt_rows]
        cols = slice(g * GROUP * HD, (g + 1) * GROUP * HD)
        stores.append(
            pltpu.make_async_copy(out_ref.at[:, cols], out_hbm.at[:, cols], sems.at[g])
        )
        stores[-1].start()

    work = [(cont_scores, finish_cont)] + [
        (functools.partial(head_scores, g), functools.partial(finish_head, g)) for g in range(KVH)
    ]
    ready = [scores() for scores, _ in work[:AHEAD]]
    for index, (_, finish) in enumerate(work):
        if index + AHEAD < len(work):
            ready.append(work[index + AHEAD][0]())
        finish(ready[index])
    for store in stores:
        store.wait()


def in_hbm(array):
    return pltpu.with_memory_space_constraint(array, pltpu.HBM)


def cost(rows, keys):
    work = rows * keys
    return pl.CostEstimate(flops=8 * work * HD, transcendentals=work, bytes_accessed=1 << 20)


def body(
    size,
    cache_keys,
    cache_values,
    new_queries,
    new_keys,
    new_values,
    cont_queries,
    suffix_keys,
    suffix_values,
    window_start,
    prefix_length,
    suffix_length,
):
    cache_rows, prompt_rows, cont_count = (
        cache_keys.shape[0], new_keys.shape[0], cont_queries.shape[0],
    )
    keys = cache_rows + prompt_rows
    chips = size // 2
    ring = ring_pairs(size)
    pair = [(device, device ^ 1) for device in range(size)]
    params = pltpu.CompilerParams(vmem_limit_bytes=24 << 20)
    rows, cont_rows = GROUP * prompt_rows, KVH * GROUP * cont_count
    shape = jax.ShapeDtypeStruct

    def send(block, pairs):
        return lax.ppermute(block, "ctx", pairs)

    rest = (new_queries, cont_queries, suffix_keys, suffix_values)
    arrays = (cache_keys, new_keys, cache_values, new_values, *rest)
    own, *rest = pl.pallas_call(
        pack_kernel,
        out_shape=[shape((keys + HD, KVH * HD), BF16)] + [shape(x.shape, BF16) for x in rest],
        in_specs=[HBM] * 8,
        out_specs=[VMEM] * 5,
        scratch_shapes=[pltpu.VMEM((keys, KVH * HD), BF16), pltpu.SemaphoreType.DMA((8,))],
        compiler_params=params,
    )(*[in_hbm(x) for x in arrays])
    other = send(own, pair)
    waiting = [((0, False, False), own), ((0, False, True), other)]

    state_shape = [
        shape((1, cont_rows), F32),
        shape((HD + ONES, cont_rows), F32),
        shape((KVH, 1, rows), F32),
        shape((KVH, HD + ONES, rows), F32),
    ]
    queries, cont_q, *state = pl.pallas_call(
        prep_kernel,
        out_shape=[
            shape(((KVH + 1) * HD, rows), BF16),
            shape((KVH * HD, cont_rows), BF16),
        ] + state_shape[:2],
        in_specs=[HBM] + [VMEM] * 4,
        out_specs=[VMEM] * 4,
        scratch_shapes=[pltpu.SMEM(suffix_length.shape, jnp.int32), pltpu.SemaphoreType.DMA(())],
        compiler_params=params,
        cost_estimate=cost(rows, keys),
    )(in_hbm(suffix_length), *rest)

    window = pl.pallas_call(
        window_kernel,
        out_shape=shape((2, HD), jnp.int32),
        in_specs=[SMEM] * 2,
        out_specs=VMEM,
        compiler_params=params,
    )(window_start, prefix_length)

    def take(state, held, kind="middle"):
        sources, blocks = zip(*held)
        specs, scratch, outs = [VMEM] * 4, [], state_shape
        if kind == "last":
            outs = [shape(new_queries.shape, BF16), shape(cont_queries.shape, BF16)]
            specs = [HBM] * 2
            scratch = [
                pltpu.VMEM(new_queries.shape, BF16),
                pltpu.VMEM(cont_queries.shape, BF16),
                pltpu.SemaphoreType.DMA((KVH + 1,)),
            ]
        aliases = {} if kind == "last" else {3 + index: index for index in range(len(state))}
        return pl.pallas_call(
            functools.partial(
                take_kernel, size, cache_rows, prompt_rows, cont_count, sources, kind
            ),
            out_shape=outs,
            in_specs=[VMEM] * (3 + len(state) + len(blocks)),
            out_specs=specs,
            scratch_shapes=scratch,
            input_output_aliases=aliases,
            compiler_params=params,
            cost_estimate=cost(rows, len(blocks) * keys),
        )(window, queries, cont_q, *state, *blocks)

    hops = chips // 2
    for hop in range(1, hops):
        own, other = send(own, ring), send(other, ring)
        swap, swop = send(own, pair), send(other, pair)
        arrived = [((hop, False, False), own), ((hop, True, False), swap)]
        if hop == 1:
            state = take(state, waiting, "first")
            waiting = []
        else:
            state = take(state, waiting[:2])
            waiting = waiting[2:]
            if hop + 1 == hops:
                waiting, arrived = waiting + arrived, []
            state = take(state, waiting)
            waiting = []
        waiting += arrived + [((hop, False, True), other), ((hop, True, True), swop)]
    own = send(own, ring)
    swapped = send(own, pair)
    state = take(state, waiting + [((hops, False, False), own)])
    return tuple(take(state, [((hops, True, False), swapped)], "last"))


def solution(mesh):
    in_specs = (
        P(("grp", "ctx"), None),
        P(("grp", "ctx"), None),
        P(("grp", "ctx"), None),
        P(("grp", "ctx"), None),
        P(("grp", "ctx"), None),
        P(("grp", "ctx"), None),
        P(("grp", "ctx"), None, None),
        P(("grp", "ctx"), None, None),
        P("grp"),
        P("grp"),
        P(("grp", "ctx")),
    )
    out_specs = (P(("grp", "ctx"), None), P(("grp", "ctx"), None))
    size = mesh.shape["ctx"]

    def run(*arrays):
        return body(size, *arrays)

    return jax.shard_map(run, mesh=mesh, in_specs=in_specs, out_specs=out_specs, check_vma=False)
```

time: 43.3 us -> 40.8 us (0.942)
  Pallas kernels: 13.6 us -> 12 us
  other arithmetic: 0.73 us -> 0 us
    pallas_call x1, Pallas kernels: 1.78 us -> 0.96 us  [body(): pl.pallas_call(prep_kernel, out_shape=[shape(((KVH + 1) * HD, rows), BF16...]
    pallas_call x9, Pallas kernels: 11.8 us -> 11 us  [the longest x7 9.62 us: take(): pl.pallas_call(functools.partial(take_kernel, size, cache_rows, prompt_ro...]
    concatenate x1 -> x0, other arithmetic: 0.73 us -> none  [body(): limits = jnp.concatenate([window_start, prefix_length, suffix_length])]
  transfers between devices with their start and end apart: 15 -> 15, of which waited for: 7 -> 7; matrix products, arithmetic and copies ran while one was open for 2% -> 0% of each run, Pallas kernels for 24% -> 22%
where the time goes in v4:
time: 40.8 us; the launch traced here: 40.6 us
  starting transfers between devices  16.5 us (40%)
  Pallas kernels  12 us (29%)
  waiting for transfers between devices  10.1 us (25%)
  between operations  2.04 us (5%)
    ppermute x15, starting transfers between devices, send(): return lax.ppermute(block, 'ctx', pairs)  16.5 us
    ppermute x15, waiting for transfers between devices, send(): return lax.ppermute(block, 'ctx', pairs)  10.1 us
    pallas_call x7, Pallas kernels, take(): pl.pallas_call(functools.partial(take_kernel, size, cache_rows, prompt_ro...  9.62 us
    pallas_call x1, Pallas kernels, body(): pl.pallas_call(pack_kernel, out_shape=[shape((keys + HD, KVH * HD), BF16)...  1.42 us
    pallas_call x1, Pallas kernels, body(): pl.pallas_call(prep_kernel, out_shape=[shape(((KVH + 1) * HD, rows), BF16...  0.96 us
  transfers between devices with their start and end apart: 15, of which 7 were waited for; matrix products, arithmetic and copies ran while one was open for 0% of the time, Pallas kernels for 22%

profile of v4, /device:TPU:0, one launch (start us, length us, event | category | flops | bytes accessed | tf_op | source)
XLA Modules:
  0.0 40.6 jit_solution(15753883682828716622)
XLA Ops:
  0.6 1.4 %shard_map.123 = (bf16[256,512]{1,0:T(8,128)(2,1)S(1)}, bf16[64,4096]{1,0:T(8,128)(2,1)S(1)}, bf16[2,4096]{1,0:T(2,128)(2,1)S(1)}, bf16[2,128,512]{2,1,0:T(8,128)(2,1)S(1)}, bf16[2,128,512]{2,1,0:T(8,128)(2,1)S(1)}) custom-call(bf16[64,512]{1,0:T(8,128)(2,1)} %ck_hbm.1, bf16[64,512]{1,0:T(8,128)(2,1)} %nk_hbm.1, bf16[64,512]{1,0:T(8,128)(2,1)} %cv_hbm.1, ...), custom_call_target="tpu_custom_call" | custom-call | tf_op jit(solution)/shard_map/pallas_call | solution.py:298
  2.1 0.6 %collective-permute-start = (bf16[256,512]{1,0:T(8,128)(2,1)S(1)}, bf16[256,512]{1,0:T(8,128)(2,1)S(1)}, u32[]{:S(2)}, u32[]{:S(2)}) collective-permute-start(bf16[256,512]{1,0:T(8,128)(2,1)S(1)} %get-tuple-element.43.refs_5_), channel_id=1, source_target_pairs={{0,1},{1,0},{2,3},{3,2},{4,5},{5,4},{6,7},{7,6},{8,9},{9,8},{10,11... | collective-permute-start | bytes 786440 | tf_op jit(solution)/shard_map/ppermute | solution.py:294
  2.6 2.6 %collective-permute-start.1 = (bf16[256,512]{1,0:T(8,128)(2,1)S(1)}, bf16[256,512]{1,0:T(8,128)(2,1)S(1)}, u32[]{:S(2)}, u32[]{:S(2)}) collective-permute-start(bf16[256,512]{1,0:T(8,128)(2,1)S(1)} %get-tuple-element.43.refs_5_), channel_id=1, source_target_pairs={{0,4},{1,3},{2,0},{3,7},{4,8},{5,1},{6,2},{7,11},{8,12},{9,5},{10,... | collective-permute-start | bytes 786440 | tf_op jit(solution)/shard_map/ppermute | solution.py:294
  5.2 0.0 collective-permute-done.refs_6_
  5.2 1.6 %collective-permute-start.3 = (bf16[256,512]{1,0:T(8,128)(2,1)S(1)}, bf16[256,512]{1,0:T(8,128)(2,1)S(1)}, u32[]{:S(2)}, u32[]{:S(2)}) collective-permute-start(bf16[256,512]{1,0:T(8,128)(2,1)S(1)} %collective-permute-done.refs_6_), channel_id=1, source_target_pairs={{0,4},{1,3},{2,0},{3,7},{4,8},{5,1},{6,2},{7,11},{8,12},{9,5},{10,... | collective-permute-start | bytes 786440 | tf_op jit(solution)/shard_map/ppermute | solution.py:294
  6.8 2.7 %collective-permute-done.1.refs_7_ = bf16[256,512]{1,0:T(8,128)(2,1)S(1)} collective-permute-done((bf16[256,512]{1,0:T(8,128)(2,1)S(1)}, bf16[256,512]{1,0:T(8,128)(2,1)S(1)}, u32[]{:S(2)}, u32[]{:S(2)}) %collective-permute-start.1) | collective-permute-done | bytes 262176 | tf_op jit(solution)/shard_map/ppermute | solution.py:294
  9.5 2.1 %collective-permute-start.5 = (bf16[256,512]{1,0:T(8,128)(2,1)S(1)}, bf16[256,512]{1,0:T(8,128)(2,1)S(1)}, u32[]{:S(2)}, u32[]{:S(2)}) collective-permute-start(bf16[256,512]{1,0:T(8,128)(2,1)S(1)} %collective-permute-done.1.refs_7_), channel_id=1, source_target_pairs={{0,4},{1,3},{2,0},{3,7},{4,8},{5,1},{6,2},{7,11},{8,12},{9,5},{10,... | collective-permute-start | bytes 786440 | tf_op jit(solution)/shard_map/ppermute | solution.py:294
  11.6 0.7 %collective-permute-done.3.refs_7_ = bf16[256,512]{1,0:T(8,128)(2,1)S(1)} collective-permute-done((bf16[256,512]{1,0:T(8,128)(2,1)S(1)}, bf16[256,512]{1,0:T(8,128)(2,1)S(1)}, u32[]{:S(2)}, u32[]{:S(2)}) %collective-permute-start.3) | collective-permute-done | bytes 262176 | tf_op jit(solution)/shard_map/ppermute | solution.py:294
  12.3 2.1 %collective-permute-start.7 = (bf16[256,512]{1,0:T(8,128)(2,1)S(1)}, bf16[256,512]{1,0:T(8,128)(2,1)S(1)}, u32[]{:S(2)}, u32[]{:S(2)}) collective-permute-start(bf16[256,512]{1,0:T(8,128)(2,1)S(1)} %collective-permute-done.3.refs_7_), channel_id=1, source_target_pairs={{0,4},{1,3},{2,0},{3,7},{4,8},{5,1},{6,2},{7,11},{8,12},{9,5},{10,... | collective-permute-start | bytes 786440 | tf_op jit(solution)/shard_map/ppermute | solution.py:294
  14.4 1.5 %collective-permute-done.5.refs_7_ = bf16[256,512]{1,0:T(8,128)(2,1)S(1)} collective-permute-done((bf16[256,512]{1,0:T(8,128)(2,1)S(1)}, bf16[256,512]{1,0:T(8,128)(2,1)S(1)}, u32[]{:S(2)}, u32[]{:S(2)}) %collective-permute-start.5) | collective-permute-done | bytes 262176 | tf_op jit(solution)/shard_map/ppermute | solution.py:294
  15.9 2.1 %collective-permute-start.9 = (bf16[256,512]{1,0:T(8,128)(2,1)S(1)}, bf16[256,512]{1,0:T(8,128)(2,1)S(1)}, u32[]{:S(2)}, u32[]{:S(2)}) collective-permute-start(bf16[256,512]{1,0:T(8,128)(2,1)S(1)} %collective-permute-done.5.refs_7_), channel_id=1, source_target_pairs={{0,4},{1,3},{2,0},{3,7},{4,8},{5,1},{6,2},{7,11},{8,12},{9,5},{10,... | collective-permute-start | bytes 786440 | tf_op jit(solution)/shard_map/ppermute | solution.py:294
  18.0 0.0 collective-permute-start.2
  18.0 0.5 %collective-permute-start.4 = (bf16[256,512]{1,0:T(8,128)(2,1)S(1)}, bf16[256,512]{1,0:T(8,128)(2,1)S(1)}, u32[]{:S(2)}, u32[]{:S(2)}) collective-permute-start(bf16[256,512]{1,0:T(8,128)(2,1)S(1)} %collective-permute-done.3.refs_7_), channel_id=1, source_target_pairs={{0,1},{1,0},{2,3},{3,2},{4,5},{5,4},{6,7},{7,6},{8,9},{9,8},{10,11... | collective-permute-start | bytes 786440 | tf_op jit(solution)/shard_map/ppermute | solution.py:294
  18.5 0.2 collective-permute-done.7.refs_7_
  18.7 2.1 %collective-permute-start.11 = (bf16[256,512]{1,0:T(8,128)(2,1)S(1)}, bf16[256,512]{1,0:T(8,128)(2,1)S(1)}, u32[]{:S(2)}, u32[]{:S(2)}) collective-permute-start(bf16[256,512]{1,0:T(8,128)(2,1)S(1)} %collective-permute-done.7.refs_7_), channel_id=1, source_target_pairs={{0,4},{1,3},{2,0},{3,7},{4,8},{5,1},{6,2},{7,11},{8,12},{9,5},{10,... | collective-permute-start | bytes 786440 | tf_op jit(solution)/shard_map/ppermute | solution.py:294
  20.8 1.5 %collective-permute-done.9.refs_9_ = bf16[256,512]{1,0:T(8,128)(2,1)S(1)} collective-permute-done((bf16[256,512]{1,0:T(8,128)(2,1)S(1)}, bf16[256,512]{1,0:T(8,128)(2,1)S(1)}, u32[]{:S(2)}, u32[]{:S(2)}) %collective-permute-start.9) | collective-permute-done | bytes 262176 | tf_op jit(solution)/shard_map/ppermute | solution.py:294
  22.3 2.1 %collective-permute-start.13 = (bf16[256,512]{1,0:T(8,128)(2,1)S(1)}, bf16[256,512]{1,0:T(8,128)(2,1)S(1)}, u32[]{:S(2)}, u32[]{:S(2)}) collective-permute-start(bf16[256,512]{1,0:T(8,128)(2,1)S(1)} %collective-permute-done.9.refs_9_), channel_id=1, source_target_pairs={{0,4},{1,3},{2,0},{3,7},{4,8},{5,1},{6,2},{7,11},{8,12},{9,5},{10,... | collective-permute-start | bytes 786440 | tf_op jit(solution)/shard_map/ppermute | solution.py:294
  24.4 0.0 collective-permute-start.6
  24.4 0.0 collective-permute-done.2.refs_8_
  24.4 0.5 %collective-permute-start.10 = (bf16[256,512]{1,0:T(8,128)(2,1)S(1)}, bf16[256,512]{1,0:T(8,128)(2,1)S(1)}, u32[]{:S(2)}, u32[]{:S(2)}) collective-permute-start(bf16[256,512]{1,0:T(8,128)(2,1)S(1)} %collective-permute-done.9.refs_9_), channel_id=1, source_target_pairs={{0,1},{1,0},{2,3},{3,2},{4,5},{5,4},{6,7},{7,6},{8,9},{9,8},{10,11... | collective-permute-start | bytes 786440 | tf_op jit(solution)/shard_map/ppermute | solution.py:294
  24.9 0.0 collective-permute-done.4.refs_8_
  24.9 0.1 collective-permute-start.8
  24.9 0.1 collective-permute-done.11.refs_7_
  25.1 0.3 collective-permute-start.12
  25.4 3.3 %collective-permute-done.13.refs_9_ = bf16[256,512]{1,0:T(8,128)(2,1)S(1)} collective-permute-done((bf16[256,512]{1,0:T(8,128)(2,1)S(1)}, bf16[256,512]{1,0:T(8,128)(2,1)S(1)}, u32[]{:S(2)}, u32[]{:S(2)}) %collective-permute-start.13) | collective-permute-done | bytes 262176 | tf_op jit(solution)/shard_map/ppermute | solution.py:294
  28.7 0.0 collective-permute-start.14
  30.0 1.0 %shard_map.124 = (bf16[640,512]{1,0:T(8,128)(2,1)S(1)}, bf16[512,64]{1,0:T(8,128)(2,1)S(1)}, f32[1,64]{1,0:T(1,128)S(1)}, f32[144,64]{1,0:T(8,128)S(1)}) custom-call(s32[2]{0:T(128)} %length_hbm.1, bf16[64,4096]{1,0:T(8,128)(2,1)S(1)} %get-tuple-element.35.query_ref, bf16[2,4096]{1,0:T(2,128)(2,1)S(1)} %get-tuple-element.36.cont_ref, ...), custom_call_target="tpu_custom_call" | custom-call | flops 67108864 | bytes 1048576 | tf_op jit(solution)/shard_map/pallas_call | solution.py:315
  30.9 1.0 %shard_map.125 = (f32[1,64]{1,0:T(1,128)S(1)}, f32[144,64]{1,0:T(8,128)S(1)}, f32[4,1,512]{2,1,0:T(1,128)S(1)}, f32[4,144,512]{2,1,0:T(8,128)S(1)}) custom-call(s32[2,128]{1,0:T(2,128)S(1)} %shard_map.122.refs_0_, bf16[640,512]{1,0:T(8,128)(2,1)S(1)} %get-tuple-element.39.refs_1_, ...), custom_call_target="tpu_custom_call", output_to_operand_aliasing={{0}: (3, {}), {1}: (4, {})} | custom-call | flops 134217728 | bytes 1048576 | tf_op jit(solution)/shard_map/pallas_call | solution.py:348
  32.0 1.2 %shard_map.126 = (f32[1,64]{1,0:T(1,128)S(1)}, f32[144,64]{1,0:T(8,128)S(1)}, f32[4,1,512]{2,1,0:T(1,128)S(1)}, f32[4,144,512]{2,1,0:T(8,128)S(1)}) custom-call(s32[2,128]{1,0:T(2,128)S(1)} %shard_map.122.refs_0_, bf16[640,512]{1,0:T(8,128)(2,1)S(1)} %get-tuple-element.39.refs_1_, ...), custom_call_target="tpu_custom_call", output_to_operand_aliasing={{0}: (3, {}), {1}: (4, {}), {2}: (5, {}), {3}: (6, {})} | custom-call | flops 134217728 | bytes 1048576 | tf_op jit(solution)/shard_map/pallas_call | solution.py:348
  33.1 1.2 %shard_map.127 = (f32[1,64]{1,0:T(1,128)S(1)}, f32[144,64]{1,0:T(8,128)S(1)}, f32[4,1,512]{2,1,0:T(1,128)S(1)}, f32[4,144,512]{2,1,0:T(8,128)S(1)}) custom-call(s32[2,128]{1,0:T(2,128)S(1)} %shard_map.122.refs_0_, bf16[640,512]{1,0:T(8,128)(2,1)S(1)} %get-tuple-element.39.refs_1_, ...), custom_call_target="tpu_custom_call", output_to_operand_aliasing={{0}: (3, {}), {1}: (4, {}), {2}: (5, {}), {3}: (6, {})} | custom-call | flops 134217728 | bytes 1048576 | tf_op jit(solution)/shard_map/pallas_call | solution.py:348
  34.3 0.0 collective-permute-done.6.refs_8_
  34.3 1.2 %shard_map.128 = (f32[1,64]{1,0:T(1,128)S(1)}, f32[144,64]{1,0:T(8,128)S(1)}, f32[4,1,512]{2,1,0:T(1,128)S(1)}, f32[4,144,512]{2,1,0:T(8,128)S(1)}) custom-call(s32[2,128]{1,0:T(2,128)S(1)} %shard_map.122.refs_0_, bf16[640,512]{1,0:T(8,128)(2,1)S(1)} %get-tuple-element.39.refs_1_, ...), custom_call_target="tpu_custom_call", output_to_operand_aliasing={{0}: (3, {}), {1}: (4, {}), {2}: (5, {}), {3}: (6, {})} | custom-call | flops 134217728 | bytes 1048576 | tf_op jit(solution)/shard_map/pallas_call | solution.py:348
  35.5 0.0 collective-permute-done.10.refs_10_
  35.5 0.0 collective-permute-done.8.refs_8_
  35.5 1.9 %shard_map.129 = (f32[1,64]{1,0:T(1,128)S(1)}, f32[144,64]{1,0:T(8,128)S(1)}, f32[4,1,512]{2,1,0:T(1,128)S(1)}, f32[4,144,512]{2,1,0:T(8,128)S(1)}) custom-call(s32[2,128]{1,0:T(2,128)S(1)} %shard_map.122.refs_0_, bf16[640,512]{1,0:T(8,128)(2,1)S(1)} %get-tuple-element.39.refs_1_, ...), custom_call_target="tpu_custom_call", output_to_operand_aliasing={{0}: (3, {}), {1}: (4, {}), {2}: (5, {}), {3}: (6, {})} | custom-call | flops 268435456 | bytes 1048576 | tf_op jit(solution)/shard_map/pallas_call | solution.py:348
  37.4 0.0 collective-permute-done.12.refs_8_
  37.4 1.7 %shard_map.130 = (f32[1,64]{1,0:T(1,128)S(1)}, f32[144,64]{1,0:T(8,128)S(1)}, f32[4,1,512]{2,1,0:T(1,128)S(1)}, f32[4,144,512]{2,1,0:T(8,128)S(1)}) custom-call(s32[2,128]{1,0:T(2,128)S(1)} %shard_map.122.refs_0_, bf16[640,512]{1,0:T(8,128)(2,1)S(1)} %get-tuple-element.39.refs_1_, ...), custom_call_target="tpu_custom_call", output_to_operand_aliasing={{0}: (3, {}), {1}: (4, {}), {2}: (5, {}), {3}: (6, {})} | custom-call | flops 201326592 | bytes 1048576 | tf_op jit(solution)/shard_map/pallas_call | solution.py:348
  39.1 0.0 collective-permute-done.14.refs_7_
  39.1 1.5 %shard_map.131 = (bf16[64,4096]{1,0:T(8,128)(2,1)}, bf16[2,4096]{1,0:T(2,128)(2,1)}) custom-call(s32[2,128]{1,0:T(2,128)S(1)} %shard_map.122.refs_0_, bf16[640,512]{1,0:T(8,128)(2,1)S(1)} %get-tuple-element.39.refs_1_, bf16[512,64]{1,0:T(8,128)(2,1)S(1)} %get-tuple-element.40.refs_2_, f32[1,64]{1,0:T(1,128)S(1)} %get-tuple-element.64.refs_3_, ...), custom_call_target="tpu_custom_call" | custom-call | flops 67108864 | bytes 1048576 | tf_op jit(solution)/shard_map/pallas_call | solution.py:348
  (1 shorter events, 0.0 us)
Async XLA Ops:
  2.1 3.2 %collective-permute-start = (bf16[256,512]{1,0:T(8,128)(2,1)S(1)}, bf16[256,512]{1,0:T(8,128)(2,1)S(1)}, u32[]{:S(2)}, u32[]{:S(2)}) collective-permute-start(bf16[256,512]{1,0:T(8,128)(2,1)S(1)} %get-tuple-element.43.refs_5_), channel_id=1, source_target_pairs={{0,1},{1,0},{2,3},{3,2},{4,5},{5,4},{6,7},{7,6},{8,9},{9,8},{10,11... | collective-permute-start | bytes 786440 | tf_op jit(solution)/shard_map/ppermute | solution.py:294
  2.6 6.9 %collective-permute-start.1 = (bf16[256,512]{1,0:T(8,128)(2,1)S(1)}, bf16[256,512]{1,0:T(8,128)(2,1)S(1)}, u32[]{:S(2)}, u32[]{:S(2)}) collective-permute-start(bf16[256,512]{1,0:T(8,128)(2,1)S(1)} %get-tuple-element.43.refs_5_), channel_id=1, source_target_pairs={{0,4},{1,3},{2,0},{3,7},{4,8},{5,1},{6,2},{7,11},{8,12},{9,5},{10,... | collective-permute-start | bytes 786440 | tf_op jit(solution)/shard_map/ppermute | solution.py:294
  5.2 7.1 %collective-permute-start.3 = (bf16[256,512]{1,0:T(8,128)(2,1)S(1)}, bf16[256,512]{1,0:T(8,128)(2,1)S(1)}, u32[]{:S(2)}, u32[]{:S(2)}) collective-permute-start(bf16[256,512]{1,0:T(8,128)(2,1)S(1)} %collective-permute-done.refs_6_), channel_id=1, source_target_pairs={{0,4},{1,3},{2,0},{3,7},{4,8},{5,1},{6,2},{7,11},{8,12},{9,5},{10,... | collective-permute-start | bytes 786440 | tf_op jit(solution)/shard_map/ppermute | solution.py:294
  9.5 6.4 %collective-permute-start.5 = (bf16[256,512]{1,0:T(8,128)(2,1)S(1)}, bf16[256,512]{1,0:T(8,128)(2,1)S(1)}, u32[]{:S(2)}, u32[]{:S(2)}) collective-permute-start(bf16[256,512]{1,0:T(8,128)(2,1)S(1)} %collective-permute-done.1.refs_7_), channel_id=1, source_target_pairs={{0,4},{1,3},{2,0},{3,7},{4,8},{5,1},{6,2},{7,11},{8,12},{9,5},{10,... | collective-permute-start | bytes 786440 | tf_op jit(solution)/shard_map/ppermute | solution.py:294
  12.3 6.4 %collective-permute-start.7 = (bf16[256,512]{1,0:T(8,128)(2,1)S(1)}, bf16[256,512]{1,0:T(8,128)(2,1)S(1)}, u32[]{:S(2)}, u32[]{:S(2)}) collective-permute-start(bf16[256,512]{1,0:T(8,128)(2,1)S(1)} %collective-permute-done.3.refs_7_), channel_id=1, source_target_pairs={{0,4},{1,3},{2,0},{3,7},{4,8},{5,1},{6,2},{7,11},{8,12},{9,5},{10,... | collective-permute-start | bytes 786440 | tf_op jit(solution)/shard_map/ppermute | solution.py:294
  15.9 6.4 %collective-permute-start.9 = (bf16[256,512]{1,0:T(8,128)(2,1)S(1)}, bf16[256,512]{1,0:T(8,128)(2,1)S(1)}, u32[]{:S(2)}, u32[]{:S(2)}) collective-permute-start(bf16[256,512]{1,0:T(8,128)(2,1)S(1)} %collective-permute-done.5.refs_7_), channel_id=1, source_target_pairs={{0,4},{1,3},{2,0},{3,7},{4,8},{5,1},{6,2},{7,11},{8,12},{9,5},{10,... | collective-permute-start | bytes 786440 | tf_op jit(solution)/shard_map/ppermute | solution.py:294
  18.0 6.4 %collective-permute-start.2 = (bf16[256,512]{1,0:T(8,128)(2,1)S(1)}, bf16[256,512]{1,0:T(8,128)(2,1)S(1)}, u32[]{:S(2)}, u32[]{:S(2)}) collective-permute-start(bf16[256,512]{1,0:T(8,128)(2,1)S(1)} %collective-permute-done.1.refs_7_), channel_id=1, source_target_pairs={{0,1},{1,0},{2,3},{3,2},{4,5},{5,4},{6,7},{7,6},{8,9},{9,8},{10,11... | collective-permute-start | bytes 786440 | tf_op jit(solution)/shard_map/ppermute | solution.py:294
  18.0 6.9 %collective-permute-start.4 = (bf16[256,512]{1,0:T(8,128)(2,1)S(1)}, bf16[256,512]{1,0:T(8,128)(2,1)S(1)}, u32[]{:S(2)}, u32[]{:S(2)}) collective-permute-start(bf16[256,512]{1,0:T(8,128)(2,1)S(1)} %collective-permute-done.3.refs_7_), channel_id=1, source_target_pairs={{0,1},{1,0},{2,3},{3,2},{4,5},{5,4},{6,7},{7,6},{8,9},{9,8},{10,11... | collective-permute-start | bytes 786440 | tf_op jit(solution)/shard_map/ppermute | solution.py:294
  18.7 6.4 %collective-permute-start.11 = (bf16[256,512]{1,0:T(8,128)(2,1)S(1)}, bf16[256,512]{1,0:T(8,128)(2,1)S(1)}, u32[]{:S(2)}, u32[]{:S(2)}) collective-permute-start(bf16[256,512]{1,0:T(8,128)(2,1)S(1)} %collective-permute-done.7.refs_7_), channel_id=1, source_target_pairs={{0,4},{1,3},{2,0},{3,7},{4,8},{5,1},{6,2},{7,11},{8,12},{9,5},{10,... | collective-permute-start | bytes 786440 | tf_op jit(solution)/shard_map/ppermute | solution.py:294
  22.3 6.4 %collective-permute-start.13 = (bf16[256,512]{1,0:T(8,128)(2,1)S(1)}, bf16[256,512]{1,0:T(8,128)(2,1)S(1)}, u32[]{:S(2)}, u32[]{:S(2)}) collective-permute-start(bf16[256,512]{1,0:T(8,128)(2,1)S(1)} %collective-permute-done.9.refs_9_), channel_id=1, source_target_pairs={{0,4},{1,3},{2,0},{3,7},{4,8},{5,1},{6,2},{7,11},{8,12},{9,5},{10,... | collective-permute-start | bytes 786440 | tf_op jit(solution)/shard_map/ppermute | solution.py:294
  24.4 9.9 %collective-permute-start.6 = (bf16[256,512]{1,0:T(8,128)(2,1)S(1)}, bf16[256,512]{1,0:T(8,128)(2,1)S(1)}, u32[]{:S(2)}, u32[]{:S(2)}) collective-permute-start(bf16[256,512]{1,0:T(8,128)(2,1)S(1)} %collective-permute-done.5.refs_7_), channel_id=1, source_target_pairs={{0,1},{1,0},{2,3},{3,2},{4,5},{5,4},{6,7},{7,6},{8,9},{9,8},{10,11... | collective-permute-start | bytes 786440 | tf_op jit(solution)/shard_map/ppermute | solution.py:294
  24.4 11.1 %collective-permute-start.10 = (bf16[256,512]{1,0:T(8,128)(2,1)S(1)}, bf16[256,512]{1,0:T(8,128)(2,1)S(1)}, u32[]{:S(2)}, u32[]{:S(2)}) collective-permute-start(bf16[256,512]{1,0:T(8,128)(2,1)S(1)} %collective-permute-done.9.refs_9_), channel_id=1, source_target_pairs={{0,1},{1,0},{2,3},{3,2},{4,5},{5,4},{6,7},{7,6},{8,9},{9,8},{10,11... | collective-permute-start | bytes 786440 | tf_op jit(solution)/shard_map/ppermute | solution.py:294
  24.9 10.6 %collective-permute-start.8 = (bf16[256,512]{1,0:T(8,128)(2,1)S(1)}, bf16[256,512]{1,0:T(8,128)(2,1)S(1)}, u32[]{:S(2)}, u32[]{:S(2)}) collective-permute-start(bf16[256,512]{1,0:T(8,128)(2,1)S(1)} %collective-permute-done.7.refs_7_), channel_id=1, source_target_pairs={{0,1},{1,0},{2,3},{3,2},{4,5},{5,4},{6,7},{7,6},{8,9},{9,8},{10,11... | collective-permute-start | bytes 786440 | tf_op jit(solution)/shard_map/ppermute | solution.py:294
  25.1 12.3 %collective-permute-start.12 = (bf16[256,512]{1,0:T(8,128)(2,1)S(1)}, bf16[256,512]{1,0:T(8,128)(2,1)S(1)}, u32[]{:S(2)}, u32[]{:S(2)}) collective-permute-start(bf16[256,512]{1,0:T(8,128)(2,1)S(1)} %collective-permute-done.11.refs_7_), channel_id=1, source_target_pairs={{0,1},{1,0},{2,3},{3,2},{4,5},{5,4},{6,7},{7,6},{8,9},{9,8},{10,11... | collective-permute-start | bytes 786440 | tf_op jit(solution)/shard_map/ppermute | solution.py:294
  28.7 10.5 %collective-permute-start.14 = (bf16[256,512]{1,0:T(8,128)(2,1)S(1)}, bf16[256,512]{1,0:T(8,128)(2,1)S(1)}, u32[]{:S(2)}, u32[]{:S(2)}) collective-permute-start(bf16[256,512]{1,0:T(8,128)(2,1)S(1)} %collective-permute-done.13.refs_9_), channel_id=1, source_target_pairs={{0,1},{1,0},{2,3},{3,2},{4,5},{5,4},{6,7},{7,6},{8,9},{9,8},{10,11... | collective-permute-start | bytes 786440 | tf_op jit(solution)/shard_map/ppermute | solution.py:294

commit v5 on v4

--- a/solution.py
+++ b/solution.py
@@ -35,22 +35,25 @@
 def ring_pairs(size):
     chips = size // 2
     order = list(range(0, chips, 2)) + list(range(chips - 1, 0, -2))
-    place = {chip: index for index, chip in enumerate(order)}
     pairs = []
-    for device in range(size):
-        chip, core = divmod(device, 2)
-        step = 1 if core == 0 else -1
-        pairs.append((device, 2 * order[(place[chip] + step) % chips] + core))
-    return pairs
+    for place, chip in enumerate(order):
+        for way, step in enumerate((1, -1)):
+            core = (place + way) % 2
+            pairs.append((2 * chip + core, 2 * order[(place + step) % chips] + 1 - core))
+    return sorted(pairs)
 
 
 def block_origin(device, hop, swapped, partner, size):
     chips = size // 2
     chip, core = device // 2, device % 2
-    via = 1 - core if swapped else core
-    held = 1 - via if partner else via
-    place = ring_place(chip, chips) + jnp.where(via == 0, -hop, hop)
-    place = lax.rem(place + 2 * chips, chips)
+    place = ring_place(chip, chips)
+    way = (core + place) % 2
+    if swapped:
+        way = 1 - way
+    place = lax.rem(place + jnp.where(way == 0, -hop, hop) + 2 * chips, chips)
+    held = (way + place) % 2
+    if partner:
+        held = 1 - held
     return 2 * ring_chip(place, chips) + held
 
 

time: 40.8 us -> 39.9 us (0.978)
  waiting for transfers between devices: 10.1 us -> 9.15 us
    ppermute x15, waiting for transfers between devices: 10.1 us -> 9.15 us  [send(): return lax.ppermute(block, 'ctx', pairs)]
  transfers between devices with their start and end apart: 15 -> 15, of which waited for: 7 -> 7; matrix products, arithmetic and copies ran while one was open for 0% -> 0% of each run, Pallas kernels for 22% -> 23%
where the time goes in v5:
time: 39.9 us; the launch traced here: 39.7 us
  starting transfers between devices  16.5 us (41%)
  Pallas kernels  12 us (30%)
  waiting for transfers between devices  9.15 us (23%)
  between operations  2.04 us (5%)
    ppermute x15, starting transfers between devices, send(): return lax.ppermute(block, 'ctx', pairs)  16.5 us
    pallas_call x7, Pallas kernels, take(): pl.pallas_call(functools.partial(take_kernel, size, cache_rows, prompt_ro...  9.66 us
    ppermute x15, waiting for transfers between devices, send(): return lax.ppermute(block, 'ctx', pairs)  9.15 us
    pallas_call x1, Pallas kernels, body(): pl.pallas_call(pack_kernel, out_shape=[shape((keys + HD, KVH * HD), BF16)...  1.42 us
    pallas_call x1, Pallas kernels, body(): pl.pallas_call(prep_kernel, out_shape=[shape(((KVH + 1) * HD, rows), BF16...  0.95 us
  transfers between devices with their start and end apart: 15, of which 7 were waited for; matrix products, arithmetic and copies ran while one was open for 0% of the time, Pallas kernels for 23%

profile of v5, /device:TPU:0, one launch (start us, length us, event | category | flops | bytes accessed | tf_op | source)
XLA Modules:
  0.0 39.7 jit_solution(5720185959251668507)
XLA Ops:
  0.6 1.4 %shard_map.123 = (bf16[256,512]{1,0:T(8,128)(2,1)S(1)}, bf16[64,4096]{1,0:T(8,128)(2,1)S(1)}, bf16[2,4096]{1,0:T(2,128)(2,1)S(1)}, bf16[2,128,512]{2,1,0:T(8,128)(2,1)S(1)}, bf16[2,128,512]{2,1,0:T(8,128)(2,1)S(1)}) custom-call(bf16[64,512]{1,0:T(8,128)(2,1)} %ck_hbm.1, bf16[64,512]{1,0:T(8,128)(2,1)} %nk_hbm.1, bf16[64,512]{1,0:T(8,128)(2,1)} %cv_hbm.1, ...), custom_call_target="tpu_custom_call" | custom-call | tf_op jit(solution)/shard_map/pallas_call | solution.py:301
  2.1 0.6 %collective-permute-start = (bf16[256,512]{1,0:T(8,128)(2,1)S(1)}, bf16[256,512]{1,0:T(8,128)(2,1)S(1)}, u32[]{:S(2)}, u32[]{:S(2)}) collective-permute-start(bf16[256,512]{1,0:T(8,128)(2,1)S(1)} %get-tuple-element.43.refs_5_), channel_id=1, source_target_pairs={{0,1},{1,0},{2,3},{3,2},{4,5},{5,4},{6,7},{7,6},{8,9},{9,8},{10,11... | collective-permute-start | bytes 786440 | tf_op jit(solution)/shard_map/ppermute | solution.py:297
  2.6 2.7 %collective-permute-start.1 = (bf16[256,512]{1,0:T(8,128)(2,1)S(1)}, bf16[256,512]{1,0:T(8,128)(2,1)S(1)}, u32[]{:S(2)}, u32[]{:S(2)}) collective-permute-start(bf16[256,512]{1,0:T(8,128)(2,1)S(1)} %get-tuple-element.43.refs_5_), channel_id=1, source_target_pairs={{0,5},{1,2},{2,7},{3,0},{4,1},{5,8},{6,3},{7,10},{8,13},{9,4},{10,... | collective-permute-start | bytes 786440 | tf_op jit(solution)/shard_map/ppermute | solution.py:297
  5.3 0.0 collective-permute-done.refs_6_
  5.3 1.2 %collective-permute-start.3 = (bf16[256,512]{1,0:T(8,128)(2,1)S(1)}, bf16[256,512]{1,0:T(8,128)(2,1)S(1)}, u32[]{:S(2)}, u32[]{:S(2)}) collective-permute-start(bf16[256,512]{1,0:T(8,128)(2,1)S(1)} %collective-permute-done.refs_6_), channel_id=1, source_target_pairs={{0,5},{1,2},{2,7},{3,0},{4,1},{5,8},{6,3},{7,10},{8,13},{9,4},{10,... | collective-permute-start | bytes 786440 | tf_op jit(solution)/shard_map/ppermute | solution.py:297
  6.5 2.7 %collective-permute-done.1.refs_7_ = bf16[256,512]{1,0:T(8,128)(2,1)S(1)} collective-permute-done((bf16[256,512]{1,0:T(8,128)(2,1)S(1)}, bf16[256,512]{1,0:T(8,128)(2,1)S(1)}, u32[]{:S(2)}, u32[]{:S(2)}) %collective-permute-start.1) | collective-permute-done | bytes 262176 | tf_op jit(solution)/shard_map/ppermute | solution.py:297
  9.3 2.1 %collective-permute-start.5 = (bf16[256,512]{1,0:T(8,128)(2,1)S(1)}, bf16[256,512]{1,0:T(8,128)(2,1)S(1)}, u32[]{:S(2)}, u32[]{:S(2)}) collective-permute-start(bf16[256,512]{1,0:T(8,128)(2,1)S(1)} %collective-permute-done.1.refs_7_), channel_id=1, source_target_pairs={{0,5},{1,2},{2,7},{3,0},{4,1},{5,8},{6,3},{7,10},{8,13},{9,4},{10,... | collective-permute-start | bytes 786440 | tf_op jit(solution)/shard_map/ppermute | solution.py:297
  11.4 0.7 %collective-permute-done.3.refs_7_ = bf16[256,512]{1,0:T(8,128)(2,1)S(1)} collective-permute-done((bf16[256,512]{1,0:T(8,128)(2,1)S(1)}, bf16[256,512]{1,0:T(8,128)(2,1)S(1)}, u32[]{:S(2)}, u32[]{:S(2)}) %collective-permute-start.3) | collective-permute-done | bytes 262176 | tf_op jit(solution)/shard_map/ppermute | solution.py:297
  12.1 2.1 %collective-permute-start.7 = (bf16[256,512]{1,0:T(8,128)(2,1)S(1)}, bf16[256,512]{1,0:T(8,128)(2,1)S(1)}, u32[]{:S(2)}, u32[]{:S(2)}) collective-permute-start(bf16[256,512]{1,0:T(8,128)(2,1)S(1)} %collective-permute-done.3.refs_7_), channel_id=1, source_target_pairs={{0,5},{1,2},{2,7},{3,0},{4,1},{5,8},{6,3},{7,10},{8,13},{9,4},{10,... | collective-permute-start | bytes 786440 | tf_op jit(solution)/shard_map/ppermute | solution.py:297
  14.2 1.2 %collective-permute-done.5.refs_7_ = bf16[256,512]{1,0:T(8,128)(2,1)S(1)} collective-permute-done((bf16[256,512]{1,0:T(8,128)(2,1)S(1)}, bf16[256,512]{1,0:T(8,128)(2,1)S(1)}, u32[]{:S(2)}, u32[]{:S(2)}) %collective-permute-start.5) | collective-permute-done | bytes 262176 | tf_op jit(solution)/shard_map/ppermute | solution.py:297
  15.4 2.1 %collective-permute-start.9 = (bf16[256,512]{1,0:T(8,128)(2,1)S(1)}, bf16[256,512]{1,0:T(8,128)(2,1)S(1)}, u32[]{:S(2)}, u32[]{:S(2)}) collective-permute-start(bf16[256,512]{1,0:T(8,128)(2,1)S(1)} %collective-permute-done.5.refs_7_), channel_id=1, source_target_pairs={{0,5},{1,2},{2,7},{3,0},{4,1},{5,8},{6,3},{7,10},{8,13},{9,4},{10,... | collective-permute-start | bytes 786440 | tf_op jit(solution)/shard_map/ppermute | solution.py:297
  17.5 0.0 collective-permute-start.2
  17.5 0.5 %collective-permute-start.4 = (bf16[256,512]{1,0:T(8,128)(2,1)S(1)}, bf16[256,512]{1,0:T(8,128)(2,1)S(1)}, u32[]{:S(2)}, u32[]{:S(2)}) collective-permute-start(bf16[256,512]{1,0:T(8,128)(2,1)S(1)} %collective-permute-done.3.refs_7_), channel_id=1, source_target_pairs={{0,1},{1,0},{2,3},{3,2},{4,5},{5,4},{6,7},{7,6},{8,9},{9,8},{10,11... | collective-permute-start | bytes 786440 | tf_op jit(solution)/shard_map/ppermute | solution.py:297
  18.0 0.2 collective-permute-done.7.refs_7_
  18.2 2.1 %collective-permute-start.11 = (bf16[256,512]{1,0:T(8,128)(2,1)S(1)}, bf16[256,512]{1,0:T(8,128)(2,1)S(1)}, u32[]{:S(2)}, u32[]{:S(2)}) collective-permute-start(bf16[256,512]{1,0:T(8,128)(2,1)S(1)} %collective-permute-done.7.refs_7_), channel_id=1, source_target_pairs={{0,5},{1,2},{2,7},{3,0},{4,1},{5,8},{6,3},{7,10},{8,13},{9,4},{10,... | collective-permute-start | bytes 786440 | tf_op jit(solution)/shard_map/ppermute | solution.py:297
  20.3 1.2 %collective-permute-done.9.refs_9_ = bf16[256,512]{1,0:T(8,128)(2,1)S(1)} collective-permute-done((bf16[256,512]{1,0:T(8,128)(2,1)S(1)}, bf16[256,512]{1,0:T(8,128)(2,1)S(1)}, u32[]{:S(2)}, u32[]{:S(2)}) %collective-permute-start.9) | collective-permute-done | bytes 262176 | tf_op jit(solution)/shard_map/ppermute | solution.py:297
  21.5 2.1 %collective-permute-start.13 = (bf16[256,512]{1,0:T(8,128)(2,1)S(1)}, bf16[256,512]{1,0:T(8,128)(2,1)S(1)}, u32[]{:S(2)}, u32[]{:S(2)}) collective-permute-start(bf16[256,512]{1,0:T(8,128)(2,1)S(1)} %collective-permute-done.9.refs_9_), channel_id=1, source_target_pairs={{0,5},{1,2},{2,7},{3,0},{4,1},{5,8},{6,3},{7,10},{8,13},{9,4},{10,... | collective-permute-start | bytes 786440 | tf_op jit(solution)/shard_map/ppermute | solution.py:297
  23.6 0.0 collective-permute-start.6
  23.6 0.0 collective-permute-done.2.refs_8_
  23.6 0.5 %collective-permute-start.10 = (bf16[256,512]{1,0:T(8,128)(2,1)S(1)}, bf16[256,512]{1,0:T(8,128)(2,1)S(1)}, u32[]{:S(2)}, u32[]{:S(2)}) collective-permute-start(bf16[256,512]{1,0:T(8,128)(2,1)S(1)} %collective-permute-done.9.refs_9_), channel_id=1, source_target_pairs={{0,1},{1,0},{2,3},{3,2},{4,5},{5,4},{6,7},{7,6},{8,9},{9,8},{10,11... | collective-permute-start | bytes 786440 | tf_op jit(solution)/shard_map/ppermute | solution.py:297
  24.1 0.0 collective-permute-done.4.refs_8_
  24.1 0.1 collective-permute-start.8
  24.2 0.1 collective-permute-done.11.refs_7_
  24.3 0.3 collective-permute-start.12
  24.6 3.0 %collective-permute-done.13.refs_9_ = bf16[256,512]{1,0:T(8,128)(2,1)S(1)} collective-permute-done((bf16[256,512]{1,0:T(8,128)(2,1)S(1)}, bf16[256,512]{1,0:T(8,128)(2,1)S(1)}, u32[]{:S(2)}, u32[]{:S(2)}) %collective-permute-start.13) | collective-permute-done | bytes 262176 | tf_op jit(solution)/shard_map/ppermute | solution.py:297
  27.6 0.1 collective-permute-start.14
  29.0 1.0 %shard_map.124 = (bf16[640,512]{1,0:T(8,128)(2,1)S(1)}, bf16[512,64]{1,0:T(8,128)(2,1)S(1)}, f32[1,64]{1,0:T(1,128)S(1)}, f32[144,64]{1,0:T(8,128)S(1)}) custom-call(s32[2]{0:T(128)} %length_hbm.1, bf16[64,4096]{1,0:T(8,128)(2,1)S(1)} %get-tuple-element.35.query_ref, bf16[2,4096]{1,0:T(2,128)(2,1)S(1)} %get-tuple-element.36.cont_ref, ...), custom_call_target="tpu_custom_call" | custom-call | flops 67108864 | bytes 1048576 | tf_op jit(solution)/shard_map/pallas_call | solution.py:318
  30.0 1.0 %shard_map.125 = (f32[1,64]{1,0:T(1,128)S(1)}, f32[144,64]{1,0:T(8,128)S(1)}, f32[4,1,512]{2,1,0:T(1,128)S(1)}, f32[4,144,512]{2,1,0:T(8,128)S(1)}) custom-call(s32[2,128]{1,0:T(2,128)S(1)} %shard_map.122.refs_0_, bf16[640,512]{1,0:T(8,128)(2,1)S(1)} %get-tuple-element.39.refs_1_, ...), custom_call_target="tpu_custom_call", output_to_operand_aliasing={{0}: (3, {}), {1}: (4, {})} | custom-call | flops 134217728 | bytes 1048576 | tf_op jit(solution)/shard_map/pallas_call | solution.py:351
  31.0 1.2 %shard_map.126 = (f32[1,64]{1,0:T(1,128)S(1)}, f32[144,64]{1,0:T(8,128)S(1)}, f32[4,1,512]{2,1,0:T(1,128)S(1)}, f32[4,144,512]{2,1,0:T(8,128)S(1)}) custom-call(s32[2,128]{1,0:T(2,128)S(1)} %shard_map.122.refs_0_, bf16[640,512]{1,0:T(8,128)(2,1)S(1)} %get-tuple-element.39.refs_1_, ...), custom_call_target="tpu_custom_call", output_to_operand_aliasing={{0}: (3, {}), {1}: (4, {}), {2}: (5, {}), {3}: (6, {})} | custom-call | flops 134217728 | bytes 1048576 | tf_op jit(solution)/shard_map/pallas_call | solution.py:351
  32.2 1.2 %shard_map.127 = (f32[1,64]{1,0:T(1,128)S(1)}, f32[144,64]{1,0:T(8,128)S(1)}, f32[4,1,512]{2,1,0:T(1,128)S(1)}, f32[4,144,512]{2,1,0:T(8,128)S(1)}) custom-call(s32[2,128]{1,0:T(2,128)S(1)} %shard_map.122.refs_0_, bf16[640,512]{1,0:T(8,128)(2,1)S(1)} %get-tuple-element.39.refs_1_, ...), custom_call_target="tpu_custom_call", output_to_operand_aliasing={{0}: (3, {}), {1}: (4, {}), {2}: (5, {}), {3}: (6, {})} | custom-call | flops 134217728 | bytes 1048576 | tf_op jit(solution)/shard_map/pallas_call | solution.py:351
  33.3 0.0 collective-permute-done.6.refs_8_
  33.3 1.2 %shard_map.128 = (f32[1,64]{1,0:T(1,128)S(1)}, f32[144,64]{1,0:T(8,128)S(1)}, f32[4,1,512]{2,1,0:T(1,128)S(1)}, f32[4,144,512]{2,1,0:T(8,128)S(1)}) custom-call(s32[2,128]{1,0:T(2,128)S(1)} %shard_map.122.refs_0_, bf16[640,512]{1,0:T(8,128)(2,1)S(1)} %get-tuple-element.39.refs_1_, ...), custom_call_target="tpu_custom_call", output_to_operand_aliasing={{0}: (3, {}), {1}: (4, {}), {2}: (5, {}), {3}: (6, {})} | custom-call | flops 134217728 | bytes 1048576 | tf_op jit(solution)/shard_map/pallas_call | solution.py:351
  34.5 0.0 collective-permute-done.10.refs_10_
  34.5 0.0 collective-permute-done.8.refs_8_
  34.5 1.9 %shard_map.129 = (f32[1,64]{1,0:T(1,128)S(1)}, f32[144,64]{1,0:T(8,128)S(1)}, f32[4,1,512]{2,1,0:T(1,128)S(1)}, f32[4,144,512]{2,1,0:T(8,128)S(1)}) custom-call(s32[2,128]{1,0:T(2,128)S(1)} %shard_map.122.refs_0_, bf16[640,512]{1,0:T(8,128)(2,1)S(1)} %get-tuple-element.39.refs_1_, ...), custom_call_target="tpu_custom_call", output_to_operand_aliasing={{0}: (3, {}), {1}: (4, {}), {2}: (5, {}), {3}: (6, {})} | custom-call | flops 268435456 | bytes 1048576 | tf_op jit(solution)/shard_map/pallas_call | solution.py:351
  36.4 0.0 collective-permute-done.12.refs_8_
  36.4 1.7 %shard_map.130 = (f32[1,64]{1,0:T(1,128)S(1)}, f32[144,64]{1,0:T(8,128)S(1)}, f32[4,1,512]{2,1,0:T(1,128)S(1)}, f32[4,144,512]{2,1,0:T(8,128)S(1)}) custom-call(s32[2,128]{1,0:T(2,128)S(1)} %shard_map.122.refs_0_, bf16[640,512]{1,0:T(8,128)(2,1)S(1)} %get-tuple-element.39.refs_1_, ...), custom_call_target="tpu_custom_call", output_to_operand_aliasing={{0}: (3, {}), {1}: (4, {}), {2}: (5, {}), {3}: (6, {})} | custom-call | flops 201326592 | bytes 1048576 | tf_op jit(solution)/shard_map/pallas_call | solution.py:351
  38.2 0.0 collective-permute-done.14.refs_7_
  38.2 1.5 %shard_map.131 = (bf16[64,4096]{1,0:T(8,128)(2,1)}, bf16[2,4096]{1,0:T(2,128)(2,1)}) custom-call(s32[2,128]{1,0:T(2,128)S(1)} %shard_map.122.refs_0_, bf16[640,512]{1,0:T(8,128)(2,1)S(1)} %get-tuple-element.39.refs_1_, bf16[512,64]{1,0:T(8,128)(2,1)S(1)} %get-tuple-element.40.refs_2_, f32[1,64]{1,0:T(1,128)S(1)} %get-tuple-element.64.refs_3_, ...), custom_call_target="tpu_custom_call" | custom-call | flops 67108864 | bytes 1048576 | tf_op jit(solution)/shard_map/pallas_call | solution.py:351
  (1 shorter events, 0.0 us)
Async XLA Ops:
  2.1 3.2 %collective-permute-start = (bf16[256,512]{1,0:T(8,128)(2,1)S(1)}, bf16[256,512]{1,0:T(8,128)(2,1)S(1)}, u32[]{:S(2)}, u32[]{:S(2)}) collective-permute-start(bf16[256,512]{1,0:T(8,128)(2,1)S(1)} %get-tuple-element.43.refs_5_), channel_id=1, source_target_pairs={{0,1},{1,0},{2,3},{3,2},{4,5},{5,4},{6,7},{7,6},{8,9},{9,8},{10,11... | collective-permute-start | bytes 786440 | tf_op jit(solution)/shard_map/ppermute | solution.py:297
  2.6 6.7 %collective-permute-start.1 = (bf16[256,512]{1,0:T(8,128)(2,1)S(1)}, bf16[256,512]{1,0:T(8,128)(2,1)S(1)}, u32[]{:S(2)}, u32[]{:S(2)}) collective-permute-start(bf16[256,512]{1,0:T(8,128)(2,1)S(1)} %get-tuple-element.43.refs_5_), channel_id=1, source_target_pairs={{0,5},{1,2},{2,7},{3,0},{4,1},{5,8},{6,3},{7,10},{8,13},{9,4},{10,... | collective-permute-start | bytes 786440 | tf_op jit(solution)/shard_map/ppermute | solution.py:297
  5.3 6.8 %collective-permute-start.3 = (bf16[256,512]{1,0:T(8,128)(2,1)S(1)}, bf16[256,512]{1,0:T(8,128)(2,1)S(1)}, u32[]{:S(2)}, u32[]{:S(2)}) collective-permute-start(bf16[256,512]{1,0:T(8,128)(2,1)S(1)} %collective-permute-done.refs_6_), channel_id=1, source_target_pairs={{0,5},{1,2},{2,7},{3,0},{4,1},{5,8},{6,3},{7,10},{8,13},{9,4},{10,... | collective-permute-start | bytes 786440 | tf_op jit(solution)/shard_map/ppermute | solution.py:297
  9.3 6.1 %collective-permute-start.5 = (bf16[256,512]{1,0:T(8,128)(2,1)S(1)}, bf16[256,512]{1,0:T(8,128)(2,1)S(1)}, u32[]{:S(2)}, u32[]{:S(2)}) collective-permute-start(bf16[256,512]{1,0:T(8,128)(2,1)S(1)} %collective-permute-done.1.refs_7_), channel_id=1, source_target_pairs={{0,5},{1,2},{2,7},{3,0},{4,1},{5,8},{6,3},{7,10},{8,13},{9,4},{10,... | collective-permute-start | bytes 786440 | tf_op jit(solution)/shard_map/ppermute | solution.py:297
  12.1 6.1 %collective-permute-start.7 = (bf16[256,512]{1,0:T(8,128)(2,1)S(1)}, bf16[256,512]{1,0:T(8,128)(2,1)S(1)}, u32[]{:S(2)}, u32[]{:S(2)}) collective-permute-start(bf16[256,512]{1,0:T(8,128)(2,1)S(1)} %collective-permute-done.3.refs_7_), channel_id=1, source_target_pairs={{0,5},{1,2},{2,7},{3,0},{4,1},{5,8},{6,3},{7,10},{8,13},{9,4},{10,... | collective-permute-start | bytes 786440 | tf_op jit(solution)/shard_map/ppermute | solution.py:297
  15.4 6.1 %collective-permute-start.9 = (bf16[256,512]{1,0:T(8,128)(2,1)S(1)}, bf16[256,512]{1,0:T(8,128)(2,1)S(1)}, u32[]{:S(2)}, u32[]{:S(2)}) collective-permute-start(bf16[256,512]{1,0:T(8,128)(2,1)S(1)} %collective-permute-done.5.refs_7_), channel_id=1, source_target_pairs={{0,5},{1,2},{2,7},{3,0},{4,1},{5,8},{6,3},{7,10},{8,13},{9,4},{10,... | collective-permute-start | bytes 786440 | tf_op jit(solution)/shard_map/ppermute | solution.py:297
  17.5 6.1 %collective-permute-start.2 = (bf16[256,512]{1,0:T(8,128)(2,1)S(1)}, bf16[256,512]{1,0:T(8,128)(2,1)S(1)}, u32[]{:S(2)}, u32[]{:S(2)}) collective-permute-start(bf16[256,512]{1,0:T(8,128)(2,1)S(1)} %collective-permute-done.1.refs_7_), channel_id=1, source_target_pairs={{0,1},{1,0},{2,3},{3,2},{4,5},{5,4},{6,7},{7,6},{8,9},{9,8},{10,11... | collective-permute-start | bytes 786440 | tf_op jit(solution)/shard_map/ppermute | solution.py:297
  17.5 6.6 %collective-permute-start.4 = (bf16[256,512]{1,0:T(8,128)(2,1)S(1)}, bf16[256,512]{1,0:T(8,128)(2,1)S(1)}, u32[]{:S(2)}, u32[]{:S(2)}) collective-permute-start(bf16[256,512]{1,0:T(8,128)(2,1)S(1)} %collective-permute-done.3.refs_7_), channel_id=1, source_target_pairs={{0,1},{1,0},{2,3},{3,2},{4,5},{5,4},{6,7},{7,6},{8,9},{9,8},{10,11... | collective-permute-start | bytes 786440 | tf_op jit(solution)/shard_map/ppermute | solution.py:297
  18.2 6.1 %collective-permute-start.11 = (bf16[256,512]{1,0:T(8,128)(2,1)S(1)}, bf16[256,512]{1,0:T(8,128)(2,1)S(1)}, u32[]{:S(2)}, u32[]{:S(2)}) collective-permute-start(bf16[256,512]{1,0:T(8,128)(2,1)S(1)} %collective-permute-done.7.refs_7_), channel_id=1, source_target_pairs={{0,5},{1,2},{2,7},{3,0},{4,1},{5,8},{6,3},{7,10},{8,13},{9,4},{10,... | collective-permute-start | bytes 786440 | tf_op jit(solution)/shard_map/ppermute | solution.py:297
  21.5 6.1 %collective-permute-start.13 = (bf16[256,512]{1,0:T(8,128)(2,1)S(1)}, bf16[256,512]{1,0:T(8,128)(2,1)S(1)}, u32[]{:S(2)}, u32[]{:S(2)}) collective-permute-start(bf16[256,512]{1,0:T(8,128)(2,1)S(1)} %collective-permute-done.9.refs_9_), channel_id=1, source_target_pairs={{0,5},{1,2},{2,7},{3,0},{4,1},{5,8},{6,3},{7,10},{8,13},{9,4},{10,... | collective-permute-start | bytes 786440 | tf_op jit(solution)/shard_map/ppermute | solution.py:297
  23.6 9.8 %collective-permute-start.6 = (bf16[256,512]{1,0:T(8,128)(2,1)S(1)}, bf16[256,512]{1,0:T(8,128)(2,1)S(1)}, u32[]{:S(2)}, u32[]{:S(2)}) collective-permute-start(bf16[256,512]{1,0:T(8,128)(2,1)S(1)} %collective-permute-done.5.refs_7_), channel_id=1, source_target_pairs={{0,1},{1,0},{2,3},{3,2},{4,5},{5,4},{6,7},{7,6},{8,9},{9,8},{10,11... | collective-permute-start | bytes 786440 | tf_op jit(solution)/shard_map/ppermute | solution.py:297
  23.6 10.9 %collective-permute-start.10 = (bf16[256,512]{1,0:T(8,128)(2,1)S(1)}, bf16[256,512]{1,0:T(8,128)(2,1)S(1)}, u32[]{:S(2)}, u32[]{:S(2)}) collective-permute-start(bf16[256,512]{1,0:T(8,128)(2,1)S(1)} %collective-permute-done.9.refs_9_), channel_id=1, source_target_pairs={{0,1},{1,0},{2,3},{3,2},{4,5},{5,4},{6,7},{7,6},{8,9},{9,8},{10,11... | collective-permute-start | bytes 786440 | tf_op jit(solution)/shard_map/ppermute | solution.py:297
  24.1 10.4 %collective-permute-start.8 = (bf16[256,512]{1,0:T(8,128)(2,1)S(1)}, bf16[256,512]{1,0:T(8,128)(2,1)S(1)}, u32[]{:S(2)}, u32[]{:S(2)}) collective-permute-start(bf16[256,512]{1,0:T(8,128)(2,1)S(1)} %collective-permute-done.7.refs_7_), channel_id=1, source_target_pairs={{0,1},{1,0},{2,3},{3,2},{4,5},{5,4},{6,7},{7,6},{8,9},{9,8},{10,11... | collective-permute-start | bytes 786440 | tf_op jit(solution)/shard_map/ppermute | solution.py:297
  24.3 12.2 %collective-permute-start.12 = (bf16[256,512]{1,0:T(8,128)(2,1)S(1)}, bf16[256,512]{1,0:T(8,128)(2,1)S(1)}, u32[]{:S(2)}, u32[]{:S(2)}) collective-permute-start(bf16[256,512]{1,0:T(8,128)(2,1)S(1)} %collective-permute-done.11.refs_7_), channel_id=1, source_target_pairs={{0,1},{1,0},{2,3},{3,2},{4,5},{5,4},{6,7},{7,6},{8,9},{9,8},{10,11... | collective-permute-start | bytes 786440 | tf_op jit(solution)/shard_map/ppermute | solution.py:297
  27.6 10.6 %collective-permute-start.14 = (bf16[256,512]{1,0:T(8,128)(2,1)S(1)}, bf16[256,512]{1,0:T(8,128)(2,1)S(1)}, u32[]{:S(2)}, u32[]{:S(2)}) collective-permute-start(bf16[256,512]{1,0:T(8,128)(2,1)S(1)} %collective-permute-done.13.refs_9_), channel_id=1, source_target_pairs={{0,1},{1,0},{2,3},{3,2},{4,5},{5,4},{6,7},{7,6},{8,9},{9,8},{10,11... | collective-permute-start | bytes 786440 | tf_op jit(solution)/shard_map/ppermute | solution.py:297

commit v6 on v5

--- a/solution.py
+++ b/solution.py
@@ -57,8 +57,7 @@
     return 2 * ring_chip(place, chips) + held
 
 
-def pack_kernel(ck_hbm, nk_hbm, cv_hbm, nv_hbm, *refs):
-    others, out_ref, targets, value_ref, sems = refs[:4], refs[4], refs[5:9], refs[9], refs[10]
+def pack_kernel(ck_hbm, nk_hbm, cv_hbm, nv_hbm, out_ref, value_ref, sems):
     cache_rows, keys = ck_hbm.shape[0], value_ref.shape[0]
     copies = [
         pltpu.make_async_copy(source, target, sems.at[index])
@@ -68,7 +67,6 @@
                 (nv_hbm, value_ref.at[cache_rows:]),
                 (ck_hbm, out_ref.at[:cache_rows]),
                 (nk_hbm, out_ref.at[cache_rows:keys]),
-                *zip(others, targets),
             ]
         )
     ]
@@ -113,17 +111,33 @@
 
 
 def prep_kernel(
-    length_hbm, query_ref, cont_ref, key_ref, value_ref,
-    q_ref, cont_q_ref, cont_max_ref, cont_total_ref, length_ref, sem,
+    length_hbm, query_hbm, cont_hbm, key_hbm, value_hbm,
+    q_ref, cont_q_ref, cont_max_ref, cont_total_ref,
+    length_ref, query_ref, cont_ref, key_ref, value_ref, sems,
 ):
-    load = pltpu.make_async_copy(length_hbm, length_ref, sem)
-    load.start()
+    loads = [
+        pltpu.make_async_copy(source, target, sems.at[index])
+        for index, (source, target) in enumerate(
+            [
+                (query_hbm, query_ref), (cont_hbm, cont_ref), (key_hbm, key_ref),
+                (value_hbm, value_ref), (length_hbm, length_ref),
+            ]
+        )
+    ]
+    for load in loads:
+        load.start()
     prompt_rows = query_ref.shape[0]
     cont_count, suffix_rows = key_ref.shape[:2]
     cont_rows = cont_count * GROUP
     dot = functools.partial(jnp.dot, preferred_element_type=F32)
+    q_ref[KVH * HD :] = row_features(GROUP * prompt_rows, prompt_rows)
+    heads = [slice(head * HD, (head + 1) * HD) for head in range(KVH * GROUP)]
+    for load in loads[:2]:
+        load.wait()
+    for g in range(KVH):
+        q = jnp.concatenate([query_ref[:, head] for head in heads[g * GROUP : (g + 1) * GROUP]], axis=0)
+        q_ref[g * HD : (g + 1) * HD] = q.T
     cont = cont_ref[...].astype(F32)
-    heads = [slice(head * HD, (head + 1) * HD) for head in range(KVH * GROUP)]
     cont_q = jnp.concatenate(
         [
             cont[c : c + 1, head]
@@ -137,14 +151,11 @@
     cont_q = jnp.concatenate([jnp.where(column == g, cont_q, 0.0) for g in range(KVH)], axis=0)
     cont_q = cont_q.astype(BF16)
     cont_q_ref[...] = cont_q
+    for load in loads[2:]:
+        load.wait()
     scores = [dot(key_ref[c], cont_q) for c in range(cont_count)]
-    for g in range(KVH):
-        q = jnp.concatenate([query_ref[:, head] for head in heads[g * GROUP : (g + 1) * GROUP]], axis=0)
-        q_ref[g * HD : (g + 1) * HD] = q.T
-    q_ref[KVH * HD :] = row_features(GROUP * prompt_rows, prompt_rows)
     v = value_ref[...].reshape(cont_count * suffix_rows, KVH * HD).T
     v = jnp.concatenate([v, jnp.ones((ONES, v.shape[1]), BF16)], axis=0)
-    load.wait()
     key = lax.broadcasted_iota(jnp.int32, scores[0].shape, 0)
     owner = lax.broadcasted_iota(jnp.int32, scores[0].shape, 1) % cont_rows // GROUP
     s = jnp.concatenate(
@@ -296,16 +307,14 @@
     def send(block, pairs):
         return lax.ppermute(block, "ctx", pairs)
 
-    rest = (new_queries, cont_queries, suffix_keys, suffix_values)
-    arrays = (cache_keys, new_keys, cache_values, new_values, *rest)
-    own, *rest = pl.pallas_call(
+    own = pl.pallas_call(
         pack_kernel,
-        out_shape=[shape((keys + HD, KVH * HD), BF16)] + [shape(x.shape, BF16) for x in rest],
-        in_specs=[HBM] * 8,
-        out_specs=[VMEM] * 5,
-        scratch_shapes=[pltpu.VMEM((keys, KVH * HD), BF16), pltpu.SemaphoreType.DMA((8,))],
+        out_shape=shape((keys + HD, KVH * HD), BF16),
+        in_specs=[HBM] * 4,
+        out_specs=VMEM,
+        scratch_shapes=[pltpu.VMEM((keys, KVH * HD), BF16), pltpu.SemaphoreType.DMA((4,))],
         compiler_params=params,
-    )(*[in_hbm(x) for x in arrays])
+    )(*[in_hbm(x) for x in (cache_keys, new_keys, cache_values, new_values)])
     other = send(own, pair)
     waiting = [((0, False, False), own), ((0, False, True), other)]
 
@@ -321,12 +330,19 @@
             shape(((KVH + 1) * HD, rows), BF16),
             shape((KVH * HD, cont_rows), BF16),
         ] + state_shape[:2],
-        in_specs=[HBM] + [VMEM] * 4,
+        in_specs=[HBM] * 5,
         out_specs=[VMEM] * 4,
-        scratch_shapes=[pltpu.SMEM(suffix_length.shape, jnp.int32), pltpu.SemaphoreType.DMA(())],
+        scratch_shapes=[
+            pltpu.SMEM(suffix_length.shape, jnp.int32),
+            pltpu.VMEM(new_queries.shape, BF16),
+            pltpu.VMEM(cont_queries.shape, BF16),
+            pltpu.VMEM(suffix_keys.shape, BF16),
+            pltpu.VMEM(suffix_values.shape, BF16),
+            pltpu.SemaphoreType.DMA((5,)),
+        ],
         compiler_params=params,
         cost_estimate=cost(rows, keys),
-    )(in_hbm(suffix_length), *rest)
+    )(*[in_hbm(x) for x in (suffix_length, new_queries, cont_queries, suffix_keys, suffix_values)])
 
     window = pl.pallas_call(
         window_kernel,

time: 39.9 us -> 40.4 us (1.013)
  Pallas kernels: 12 us -> 12.5 us
    pallas_call x1, Pallas kernels: 0.95 us -> 1.8 us  [body(): pl.pallas_call(prep_kernel, out_shape=[shape(((KVH + 1) * HD, rows), BF16...]
    pallas_call x1, Pallas kernels: 1.42 us -> 1 us  [body(): pl.pallas_call(pack_kernel, out_shape=shape((keys + HD, KVH * HD), BF16),...]
  transfers between devices with their start and end apart: 15 -> 15, of which waited for: 7 -> 7; matrix products, arithmetic and copies ran while one was open for 0% -> 0% of each run, Pallas kernels for 23% -> 25%
where the time goes in v6:
time: 40.4 us; the launch traced here: 40.2 us
  starting transfers between devices  16.5 us (41%)
  Pallas kernels  12.5 us (31%)
  waiting for transfers between devices  9.15 us (23%)
  between operations  2.04 us (5%)
    ppermute x15, starting transfers between devices, send(): return lax.ppermute(block, 'ctx', pairs)  16.5 us
    pallas_call x7, Pallas kernels, take(): pl.pallas_call(functools.partial(take_kernel, size, cache_rows, prompt_ro...  9.71 us
    ppermute x15, waiting for transfers between devices, send(): return lax.ppermute(block, 'ctx', pairs)  9.15 us
    pallas_call x1, Pallas kernels, body(): pl.pallas_call(prep_kernel, out_shape=[shape(((KVH + 1) * HD, rows), BF16...  1.8 us
    pallas_call x1, Pallas kernels, body(): pl.pallas_call(pack_kernel, out_shape=shape((keys + HD, KVH * HD), BF16),...  1 us
  transfers between devices with their start and end apart: 15, of which 7 were waited for; matrix products, arithmetic and copies ran while one was open for 0% of the time, Pallas kernels for 25%

profile of v6, /device:TPU:0, one launch (start us, length us, event | category | flops | bytes accessed | tf_op | source)
XLA Modules:
  0.0 40.2 jit_solution(17555455440352380506)
XLA Ops:
  0.6 1.0 %shard_map.124.refs_5_ = bf16[256,512]{1,0:T(8,128)(2,1)S(1)} custom-call(bf16[64,512]{1,0:T(8,128)(2,1)} %ck_hbm.1, bf16[64,512]{1,0:T(8,128)(2,1)} %nk_hbm.1, bf16[64,512]{1,0:T(8,128)(2,1)} %cv_hbm.1, bf16[64,512]{1,0:T(8,128)(2,1)} %nv_hbm.1), custom_call_target="tpu_custom_call" | custom-call | tf_op jit(solution)/shard_map/pallas_call | solution.py:310
  1.6 0.6 %collective-permute-start = (bf16[256,512]{1,0:T(8,128)(2,1)S(1)}, bf16[256,512]{1,0:T(8,128)(2,1)S(1)}, u32[]{:S(2)}, u32[]{:S(2)}) collective-permute-start(bf16[256,512]{1,0:T(8,128)(2,1)S(1)} %shard_map.124.refs_5_), channel_id=1, source_target_pairs={{0,1},{1,0},{2,3},{3,2},{4,5},{5,4},{6,7},{7,6},{8,9},{9,8},{10,11... | collective-permute-start | bytes 786440 | tf_op jit(solution)/shard_map/ppermute | solution.py:308
  2.2 2.7 %collective-permute-start.1 = (bf16[256,512]{1,0:T(8,128)(2,1)S(1)}, bf16[256,512]{1,0:T(8,128)(2,1)S(1)}, u32[]{:S(2)}, u32[]{:S(2)}) collective-permute-start(bf16[256,512]{1,0:T(8,128)(2,1)S(1)} %shard_map.124.refs_5_), channel_id=1, source_target_pairs={{0,5},{1,2},{2,7},{3,0},{4,1},{5,8},{6,3},{7,10},{8,13},{9,4},{10,... | collective-permute-start | bytes 786440 | tf_op jit(solution)/shard_map/ppermute | solution.py:308
  4.9 0.0 collective-permute-done.refs_6_
  4.9 1.2 %collective-permute-start.3 = (bf16[256,512]{1,0:T(8,128)(2,1)S(1)}, bf16[256,512]{1,0:T(8,128)(2,1)S(1)}, u32[]{:S(2)}, u32[]{:S(2)}) collective-permute-start(bf16[256,512]{1,0:T(8,128)(2,1)S(1)} %collective-permute-done.refs_6_), channel_id=1, source_target_pairs={{0,5},{1,2},{2,7},{3,0},{4,1},{5,8},{6,3},{7,10},{8,13},{9,4},{10,... | collective-permute-start | bytes 786440 | tf_op jit(solution)/shard_map/ppermute | solution.py:308
  6.1 2.7 %collective-permute-done.1.refs_7_ = bf16[256,512]{1,0:T(8,128)(2,1)S(1)} collective-permute-done((bf16[256,512]{1,0:T(8,128)(2,1)S(1)}, bf16[256,512]{1,0:T(8,128)(2,1)S(1)}, u32[]{:S(2)}, u32[]{:S(2)}) %collective-permute-start.1) | collective-permute-done | bytes 262176 | tf_op jit(solution)/shard_map/ppermute | solution.py:308
  8.9 2.1 %collective-permute-start.5 = (bf16[256,512]{1,0:T(8,128)(2,1)S(1)}, bf16[256,512]{1,0:T(8,128)(2,1)S(1)}, u32[]{:S(2)}, u32[]{:S(2)}) collective-permute-start(bf16[256,512]{1,0:T(8,128)(2,1)S(1)} %collective-permute-done.1.refs_7_), channel_id=1, source_target_pairs={{0,5},{1,2},{2,7},{3,0},{4,1},{5,8},{6,3},{7,10},{8,13},{9,4},{10,... | collective-permute-start | bytes 786440 | tf_op jit(solution)/shard_map/ppermute | solution.py:308
  11.0 0.7 %collective-permute-done.3.refs_7_ = bf16[256,512]{1,0:T(8,128)(2,1)S(1)} collective-permute-done((bf16[256,512]{1,0:T(8,128)(2,1)S(1)}, bf16[256,512]{1,0:T(8,128)(2,1)S(1)}, u32[]{:S(2)}, u32[]{:S(2)}) %collective-permute-start.3) | collective-permute-done | bytes 262176 | tf_op jit(solution)/shard_map/ppermute | solution.py:308
  11.7 2.1 %collective-permute-start.7 = (bf16[256,512]{1,0:T(8,128)(2,1)S(1)}, bf16[256,512]{1,0:T(8,128)(2,1)S(1)}, u32[]{:S(2)}, u32[]{:S(2)}) collective-permute-start(bf16[256,512]{1,0:T(8,128)(2,1)S(1)} %collective-permute-done.3.refs_7_), channel_id=1, source_target_pairs={{0,5},{1,2},{2,7},{3,0},{4,1},{5,8},{6,3},{7,10},{8,13},{9,4},{10,... | collective-permute-start | bytes 786440 | tf_op jit(solution)/shard_map/ppermute | solution.py:308
  13.8 1.2 %collective-permute-done.5.refs_7_ = bf16[256,512]{1,0:T(8,128)(2,1)S(1)} collective-permute-done((bf16[256,512]{1,0:T(8,128)(2,1)S(1)}, bf16[256,512]{1,0:T(8,128)(2,1)S(1)}, u32[]{:S(2)}, u32[]{:S(2)}) %collective-permute-start.5) | collective-permute-done | bytes 262176 | tf_op jit(solution)/shard_map/ppermute | solution.py:308
  15.0 2.1 %collective-permute-start.9 = (bf16[256,512]{1,0:T(8,128)(2,1)S(1)}, bf16[256,512]{1,0:T(8,128)(2,1)S(1)}, u32[]{:S(2)}, u32[]{:S(2)}) collective-permute-start(bf16[256,512]{1,0:T(8,128)(2,1)S(1)} %collective-permute-done.5.refs_7_), channel_id=1, source_target_pairs={{0,5},{1,2},{2,7},{3,0},{4,1},{5,8},{6,3},{7,10},{8,13},{9,4},{10,... | collective-permute-start | bytes 786440 | tf_op jit(solution)/shard_map/ppermute | solution.py:308
  17.1 0.0 collective-permute-start.2
  17.1 0.5 %collective-permute-start.4 = (bf16[256,512]{1,0:T(8,128)(2,1)S(1)}, bf16[256,512]{1,0:T(8,128)(2,1)S(1)}, u32[]{:S(2)}, u32[]{:S(2)}) collective-permute-start(bf16[256,512]{1,0:T(8,128)(2,1)S(1)} %collective-permute-done.3.refs_7_), channel_id=1, source_target_pairs={{0,1},{1,0},{2,3},{3,2},{4,5},{5,4},{6,7},{7,6},{8,9},{9,8},{10,11... | collective-permute-start | bytes 786440 | tf_op jit(solution)/shard_map/ppermute | solution.py:308
  17.6 0.2 collective-permute-done.7.refs_7_
  17.8 2.1 %collective-permute-start.11 = (bf16[256,512]{1,0:T(8,128)(2,1)S(1)}, bf16[256,512]{1,0:T(8,128)(2,1)S(1)}, u32[]{:S(2)}, u32[]{:S(2)}) collective-permute-start(bf16[256,512]{1,0:T(8,128)(2,1)S(1)} %collective-permute-done.7.refs_7_), channel_id=1, source_target_pairs={{0,5},{1,2},{2,7},{3,0},{4,1},{5,8},{6,3},{7,10},{8,13},{9,4},{10,... | collective-permute-start | bytes 786440 | tf_op jit(solution)/shard_map/ppermute | solution.py:308
  19.9 1.2 %collective-permute-done.9.refs_9_ = bf16[256,512]{1,0:T(8,128)(2,1)S(1)} collective-permute-done((bf16[256,512]{1,0:T(8,128)(2,1)S(1)}, bf16[256,512]{1,0:T(8,128)(2,1)S(1)}, u32[]{:S(2)}, u32[]{:S(2)}) %collective-permute-start.9) | collective-permute-done | bytes 262176 | tf_op jit(solution)/shard_map/ppermute | solution.py:308
  21.1 2.1 %collective-permute-start.13 = (bf16[256,512]{1,0:T(8,128)(2,1)S(1)}, bf16[256,512]{1,0:T(8,128)(2,1)S(1)}, u32[]{:S(2)}, u32[]{:S(2)}) collective-permute-start(bf16[256,512]{1,0:T(8,128)(2,1)S(1)} %collective-permute-done.9.refs_9_), channel_id=1, source_target_pairs={{0,5},{1,2},{2,7},{3,0},{4,1},{5,8},{6,3},{7,10},{8,13},{9,4},{10,... | collective-permute-start | bytes 786440 | tf_op jit(solution)/shard_map/ppermute | solution.py:308
  23.1 0.0 collective-permute-start.6
  23.1 0.0 collective-permute-done.2.refs_8_
  23.2 0.5 %collective-permute-start.10 = (bf16[256,512]{1,0:T(8,128)(2,1)S(1)}, bf16[256,512]{1,0:T(8,128)(2,1)S(1)}, u32[]{:S(2)}, u32[]{:S(2)}) collective-permute-start(bf16[256,512]{1,0:T(8,128)(2,1)S(1)} %collective-permute-done.9.refs_9_), channel_id=1, source_target_pairs={{0,1},{1,0},{2,3},{3,2},{4,5},{5,4},{6,7},{7,6},{8,9},{9,8},{10,11... | collective-permute-start | bytes 786440 | tf_op jit(solution)/shard_map/ppermute | solution.py:308
  23.7 0.0 collective-permute-done.4.refs_8_
  23.7 0.1 collective-permute-start.8
  23.7 0.1 collective-permute-done.11.refs_7_
  23.9 0.3 collective-permute-start.12
  24.2 3.0 %collective-permute-done.13.refs_9_ = bf16[256,512]{1,0:T(8,128)(2,1)S(1)} collective-permute-done((bf16[256,512]{1,0:T(8,128)(2,1)S(1)}, bf16[256,512]{1,0:T(8,128)(2,1)S(1)}, u32[]{:S(2)}, u32[]{:S(2)}) %collective-permute-start.13) | collective-permute-done | bytes 262176 | tf_op jit(solution)/shard_map/ppermute | solution.py:308
  27.1 0.1 collective-permute-start.14
  28.6 1.8 %shard_map.123 = (bf16[640,512]{1,0:T(8,128)(2,1)S(1)}, bf16[512,64]{1,0:T(8,128)(2,1)S(1)}, f32[1,64]{1,0:T(1,128)S(1)}, f32[144,64]{1,0:T(8,128)S(1)}) custom-call(s32[2]{0:T(128)} %length_hbm.1, bf16[64,4096]{1,0:T(8,128)(2,1)} %query_hbm.1, bf16[2,4096]{1,0:T(2,128)(2,1)} %cont_hbm.1, bf16[2,128,512]{2,1,0:T(8,128)(2,1)} %key_hbm.1, ...), custom_call_target="tpu_custom_call" | custom-call | flops 67108864 | bytes 1048576 | tf_op jit(solution)/shard_map/pallas_call | solution.py:327
  30.4 1.0 %shard_map.125 = (f32[1,64]{1,0:T(1,128)S(1)}, f32[144,64]{1,0:T(8,128)S(1)}, f32[4,1,512]{2,1,0:T(1,128)S(1)}, f32[4,144,512]{2,1,0:T(8,128)S(1)}) custom-call(s32[2,128]{1,0:T(2,128)S(1)} %shard_map.122.refs_0_, bf16[640,512]{1,0:T(8,128)(2,1)S(1)} %get-tuple-element.30.refs_1_, ...), custom_call_target="tpu_custom_call", output_to_operand_aliasing={{0}: (3, {}), {1}: (4, {})} | custom-call | flops 134217728 | bytes 1048576 | tf_op jit(solution)/shard_map/pallas_call | solution.py:367
  31.4 1.2 %shard_map.126 = (f32[1,64]{1,0:T(1,128)S(1)}, f32[144,64]{1,0:T(8,128)S(1)}, f32[4,1,512]{2,1,0:T(1,128)S(1)}, f32[4,144,512]{2,1,0:T(8,128)S(1)}) custom-call(s32[2,128]{1,0:T(2,128)S(1)} %shard_map.122.refs_0_, bf16[640,512]{1,0:T(8,128)(2,1)S(1)} %get-tuple-element.30.refs_1_, ...), custom_call_target="tpu_custom_call", output_to_operand_aliasing={{0}: (3, {}), {1}: (4, {}), {2}: (5, {}), {3}: (6, {})} | custom-call | flops 134217728 | bytes 1048576 | tf_op jit(solution)/shard_map/pallas_call | solution.py:367
  32.6 1.2 %shard_map.127 = (f32[1,64]{1,0:T(1,128)S(1)}, f32[144,64]{1,0:T(8,128)S(1)}, f32[4,1,512]{2,1,0:T(1,128)S(1)}, f32[4,144,512]{2,1,0:T(8,128)S(1)}) custom-call(s32[2,128]{1,0:T(2,128)S(1)} %shard_map.122.refs_0_, bf16[640,512]{1,0:T(8,128)(2,1)S(1)} %get-tuple-element.30.refs_1_, ...), custom_call_target="tpu_custom_call", output_to_operand_aliasing={{0}: (3, {}), {1}: (4, {}), {2}: (5, {}), {3}: (6, {})} | custom-call | flops 134217728 | bytes 1048576 | tf_op jit(solution)/shard_map/pallas_call | solution.py:367
  33.8 0.0 collective-permute-done.6.refs_8_
  33.8 1.2 %shard_map.128 = (f32[1,64]{1,0:T(1,128)S(1)}, f32[144,64]{1,0:T(8,128)S(1)}, f32[4,1,512]{2,1,0:T(1,128)S(1)}, f32[4,144,512]{2,1,0:T(8,128)S(1)}) custom-call(s32[2,128]{1,0:T(2,128)S(1)} %shard_map.122.refs_0_, bf16[640,512]{1,0:T(8,128)(2,1)S(1)} %get-tuple-element.30.refs_1_, ...), custom_call_target="tpu_custom_call", output_to_operand_aliasing={{0}: (3, {}), {1}: (4, {}), {2}: (5, {}), {3}: (6, {})} | custom-call | flops 134217728 | bytes 1048576 | tf_op jit(solution)/shard_map/pallas_call | solution.py:367
  34.9 0.0 collective-permute-done.10.refs_10_
  35.0 0.0 collective-permute-done.8.refs_8_
  35.0 1.9 %shard_map.129 = (f32[1,64]{1,0:T(1,128)S(1)}, f32[144,64]{1,0:T(8,128)S(1)}, f32[4,1,512]{2,1,0:T(1,128)S(1)}, f32[4,144,512]{2,1,0:T(8,128)S(1)}) custom-call(s32[2,128]{1,0:T(2,128)S(1)} %shard_map.122.refs_0_, bf16[640,512]{1,0:T(8,128)(2,1)S(1)} %get-tuple-element.30.refs_1_, ...), custom_call_target="tpu_custom_call", output_to_operand_aliasing={{0}: (3, {}), {1}: (4, {}), {2}: (5, {}), {3}: (6, {})} | custom-call | flops 268435456 | bytes 1048576 | tf_op jit(solution)/shard_map/pallas_call | solution.py:367
  36.9 0.0 collective-permute-done.12.refs_8_
  36.9 1.7 %shard_map.130 = (f32[1,64]{1,0:T(1,128)S(1)}, f32[144,64]{1,0:T(8,128)S(1)}, f32[4,1,512]{2,1,0:T(1,128)S(1)}, f32[4,144,512]{2,1,0:T(8,128)S(1)}) custom-call(s32[2,128]{1,0:T(2,128)S(1)} %shard_map.122.refs_0_, bf16[640,512]{1,0:T(8,128)(2,1)S(1)} %get-tuple-element.30.refs_1_, ...), custom_call_target="tpu_custom_call", output_to_operand_aliasing={{0}: (3, {}), {1}: (4, {}), {2}: (5, {}), {3}: (6, {})} | custom-call | flops 201326592 | bytes 1048576 | tf_op jit(solution)/shard_map/pallas_call | solution.py:367
  38.7 0.0 collective-permute-done.14.refs_7_
  38.7 1.5 %shard_map.131 = (bf16[64,4096]{1,0:T(8,128)(2,1)}, bf16[2,4096]{1,0:T(2,128)(2,1)}) custom-call(s32[2,128]{1,0:T(2,128)S(1)} %shard_map.122.refs_0_, bf16[640,512]{1,0:T(8,128)(2,1)S(1)} %get-tuple-element.30.refs_1_, bf16[512,64]{1,0:T(8,128)(2,1)S(1)} %get-tuple-element.31.refs_2_, f32[1,64]{1,0:T(1,128)S(1)} %get-tuple-element.54.refs_3_, ...), custom_call_target="tpu_custom_call" | custom-call | flops 67108864 | bytes 1048576 | tf_op jit(solution)/shard_map/pallas_call | solution.py:367
  (1 shorter events, 0.0 us)
Async XLA Ops:
  1.6 3.2 %collective-permute-start = (bf16[256,512]{1,0:T(8,128)(2,1)S(1)}, bf16[256,512]{1,0:T(8,128)(2,1)S(1)}, u32[]{:S(2)}, u32[]{:S(2)}) collective-permute-start(bf16[256,512]{1,0:T(8,128)(2,1)S(1)} %shard_map.124.refs_5_), channel_id=1, source_target_pairs={{0,1},{1,0},{2,3},{3,2},{4,5},{5,4},{6,7},{7,6},{8,9},{9,8},{10,11... | collective-permute-start | bytes 786440 | tf_op jit(solution)/shard_map/ppermute | solution.py:308
  2.2 6.7 %collective-permute-start.1 = (bf16[256,512]{1,0:T(8,128)(2,1)S(1)}, bf16[256,512]{1,0:T(8,128)(2,1)S(1)}, u32[]{:S(2)}, u32[]{:S(2)}) collective-permute-start(bf16[256,512]{1,0:T(8,128)(2,1)S(1)} %shard_map.124.refs_5_), channel_id=1, source_target_pairs={{0,5},{1,2},{2,7},{3,0},{4,1},{5,8},{6,3},{7,10},{8,13},{9,4},{10,... | collective-permute-start | bytes 786440 | tf_op jit(solution)/shard_map/ppermute | solution.py:308
  4.9 6.8 %collective-permute-start.3 = (bf16[256,512]{1,0:T(8,128)(2,1)S(1)}, bf16[256,512]{1,0:T(8,128)(2,1)S(1)}, u32[]{:S(2)}, u32[]{:S(2)}) collective-permute-start(bf16[256,512]{1,0:T(8,128)(2,1)S(1)} %collective-permute-done.refs_6_), channel_id=1, source_target_pairs={{0,5},{1,2},{2,7},{3,0},{4,1},{5,8},{6,3},{7,10},{8,13},{9,4},{10,... | collective-permute-start | bytes 786440 | tf_op jit(solution)/shard_map/ppermute | solution.py:308
  8.9 6.1 %collective-permute-start.5 = (bf16[256,512]{1,0:T(8,128)(2,1)S(1)}, bf16[256,512]{1,0:T(8,128)(2,1)S(1)}, u32[]{:S(2)}, u32[]{:S(2)}) collective-permute-start(bf16[256,512]{1,0:T(8,128)(2,1)S(1)} %collective-permute-done.1.refs_7_), channel_id=1, source_target_pairs={{0,5},{1,2},{2,7},{3,0},{4,1},{5,8},{6,3},{7,10},{8,13},{9,4},{10,... | collective-permute-start | bytes 786440 | tf_op jit(solution)/shard_map/ppermute | solution.py:308
  11.7 6.1 %collective-permute-start.7 = (bf16[256,512]{1,0:T(8,128)(2,1)S(1)}, bf16[256,512]{1,0:T(8,128)(2,1)S(1)}, u32[]{:S(2)}, u32[]{:S(2)}) collective-permute-start(bf16[256,512]{1,0:T(8,128)(2,1)S(1)} %collective-permute-done.3.refs_7_), channel_id=1, source_target_pairs={{0,5},{1,2},{2,7},{3,0},{4,1},{5,8},{6,3},{7,10},{8,13},{9,4},{10,... | collective-permute-start | bytes 786440 | tf_op jit(solution)/shard_map/ppermute | solution.py:308
  15.0 6.1 %collective-permute-start.9 = (bf16[256,512]{1,0:T(8,128)(2,1)S(1)}, bf16[256,512]{1,0:T(8,128)(2,1)S(1)}, u32[]{:S(2)}, u32[]{:S(2)}) collective-permute-start(bf16[256,512]{1,0:T(8,128)(2,1)S(1)} %collective-permute-done.5.refs_7_), channel_id=1, source_target_pairs={{0,5},{1,2},{2,7},{3,0},{4,1},{5,8},{6,3},{7,10},{8,13},{9,4},{10,... | collective-permute-start | bytes 786440 | tf_op jit(solution)/shard_map/ppermute | solution.py:308
  17.1 6.1 %collective-permute-start.2 = (bf16[256,512]{1,0:T(8,128)(2,1)S(1)}, bf16[256,512]{1,0:T(8,128)(2,1)S(1)}, u32[]{:S(2)}, u32[]{:S(2)}) collective-permute-start(bf16[256,512]{1,0:T(8,128)(2,1)S(1)} %collective-permute-done.1.refs_7_), channel_id=1, source_target_pairs={{0,1},{1,0},{2,3},{3,2},{4,5},{5,4},{6,7},{7,6},{8,9},{9,8},{10,11... | collective-permute-start | bytes 786440 | tf_op jit(solution)/shard_map/ppermute | solution.py:308
  17.1 6.6 %collective-permute-start.4 = (bf16[256,512]{1,0:T(8,128)(2,1)S(1)}, bf16[256,512]{1,0:T(8,128)(2,1)S(1)}, u32[]{:S(2)}, u32[]{:S(2)}) collective-permute-start(bf16[256,512]{1,0:T(8,128)(2,1)S(1)} %collective-permute-done.3.refs_7_), channel_id=1, source_target_pairs={{0,1},{1,0},{2,3},{3,2},{4,5},{5,4},{6,7},{7,6},{8,9},{9,8},{10,11... | collective-permute-start | bytes 786440 | tf_op jit(solution)/shard_map/ppermute | solution.py:308
  17.8 6.1 %collective-permute-start.11 = (bf16[256,512]{1,0:T(8,128)(2,1)S(1)}, bf16[256,512]{1,0:T(8,128)(2,1)S(1)}, u32[]{:S(2)}, u32[]{:S(2)}) collective-permute-start(bf16[256,512]{1,0:T(8,128)(2,1)S(1)} %collective-permute-done.7.refs_7_), channel_id=1, source_target_pairs={{0,5},{1,2},{2,7},{3,0},{4,1},{5,8},{6,3},{7,10},{8,13},{9,4},{10,... | collective-permute-start | bytes 786440 | tf_op jit(solution)/shard_map/ppermute | solution.py:308
  21.1 6.1 %collective-permute-start.13 = (bf16[256,512]{1,0:T(8,128)(2,1)S(1)}, bf16[256,512]{1,0:T(8,128)(2,1)S(1)}, u32[]{:S(2)}, u32[]{:S(2)}) collective-permute-start(bf16[256,512]{1,0:T(8,128)(2,1)S(1)} %collective-permute-done.9.refs_9_), channel_id=1, source_target_pairs={{0,5},{1,2},{2,7},{3,0},{4,1},{5,8},{6,3},{7,10},{8,13},{9,4},{10,... | collective-permute-start | bytes 786440 | tf_op jit(solution)/shard_map/ppermute | solution.py:308
  23.1 10.6 %collective-permute-start.6 = (bf16[256,512]{1,0:T(8,128)(2,1)S(1)}, bf16[256,512]{1,0:T(8,128)(2,1)S(1)}, u32[]{:S(2)}, u32[]{:S(2)}) collective-permute-start(bf16[256,512]{1,0:T(8,128)(2,1)S(1)} %collective-permute-done.5.refs_7_), channel_id=1, source_target_pairs={{0,1},{1,0},{2,3},{3,2},{4,5},{5,4},{6,7},{7,6},{8,9},{9,8},{10,11... | collective-permute-start | bytes 786440 | tf_op jit(solution)/shard_map/ppermute | solution.py:308
  23.2 11.8 %collective-permute-start.10 = (bf16[256,512]{1,0:T(8,128)(2,1)S(1)}, bf16[256,512]{1,0:T(8,128)(2,1)S(1)}, u32[]{:S(2)}, u32[]{:S(2)}) collective-permute-start(bf16[256,512]{1,0:T(8,128)(2,1)S(1)} %collective-permute-done.9.refs_9_), channel_id=1, source_target_pairs={{0,1},{1,0},{2,3},{3,2},{4,5},{5,4},{6,7},{7,6},{8,9},{9,8},{10,11... | collective-permute-start | bytes 786440 | tf_op jit(solution)/shard_map/ppermute | solution.py:308
  23.7 11.3 %collective-permute-start.8 = (bf16[256,512]{1,0:T(8,128)(2,1)S(1)}, bf16[256,512]{1,0:T(8,128)(2,1)S(1)}, u32[]{:S(2)}, u32[]{:S(2)}) collective-permute-start(bf16[256,512]{1,0:T(8,128)(2,1)S(1)} %collective-permute-done.7.refs_7_), channel_id=1, source_target_pairs={{0,1},{1,0},{2,3},{3,2},{4,5},{5,4},{6,7},{7,6},{8,9},{9,8},{10,11... | collective-permute-start | bytes 786440 | tf_op jit(solution)/shard_map/ppermute | solution.py:308
  23.9 13.0 %collective-permute-start.12 = (bf16[256,512]{1,0:T(8,128)(2,1)S(1)}, bf16[256,512]{1,0:T(8,128)(2,1)S(1)}, u32[]{:S(2)}, u32[]{:S(2)}) collective-permute-start(bf16[256,512]{1,0:T(8,128)(2,1)S(1)} %collective-permute-done.11.refs_7_), channel_id=1, source_target_pairs={{0,1},{1,0},{2,3},{3,2},{4,5},{5,4},{6,7},{7,6},{8,9},{9,8},{10,11... | collective-permute-start | bytes 786440 | tf_op jit(solution)/shard_map/ppermute | solution.py:308
  27.1 11.5 %collective-permute-start.14 = (bf16[256,512]{1,0:T(8,128)(2,1)S(1)}, bf16[256,512]{1,0:T(8,128)(2,1)S(1)}, u32[]{:S(2)}, u32[]{:S(2)}) collective-permute-start(bf16[256,512]{1,0:T(8,128)(2,1)S(1)} %collective-permute-done.13.refs_9_), channel_id=1, source_target_pairs={{0,1},{1,0},{2,3},{3,2},{4,5},{5,4},{6,7},{7,6},{8,9},{9,8},{10,11... | collective-permute-start | bytes 786440 | tf_op jit(solution)/shard_map/ppermute | solution.py:308

commit v7 on v6

--- a/solution.py
+++ b/solution.py
@@ -381,18 +381,12 @@
     for hop in range(1, hops):
         own, other = send(own, ring), send(other, ring)
         swap, swop = send(own, pair), send(other, pair)
+        state = take(state, waiting, "first" if hop == 1 else "middle")
         arrived = [((hop, False, False), own), ((hop, True, False), swap)]
-        if hop == 1:
-            state = take(state, waiting, "first")
-            waiting = []
-        else:
-            state = take(state, waiting[:2])
-            waiting = waiting[2:]
-            if hop + 1 == hops:
-                waiting, arrived = waiting + arrived, []
-            state = take(state, waiting)
-            waiting = []
-        waiting += arrived + [((hop, False, True), other), ((hop, True, True), swop)]
+        waiting = [((hop, False, True), other), ((hop, True, True), swop)]
+        if hop + 1 == hops:
+            arrived, waiting = arrived + waiting[:1], waiting[1:]
+        state = take(state, arrived)
     own = send(own, ring)
     swapped = send(own, pair)
     state = take(state, waiting + [((hops, False, False), own)])

time: 40.4 us -> 40.8 us (level)
    pallas_call x7 -> x8, Pallas kernels: 9.71 us -> 10.1 us  [take(): pl.pallas_call(functools.partial(take_kernel, size, cache_rows, prompt_ro...]
  transfers between devices with their start and end apart: 15 -> 15, of which waited for: 7 -> 7; matrix products, arithmetic and copies ran while one was open for 0% -> 0% of each run, Pallas kernels for 25% -> 26%
where the time goes in v7:
time: 40.8 us; the launch traced here: 40.6 us
  starting transfers between devices  16.5 us (40%)
  Pallas kernels  12.9 us (32%)
  waiting for transfers between devices  9.15 us (22%)
  between operations  2.05 us (5%)
    ppermute x15, starting transfers between devices, send(): return lax.ppermute(block, 'ctx', pairs)  16.5 us
    pallas_call x8, Pallas kernels, take(): pl.pallas_call(functools.partial(take_kernel, size, cache_rows, prompt_ro...  10.1 us
    ppermute x15, waiting for transfers between devices, send(): return lax.ppermute(block, 'ctx', pairs)  9.15 us
    pallas_call x1, Pallas kernels, body(): pl.pallas_call(prep_kernel, out_shape=[shape(((KVH + 1) * HD, rows), BF16...  1.8 us
    pallas_call x1, Pallas kernels, body(): pl.pallas_call(pack_kernel, out_shape=shape((keys + HD, KVH * HD), BF16),...  1 us
  transfers between devices with their start and end apart: 15, of which 7 were waited for; matrix products, arithmetic and copies ran while one was open for 0% of the time, Pallas kernels for 26%

profile of v7, /device:TPU:0, one launch (start us, length us, event | category | flops | bytes accessed | tf_op | source)
XLA Modules:
  0.0 40.6 jit_solution(16762340411632275464)
XLA Ops:
  0.6 1.0 %shard_map.124.refs_5_ = bf16[256,512]{1,0:T(8,128)(2,1)S(1)} custom-call(bf16[64,512]{1,0:T(8,128)(2,1)} %ck_hbm.1, bf16[64,512]{1,0:T(8,128)(2,1)} %nk_hbm.1, bf16[64,512]{1,0:T(8,128)(2,1)} %cv_hbm.1, bf16[64,512]{1,0:T(8,128)(2,1)} %nv_hbm.1), custom_call_target="tpu_custom_call" | custom-call | tf_op jit(solution)/shard_map/pallas_call | solution.py:310
  1.6 0.6 %collective-permute-start = (bf16[256,512]{1,0:T(8,128)(2,1)S(1)}, bf16[256,512]{1,0:T(8,128)(2,1)S(1)}, u32[]{:S(2)}, u32[]{:S(2)}) collective-permute-start(bf16[256,512]{1,0:T(8,128)(2,1)S(1)} %shard_map.124.refs_5_), channel_id=1, source_target_pairs={{0,1},{1,0},{2,3},{3,2},{4,5},{5,4},{6,7},{7,6},{8,9},{9,8},{10,11... | collective-permute-start | bytes 786440 | tf_op jit(solution)/shard_map/ppermute | solution.py:308
  2.2 2.7 %collective-permute-start.1 = (bf16[256,512]{1,0:T(8,128)(2,1)S(1)}, bf16[256,512]{1,0:T(8,128)(2,1)S(1)}, u32[]{:S(2)}, u32[]{:S(2)}) collective-permute-start(bf16[256,512]{1,0:T(8,128)(2,1)S(1)} %shard_map.124.refs_5_), channel_id=1, source_target_pairs={{0,5},{1,2},{2,7},{3,0},{4,1},{5,8},{6,3},{7,10},{8,13},{9,4},{10,... | collective-permute-start | bytes 786440 | tf_op jit(solution)/shard_map/ppermute | solution.py:308
  4.9 0.0 collective-permute-done.refs_6_
  4.9 1.2 %collective-permute-start.3 = (bf16[256,512]{1,0:T(8,128)(2,1)S(1)}, bf16[256,512]{1,0:T(8,128)(2,1)S(1)}, u32[]{:S(2)}, u32[]{:S(2)}) collective-permute-start(bf16[256,512]{1,0:T(8,128)(2,1)S(1)} %collective-permute-done.refs_6_), channel_id=1, source_target_pairs={{0,5},{1,2},{2,7},{3,0},{4,1},{5,8},{6,3},{7,10},{8,13},{9,4},{10,... | collective-permute-start | bytes 786440 | tf_op jit(solution)/shard_map/ppermute | solution.py:308
  6.1 2.7 %collective-permute-done.1.refs_7_ = bf16[256,512]{1,0:T(8,128)(2,1)S(1)} collective-permute-done((bf16[256,512]{1,0:T(8,128)(2,1)S(1)}, bf16[256,512]{1,0:T(8,128)(2,1)S(1)}, u32[]{:S(2)}, u32[]{:S(2)}) %collective-permute-start.1) | collective-permute-done | bytes 262176 | tf_op jit(solution)/shard_map/ppermute | solution.py:308
  8.9 2.1 %collective-permute-start.5 = (bf16[256,512]{1,0:T(8,128)(2,1)S(1)}, bf16[256,512]{1,0:T(8,128)(2,1)S(1)}, u32[]{:S(2)}, u32[]{:S(2)}) collective-permute-start(bf16[256,512]{1,0:T(8,128)(2,1)S(1)} %collective-permute-done.1.refs_7_), channel_id=1, source_target_pairs={{0,5},{1,2},{2,7},{3,0},{4,1},{5,8},{6,3},{7,10},{8,13},{9,4},{10,... | collective-permute-start | bytes 786440 | tf_op jit(solution)/shard_map/ppermute | solution.py:308
  11.0 0.7 %collective-permute-done.3.refs_7_ = bf16[256,512]{1,0:T(8,128)(2,1)S(1)} collective-permute-done((bf16[256,512]{1,0:T(8,128)(2,1)S(1)}, bf16[256,512]{1,0:T(8,128)(2,1)S(1)}, u32[]{:S(2)}, u32[]{:S(2)}) %collective-permute-start.3) | collective-permute-done | bytes 262176 | tf_op jit(solution)/shard_map/ppermute | solution.py:308
  11.7 2.1 %collective-permute-start.7 = (bf16[256,512]{1,0:T(8,128)(2,1)S(1)}, bf16[256,512]{1,0:T(8,128)(2,1)S(1)}, u32[]{:S(2)}, u32[]{:S(2)}) collective-permute-start(bf16[256,512]{1,0:T(8,128)(2,1)S(1)} %collective-permute-done.3.refs_7_), channel_id=1, source_target_pairs={{0,5},{1,2},{2,7},{3,0},{4,1},{5,8},{6,3},{7,10},{8,13},{9,4},{10,... | collective-permute-start | bytes 786440 | tf_op jit(solution)/shard_map/ppermute | solution.py:308
  13.8 1.2 %collective-permute-done.5.refs_7_ = bf16[256,512]{1,0:T(8,128)(2,1)S(1)} collective-permute-done((bf16[256,512]{1,0:T(8,128)(2,1)S(1)}, bf16[256,512]{1,0:T(8,128)(2,1)S(1)}, u32[]{:S(2)}, u32[]{:S(2)}) %collective-permute-start.5) | collective-permute-done | bytes 262176 | tf_op jit(solution)/shard_map/ppermute | solution.py:308
  15.0 2.1 %collective-permute-start.9 = (bf16[256,512]{1,0:T(8,128)(2,1)S(1)}, bf16[256,512]{1,0:T(8,128)(2,1)S(1)}, u32[]{:S(2)}, u32[]{:S(2)}) collective-permute-start(bf16[256,512]{1,0:T(8,128)(2,1)S(1)} %collective-permute-done.5.refs_7_), channel_id=1, source_target_pairs={{0,5},{1,2},{2,7},{3,0},{4,1},{5,8},{6,3},{7,10},{8,13},{9,4},{10,... | collective-permute-start | bytes 786440 | tf_op jit(solution)/shard_map/ppermute | solution.py:308
  17.1 0.0 collective-permute-start.2
  17.1 0.5 %collective-permute-start.4 = (bf16[256,512]{1,0:T(8,128)(2,1)S(1)}, bf16[256,512]{1,0:T(8,128)(2,1)S(1)}, u32[]{:S(2)}, u32[]{:S(2)}) collective-permute-start(bf16[256,512]{1,0:T(8,128)(2,1)S(1)} %collective-permute-done.3.refs_7_), channel_id=1, source_target_pairs={{0,1},{1,0},{2,3},{3,2},{4,5},{5,4},{6,7},{7,6},{8,9},{9,8},{10,11... | collective-permute-start | bytes 786440 | tf_op jit(solution)/shard_map/ppermute | solution.py:308
  17.6 0.2 collective-permute-done.7.refs_7_
  17.8 2.1 %collective-permute-start.11 = (bf16[256,512]{1,0:T(8,128)(2,1)S(1)}, bf16[256,512]{1,0:T(8,128)(2,1)S(1)}, u32[]{:S(2)}, u32[]{:S(2)}) collective-permute-start(bf16[256,512]{1,0:T(8,128)(2,1)S(1)} %collective-permute-done.7.refs_7_), channel_id=1, source_target_pairs={{0,5},{1,2},{2,7},{3,0},{4,1},{5,8},{6,3},{7,10},{8,13},{9,4},{10,... | collective-permute-start | bytes 786440 | tf_op jit(solution)/shard_map/ppermute | solution.py:308
  19.9 1.2 %collective-permute-done.9.refs_7_ = bf16[256,512]{1,0:T(8,128)(2,1)S(1)} collective-permute-done((bf16[256,512]{1,0:T(8,128)(2,1)S(1)}, bf16[256,512]{1,0:T(8,128)(2,1)S(1)}, u32[]{:S(2)}, u32[]{:S(2)}) %collective-permute-start.9) | collective-permute-done | bytes 262176 | tf_op jit(solution)/shard_map/ppermute | solution.py:308
  21.1 2.1 %collective-permute-start.13 = (bf16[256,512]{1,0:T(8,128)(2,1)S(1)}, bf16[256,512]{1,0:T(8,128)(2,1)S(1)}, u32[]{:S(2)}, u32[]{:S(2)}) collective-permute-start(bf16[256,512]{1,0:T(8,128)(2,1)S(1)} %collective-permute-done.9.refs_7_), channel_id=1, source_target_pairs={{0,5},{1,2},{2,7},{3,0},{4,1},{5,8},{6,3},{7,10},{8,13},{9,4},{10,... | collective-permute-start | bytes 786440 | tf_op jit(solution)/shard_map/ppermute | solution.py:308
  23.1 0.0 collective-permute-start.6
  23.1 0.0 collective-permute-done.2.refs_8_
  23.2 0.5 %collective-permute-start.8 = (bf16[256,512]{1,0:T(8,128)(2,1)S(1)}, bf16[256,512]{1,0:T(8,128)(2,1)S(1)}, u32[]{:S(2)}, u32[]{:S(2)}) collective-permute-start(bf16[256,512]{1,0:T(8,128)(2,1)S(1)} %collective-permute-done.7.refs_7_), channel_id=1, source_target_pairs={{0,1},{1,0},{2,3},{3,2},{4,5},{5,4},{6,7},{7,6},{8,9},{9,8},{10,11... | collective-permute-start | bytes 786440 | tf_op jit(solution)/shard_map/ppermute | solution.py:308
  23.7 0.0 collective-permute-done.4.refs_8_
  23.7 0.1 collective-permute-start.10
  23.7 0.1 collective-permute-done.11.refs_9_
  23.9 0.3 collective-permute-start.12
  24.2 3.0 %collective-permute-done.13.refs_8_ = bf16[256,512]{1,0:T(8,128)(2,1)S(1)} collective-permute-done((bf16[256,512]{1,0:T(8,128)(2,1)S(1)}, bf16[256,512]{1,0:T(8,128)(2,1)S(1)}, u32[]{:S(2)}, u32[]{:S(2)}) %collective-permute-start.13) | collective-permute-done | bytes 262176 | tf_op jit(solution)/shard_map/ppermute | solution.py:308
  27.1 0.1 collective-permute-start.14
  28.6 1.8 %shard_map.123 = (bf16[640,512]{1,0:T(8,128)(2,1)S(1)}, bf16[512,64]{1,0:T(8,128)(2,1)S(1)}, f32[1,64]{1,0:T(1,128)S(1)}, f32[144,64]{1,0:T(8,128)S(1)}) custom-call(s32[2]{0:T(128)} %length_hbm.1, bf16[64,4096]{1,0:T(8,128)(2,1)} %query_hbm.1, bf16[2,4096]{1,0:T(2,128)(2,1)} %cont_hbm.1, bf16[2,128,512]{2,1,0:T(8,128)(2,1)} %key_hbm.1, ...), custom_call_target="tpu_custom_call" | custom-call | flops 67108864 | bytes 1048576 | tf_op jit(solution)/shard_map/pallas_call | solution.py:327
  30.4 1.0 %shard_map.125 = (f32[1,64]{1,0:T(1,128)S(1)}, f32[144,64]{1,0:T(8,128)S(1)}, f32[4,1,512]{2,1,0:T(1,128)S(1)}, f32[4,144,512]{2,1,0:T(8,128)S(1)}) custom-call(s32[2,128]{1,0:T(2,128)S(1)} %shard_map.122.refs_0_, bf16[640,512]{1,0:T(8,128)(2,1)S(1)} %get-tuple-element.34.refs_1_, ...), custom_call_target="tpu_custom_call", output_to_operand_aliasing={{0}: (3, {}), {1}: (4, {})} | custom-call | flops 134217728 | bytes 1048576 | tf_op jit(solution)/shard_map/pallas_call | solution.py:367
  31.4 1.2 %shard_map.126 = (f32[1,64]{1,0:T(1,128)S(1)}, f32[144,64]{1,0:T(8,128)S(1)}, f32[4,1,512]{2,1,0:T(1,128)S(1)}, f32[4,144,512]{2,1,0:T(8,128)S(1)}) custom-call(s32[2,128]{1,0:T(2,128)S(1)} %shard_map.122.refs_0_, bf16[640,512]{1,0:T(8,128)(2,1)S(1)} %get-tuple-element.34.refs_1_, ...), custom_call_target="tpu_custom_call", output_to_operand_aliasing={{0}: (3, {}), {1}: (4, {}), {2}: (5, {}), {3}: (6, {})} | custom-call | flops 134217728 | bytes 1048576 | tf_op jit(solution)/shard_map/pallas_call | solution.py:367
  32.6 1.2 %shard_map.127 = (f32[1,64]{1,0:T(1,128)S(1)}, f32[144,64]{1,0:T(8,128)S(1)}, f32[4,1,512]{2,1,0:T(1,128)S(1)}, f32[4,144,512]{2,1,0:T(8,128)S(1)}) custom-call(s32[2,128]{1,0:T(2,128)S(1)} %shard_map.122.refs_0_, bf16[640,512]{1,0:T(8,128)(2,1)S(1)} %get-tuple-element.34.refs_1_, ...), custom_call_target="tpu_custom_call", output_to_operand_aliasing={{0}: (3, {}), {1}: (4, {}), {2}: (5, {}), {3}: (6, {})} | custom-call | flops 134217728 | bytes 1048576 | tf_op jit(solution)/shard_map/pallas_call | solution.py:367
  33.8 0.0 collective-permute-done.6.refs_8_
  33.8 1.2 %shard_map.128 = (f32[1,64]{1,0:T(1,128)S(1)}, f32[144,64]{1,0:T(8,128)S(1)}, f32[4,1,512]{2,1,0:T(1,128)S(1)}, f32[4,144,512]{2,1,0:T(8,128)S(1)}) custom-call(s32[2,128]{1,0:T(2,128)S(1)} %shard_map.122.refs_0_, bf16[640,512]{1,0:T(8,128)(2,1)S(1)} %get-tuple-element.34.refs_1_, ...), custom_call_target="tpu_custom_call", output_to_operand_aliasing={{0}: (3, {}), {1}: (4, {}), {2}: (5, {}), {3}: (6, {})} | custom-call | flops 134217728 | bytes 1048576 | tf_op jit(solution)/shard_map/pallas_call | solution.py:367
  34.9 0.0 collective-permute-done.8.refs_8_
  35.0 1.2 %shard_map.129 = (f32[1,64]{1,0:T(1,128)S(1)}, f32[144,64]{1,0:T(8,128)S(1)}, f32[4,1,512]{2,1,0:T(1,128)S(1)}, f32[4,144,512]{2,1,0:T(8,128)S(1)}) custom-call(s32[2,128]{1,0:T(2,128)S(1)} %shard_map.122.refs_0_, bf16[640,512]{1,0:T(8,128)(2,1)S(1)} %get-tuple-element.34.refs_1_, ...), custom_call_target="tpu_custom_call", output_to_operand_aliasing={{0}: (3, {}), {1}: (4, {}), {2}: (5, {}), {3}: (6, {})} | custom-call | flops 134217728 | bytes 1048576 | tf_op jit(solution)/shard_map/pallas_call | solution.py:367
  36.1 0.0 collective-permute-done.10.refs_8_
  36.1 1.7 %shard_map.130 = (f32[1,64]{1,0:T(1,128)S(1)}, f32[144,64]{1,0:T(8,128)S(1)}, f32[4,1,512]{2,1,0:T(1,128)S(1)}, f32[4,144,512]{2,1,0:T(8,128)S(1)}) custom-call(s32[2,128]{1,0:T(2,128)S(1)} %shard_map.122.refs_0_, bf16[640,512]{1,0:T(8,128)(2,1)S(1)} %get-tuple-element.34.refs_1_, ...), custom_call_target="tpu_custom_call", output_to_operand_aliasing={{0}: (3, {}), {1}: (4, {}), {2}: (5, {}), {3}: (6, {})} | custom-call | flops 201326592 | bytes 1048576 | tf_op jit(solution)/shard_map/pallas_call | solution.py:367
  37.9 0.0 collective-permute-done.12.refs_7_
  37.9 1.2 %shard_map.131 = (f32[1,64]{1,0:T(1,128)S(1)}, f32[144,64]{1,0:T(8,128)S(1)}, f32[4,1,512]{2,1,0:T(1,128)S(1)}, f32[4,144,512]{2,1,0:T(8,128)S(1)}) custom-call(s32[2,128]{1,0:T(2,128)S(1)} %shard_map.122.refs_0_, bf16[640,512]{1,0:T(8,128)(2,1)S(1)} %get-tuple-element.34.refs_1_, ...), custom_call_target="tpu_custom_call", output_to_operand_aliasing={{0}: (3, {}), {1}: (4, {}), {2}: (5, {}), {3}: (6, {})} | custom-call | flops 134217728 | bytes 1048576 | tf_op jit(solution)/shard_map/pallas_call | solution.py:367
  39.1 0.0 collective-permute-done.14.refs_7_
  39.1 1.5 %shard_map.132 = (bf16[64,4096]{1,0:T(8,128)(2,1)}, bf16[2,4096]{1,0:T(2,128)(2,1)}) custom-call(s32[2,128]{1,0:T(2,128)S(1)} %shard_map.122.refs_0_, bf16[640,512]{1,0:T(8,128)(2,1)S(1)} %get-tuple-element.34.refs_1_, bf16[512,64]{1,0:T(8,128)(2,1)S(1)} %get-tuple-element.35.refs_2_, f32[1,64]{1,0:T(1,128)S(1)} %get-tuple-element.62.refs_3_, ...), custom_call_target="tpu_custom_call" | custom-call | flops 67108864 | bytes 1048576 | tf_op jit(solution)/shard_map/pallas_call | solution.py:367
  (1 shorter events, 0.0 us)
Async XLA Ops:
  1.6 3.2 %collective-permute-start = (bf16[256,512]{1,0:T(8,128)(2,1)S(1)}, bf16[256,512]{1,0:T(8,128)(2,1)S(1)}, u32[]{:S(2)}, u32[]{:S(2)}) collective-permute-start(bf16[256,512]{1,0:T(8,128)(2,1)S(1)} %shard_map.124.refs_5_), channel_id=1, source_target_pairs={{0,1},{1,0},{2,3},{3,2},{4,5},{5,4},{6,7},{7,6},{8,9},{9,8},{10,11... | collective-permute-start | bytes 786440 | tf_op jit(solution)/shard_map/ppermute | solution.py:308
  2.2 6.7 %collective-permute-start.1 = (bf16[256,512]{1,0:T(8,128)(2,1)S(1)}, bf16[256,512]{1,0:T(8,128)(2,1)S(1)}, u32[]{:S(2)}, u32[]{:S(2)}) collective-permute-start(bf16[256,512]{1,0:T(8,128)(2,1)S(1)} %shard_map.124.refs_5_), channel_id=1, source_target_pairs={{0,5},{1,2},{2,7},{3,0},{4,1},{5,8},{6,3},{7,10},{8,13},{9,4},{10,... | collective-permute-start | bytes 786440 | tf_op jit(solution)/shard_map/ppermute | solution.py:308
  4.9 6.8 %collective-permute-start.3 = (bf16[256,512]{1,0:T(8,128)(2,1)S(1)}, bf16[256,512]{1,0:T(8,128)(2,1)S(1)}, u32[]{:S(2)}, u32[]{:S(2)}) collective-permute-start(bf16[256,512]{1,0:T(8,128)(2,1)S(1)} %collective-permute-done.refs_6_), channel_id=1, source_target_pairs={{0,5},{1,2},{2,7},{3,0},{4,1},{5,8},{6,3},{7,10},{8,13},{9,4},{10,... | collective-permute-start | bytes 786440 | tf_op jit(solution)/shard_map/ppermute | solution.py:308
  8.9 6.1 %collective-permute-start.5 = (bf16[256,512]{1,0:T(8,128)(2,1)S(1)}, bf16[256,512]{1,0:T(8,128)(2,1)S(1)}, u32[]{:S(2)}, u32[]{:S(2)}) collective-permute-start(bf16[256,512]{1,0:T(8,128)(2,1)S(1)} %collective-permute-done.1.refs_7_), channel_id=1, source_target_pairs={{0,5},{1,2},{2,7},{3,0},{4,1},{5,8},{6,3},{7,10},{8,13},{9,4},{10,... | collective-permute-start | bytes 786440 | tf_op jit(solution)/shard_map/ppermute | solution.py:308
  11.7 6.1 %collective-permute-start.7 = (bf16[256,512]{1,0:T(8,128)(2,1)S(1)}, bf16[256,512]{1,0:T(8,128)(2,1)S(1)}, u32[]{:S(2)}, u32[]{:S(2)}) collective-permute-start(bf16[256,512]{1,0:T(8,128)(2,1)S(1)} %collective-permute-done.3.refs_7_), channel_id=1, source_target_pairs={{0,5},{1,2},{2,7},{3,0},{4,1},{5,8},{6,3},{7,10},{8,13},{9,4},{10,... | collective-permute-start | bytes 786440 | tf_op jit(solution)/shard_map/ppermute | solution.py:308
  15.0 6.1 %collective-permute-start.9 = (bf16[256,512]{1,0:T(8,128)(2,1)S(1)}, bf16[256,512]{1,0:T(8,128)(2,1)S(1)}, u32[]{:S(2)}, u32[]{:S(2)}) collective-permute-start(bf16[256,512]{1,0:T(8,128)(2,1)S(1)} %collective-permute-done.5.refs_7_), channel_id=1, source_target_pairs={{0,5},{1,2},{2,7},{3,0},{4,1},{5,8},{6,3},{7,10},{8,13},{9,4},{10,... | collective-permute-start | bytes 786440 | tf_op jit(solution)/shard_map/ppermute | solution.py:308
  17.1 6.1 %collective-permute-start.2 = (bf16[256,512]{1,0:T(8,128)(2,1)S(1)}, bf16[256,512]{1,0:T(8,128)(2,1)S(1)}, u32[]{:S(2)}, u32[]{:S(2)}) collective-permute-start(bf16[256,512]{1,0:T(8,128)(2,1)S(1)} %collective-permute-done.1.refs_7_), channel_id=1, source_target_pairs={{0,1},{1,0},{2,3},{3,2},{4,5},{5,4},{6,7},{7,6},{8,9},{9,8},{10,11... | collective-permute-start | bytes 786440 | tf_op jit(solution)/shard_map/ppermute | solution.py:308
  17.1 6.6 %collective-permute-start.4 = (bf16[256,512]{1,0:T(8,128)(2,1)S(1)}, bf16[256,512]{1,0:T(8,128)(2,1)S(1)}, u32[]{:S(2)}, u32[]{:S(2)}) collective-permute-start(bf16[256,512]{1,0:T(8,128)(2,1)S(1)} %collective-permute-done.3.refs_7_), channel_id=1, source_target_pairs={{0,1},{1,0},{2,3},{3,2},{4,5},{5,4},{6,7},{7,6},{8,9},{9,8},{10,11... | collective-permute-start | bytes 786440 | tf_op jit(solution)/shard_map/ppermute | solution.py:308
  17.8 6.1 %collective-permute-start.11 = (bf16[256,512]{1,0:T(8,128)(2,1)S(1)}, bf16[256,512]{1,0:T(8,128)(2,1)S(1)}, u32[]{:S(2)}, u32[]{:S(2)}) collective-permute-start(bf16[256,512]{1,0:T(8,128)(2,1)S(1)} %collective-permute-done.7.refs_7_), channel_id=1, source_target_pairs={{0,5},{1,2},{2,7},{3,0},{4,1},{5,8},{6,3},{7,10},{8,13},{9,4},{10,... | collective-permute-start | bytes 786440 | tf_op jit(solution)/shard_map/ppermute | solution.py:308
  21.1 6.1 %collective-permute-start.13 = (bf16[256,512]{1,0:T(8,128)(2,1)S(1)}, bf16[256,512]{1,0:T(8,128)(2,1)S(1)}, u32[]{:S(2)}, u32[]{:S(2)}) collective-permute-start(bf16[256,512]{1,0:T(8,128)(2,1)S(1)} %collective-permute-done.9.refs_7_), channel_id=1, source_target_pairs={{0,5},{1,2},{2,7},{3,0},{4,1},{5,8},{6,3},{7,10},{8,13},{9,4},{10,... | collective-permute-start | bytes 786440 | tf_op jit(solution)/shard_map/ppermute | solution.py:308
  23.1 10.6 %collective-permute-start.6 = (bf16[256,512]{1,0:T(8,128)(2,1)S(1)}, bf16[256,512]{1,0:T(8,128)(2,1)S(1)}, u32[]{:S(2)}, u32[]{:S(2)}) collective-permute-start(bf16[256,512]{1,0:T(8,128)(2,1)S(1)} %collective-permute-done.5.refs_7_), channel_id=1, source_target_pairs={{0,1},{1,0},{2,3},{3,2},{4,5},{5,4},{6,7},{7,6},{8,9},{9,8},{10,11... | collective-permute-start | bytes 786440 | tf_op jit(solution)/shard_map/ppermute | solution.py:308
  23.2 11.8 %collective-permute-start.8 = (bf16[256,512]{1,0:T(8,128)(2,1)S(1)}, bf16[256,512]{1,0:T(8,128)(2,1)S(1)}, u32[]{:S(2)}, u32[]{:S(2)}) collective-permute-start(bf16[256,512]{1,0:T(8,128)(2,1)S(1)} %collective-permute-done.7.refs_7_), channel_id=1, source_target_pairs={{0,1},{1,0},{2,3},{3,2},{4,5},{5,4},{6,7},{7,6},{8,9},{9,8},{10,11... | collective-permute-start | bytes 786440 | tf_op jit(solution)/shard_map/ppermute | solution.py:308
  23.7 12.5 %collective-permute-start.10 = (bf16[256,512]{1,0:T(8,128)(2,1)S(1)}, bf16[256,512]{1,0:T(8,128)(2,1)S(1)}, u32[]{:S(2)}, u32[]{:S(2)}) collective-permute-start(bf16[256,512]{1,0:T(8,128)(2,1)S(1)} %collective-permute-done.9.refs_7_), channel_id=1, source_target_pairs={{0,1},{1,0},{2,3},{3,2},{4,5},{5,4},{6,7},{7,6},{8,9},{9,8},{10,11... | collective-permute-start | bytes 786440 | tf_op jit(solution)/shard_map/ppermute | solution.py:308
  23.9 14.0 %collective-permute-start.12 = (bf16[256,512]{1,0:T(8,128)(2,1)S(1)}, bf16[256,512]{1,0:T(8,128)(2,1)S(1)}, u32[]{:S(2)}, u32[]{:S(2)}) collective-permute-start(bf16[256,512]{1,0:T(8,128)(2,1)S(1)} %collective-permute-done.11.refs_9_), channel_id=1, source_target_pairs={{0,1},{1,0},{2,3},{3,2},{4,5},{5,4},{6,7},{7,6},{8,9},{9,8},{10,11... | collective-permute-start | bytes 786440 | tf_op jit(solution)/shard_map/ppermute | solution.py:308
  27.1 11.9 %collective-permute-start.14 = (bf16[256,512]{1,0:T(8,128)(2,1)S(1)}, bf16[256,512]{1,0:T(8,128)(2,1)S(1)}, u32[]{:S(2)}, u32[]{:S(2)}) collective-permute-start(bf16[256,512]{1,0:T(8,128)(2,1)S(1)} %collective-permute-done.13.refs_8_), channel_id=1, source_target_pairs={{0,1},{1,0},{2,3},{3,2},{4,5},{5,4},{6,7},{7,6},{8,9},{9,8},{10,11... | collective-permute-start | bytes 786440 | tf_op jit(solution)/shard_map/ppermute | solution.py:308

commit v8 on v7

--- a/solution.py
+++ b/solution.py
@@ -119,8 +119,14 @@
         pltpu.make_async_copy(source, target, sems.at[index])
         for index, (source, target) in enumerate(
             [
-                (query_hbm, query_ref), (cont_hbm, cont_ref), (key_hbm, key_ref),
-                (value_hbm, value_ref), (length_hbm, length_ref),
+                *[
+                    (query_hbm.at[:, cols], query_ref.at[:, cols])
+                    for cols in (
+                        slice(g * GROUP * HD, (g + 1) * GROUP * HD) for g in range(KVH)
+                    )
+                ],
+                (cont_hbm, cont_ref), (key_hbm, key_ref), (value_hbm, value_ref),
+                (length_hbm, length_ref),
             ]
         )
     ]
@@ -132,11 +138,11 @@
     dot = functools.partial(jnp.dot, preferred_element_type=F32)
     q_ref[KVH * HD :] = row_features(GROUP * prompt_rows, prompt_rows)
     heads = [slice(head * HD, (head + 1) * HD) for head in range(KVH * GROUP)]
-    for load in loads[:2]:
-        load.wait()
     for g in range(KVH):
+        loads[g].wait()
         q = jnp.concatenate([query_ref[:, head] for head in heads[g * GROUP : (g + 1) * GROUP]], axis=0)
         q_ref[g * HD : (g + 1) * HD] = q.T
+    loads[KVH].wait()
     cont = cont_ref[...].astype(F32)
     cont_q = jnp.concatenate(
         [
@@ -151,7 +157,7 @@
     cont_q = jnp.concatenate([jnp.where(column == g, cont_q, 0.0) for g in range(KVH)], axis=0)
     cont_q = cont_q.astype(BF16)
     cont_q_ref[...] = cont_q
-    for load in loads[2:]:
+    for load in loads[KVH + 1 :]:
         load.wait()
     scores = [dot(key_ref[c], cont_q) for c in range(cont_count)]
     v = value_ref[...].reshape(cont_count * suffix_rows, KVH * HD).T
@@ -338,7 +344,7 @@
             pltpu.VMEM(cont_queries.shape, BF16),
             pltpu.VMEM(suffix_keys.shape, BF16),
             pltpu.VMEM(suffix_values.shape, BF16),
-            pltpu.SemaphoreType.DMA((5,)),
+            pltpu.SemaphoreType.DMA((KVH + 4,)),
         ],
         compiler_params=params,
         cost_estimate=cost(rows, keys),

time: 40.8 us -> 40.9 us (level)
  no operation moved by 1% of the time
where the time goes in v8:
time: 40.9 us; the launch traced here: 40.7 us
  starting transfers between devices  16.5 us (40%)
  Pallas kernels  13 us (32%)
  waiting for transfers between devices  9.15 us (22%)
  between operations  2.05 us (5%)
    ppermute x15, starting transfers between devices, send(): return lax.ppermute(block, 'ctx', pairs)  16.5 us
    pallas_call x8, Pallas kernels, take(): pl.pallas_call(functools.partial(take_kernel, size, cache_rows, prompt_ro...  10.1 us
    ppermute x15, waiting for transfers between devices, send(): return lax.ppermute(block, 'ctx', pairs)  9.15 us
    pallas_call x1, Pallas kernels, body(): pl.pallas_call(prep_kernel, out_shape=[shape(((KVH + 1) * HD, rows), BF16...  1.94 us
    pallas_call x1, Pallas kernels, body(): pl.pallas_call(pack_kernel, out_shape=shape((keys + HD, KVH * HD), BF16),...  1 us
  transfers between devices with their start and end apart: 15, of which 7 were waited for; matrix products, arithmetic and copies ran while one was open for 0% of the time, Pallas kernels for 26%

profile of v8, /device:TPU:0, one launch (start us, length us, event | category | flops | bytes accessed | tf_op | source)
XLA Modules:
  0.0 40.7 jit_solution(15223701213194767031)
XLA Ops:
  0.6 1.0 %shard_map.124.refs_5_ = bf16[256,512]{1,0:T(8,128)(2,1)S(1)} custom-call(bf16[64,512]{1,0:T(8,128)(2,1)} %ck_hbm.1, bf16[64,512]{1,0:T(8,128)(2,1)} %nk_hbm.1, bf16[64,512]{1,0:T(8,128)(2,1)} %cv_hbm.1, bf16[64,512]{1,0:T(8,128)(2,1)} %nv_hbm.1), custom_call_target="tpu_custom_call" | custom-call | tf_op jit(solution)/shard_map/pallas_call | solution.py:316
  1.6 0.6 %collective-permute-start = (bf16[256,512]{1,0:T(8,128)(2,1)S(1)}, bf16[256,512]{1,0:T(8,128)(2,1)S(1)}, u32[]{:S(2)}, u32[]{:S(2)}) collective-permute-start(bf16[256,512]{1,0:T(8,128)(2,1)S(1)} %shard_map.124.refs_5_), channel_id=1, source_target_pairs={{0,1},{1,0},{2,3},{3,2},{4,5},{5,4},{6,7},{7,6},{8,9},{9,8},{10,11... | collective-permute-start | bytes 786440 | tf_op jit(solution)/shard_map/ppermute | solution.py:314
  2.2 2.7 %collective-permute-start.1 = (bf16[256,512]{1,0:T(8,128)(2,1)S(1)}, bf16[256,512]{1,0:T(8,128)(2,1)S(1)}, u32[]{:S(2)}, u32[]{:S(2)}) collective-permute-start(bf16[256,512]{1,0:T(8,128)(2,1)S(1)} %shard_map.124.refs_5_), channel_id=1, source_target_pairs={{0,5},{1,2},{2,7},{3,0},{4,1},{5,8},{6,3},{7,10},{8,13},{9,4},{10,... | collective-permute-start | bytes 786440 | tf_op jit(solution)/shard_map/ppermute | solution.py:314
  4.9 0.0 collective-permute-done.refs_6_
  4.9 1.2 %collective-permute-start.3 = (bf16[256,512]{1,0:T(8,128)(2,1)S(1)}, bf16[256,512]{1,0:T(8,128)(2,1)S(1)}, u32[]{:S(2)}, u32[]{:S(2)}) collective-permute-start(bf16[256,512]{1,0:T(8,128)(2,1)S(1)} %collective-permute-done.refs_6_), channel_id=1, source_target_pairs={{0,5},{1,2},{2,7},{3,0},{4,1},{5,8},{6,3},{7,10},{8,13},{9,4},{10,... | collective-permute-start | bytes 786440 | tf_op jit(solution)/shard_map/ppermute | solution.py:314
  6.1 2.7 %collective-permute-done.1.refs_7_ = bf16[256,512]{1,0:T(8,128)(2,1)S(1)} collective-permute-done((bf16[256,512]{1,0:T(8,128)(2,1)S(1)}, bf16[256,512]{1,0:T(8,128)(2,1)S(1)}, u32[]{:S(2)}, u32[]{:S(2)}) %collective-permute-start.1) | collective-permute-done | bytes 262176 | tf_op jit(solution)/shard_map/ppermute | solution.py:314
  8.9 2.1 %collective-permute-start.5 = (bf16[256,512]{1,0:T(8,128)(2,1)S(1)}, bf16[256,512]{1,0:T(8,128)(2,1)S(1)}, u32[]{:S(2)}, u32[]{:S(2)}) collective-permute-start(bf16[256,512]{1,0:T(8,128)(2,1)S(1)} %collective-permute-done.1.refs_7_), channel_id=1, source_target_pairs={{0,5},{1,2},{2,7},{3,0},{4,1},{5,8},{6,3},{7,10},{8,13},{9,4},{10,... | collective-permute-start | bytes 786440 | tf_op jit(solution)/shard_map/ppermute | solution.py:314
  11.0 0.7 %collective-permute-done.3.refs_7_ = bf16[256,512]{1,0:T(8,128)(2,1)S(1)} collective-permute-done((bf16[256,512]{1,0:T(8,128)(2,1)S(1)}, bf16[256,512]{1,0:T(8,128)(2,1)S(1)}, u32[]{:S(2)}, u32[]{:S(2)}) %collective-permute-start.3) | collective-permute-done | bytes 262176 | tf_op jit(solution)/shard_map/ppermute | solution.py:314
  11.7 2.1 %collective-permute-start.7 = (bf16[256,512]{1,0:T(8,128)(2,1)S(1)}, bf16[256,512]{1,0:T(8,128)(2,1)S(1)}, u32[]{:S(2)}, u32[]{:S(2)}) collective-permute-start(bf16[256,512]{1,0:T(8,128)(2,1)S(1)} %collective-permute-done.3.refs_7_), channel_id=1, source_target_pairs={{0,5},{1,2},{2,7},{3,0},{4,1},{5,8},{6,3},{7,10},{8,13},{9,4},{10,... | collective-permute-start | bytes 786440 | tf_op jit(solution)/shard_map/ppermute | solution.py:314
  13.8 1.2 %collective-permute-done.5.refs_7_ = bf16[256,512]{1,0:T(8,128)(2,1)S(1)} collective-permute-done((bf16[256,512]{1,0:T(8,128)(2,1)S(1)}, bf16[256,512]{1,0:T(8,128)(2,1)S(1)}, u32[]{:S(2)}, u32[]{:S(2)}) %collective-permute-start.5) | collective-permute-done | bytes 262176 | tf_op jit(solution)/shard_map/ppermute | solution.py:314
  15.0 2.1 %collective-permute-start.9 = (bf16[256,512]{1,0:T(8,128)(2,1)S(1)}, bf16[256,512]{1,0:T(8,128)(2,1)S(1)}, u32[]{:S(2)}, u32[]{:S(2)}) collective-permute-start(bf16[256,512]{1,0:T(8,128)(2,1)S(1)} %collective-permute-done.5.refs_7_), channel_id=1, source_target_pairs={{0,5},{1,2},{2,7},{3,0},{4,1},{5,8},{6,3},{7,10},{8,13},{9,4},{10,... | collective-permute-start | bytes 786440 | tf_op jit(solution)/shard_map/ppermute | solution.py:314
  17.1 0.0 collective-permute-start.2
  17.1 0.5 %collective-permute-start.4 = (bf16[256,512]{1,0:T(8,128)(2,1)S(1)}, bf16[256,512]{1,0:T(8,128)(2,1)S(1)}, u32[]{:S(2)}, u32[]{:S(2)}) collective-permute-start(bf16[256,512]{1,0:T(8,128)(2,1)S(1)} %collective-permute-done.3.refs_7_), channel_id=1, source_target_pairs={{0,1},{1,0},{2,3},{3,2},{4,5},{5,4},{6,7},{7,6},{8,9},{9,8},{10,11... | collective-permute-start | bytes 786440 | tf_op jit(solution)/shard_map/ppermute | solution.py:314
  17.6 0.2 collective-permute-done.7.refs_7_
  17.8 2.1 %collective-permute-start.11 = (bf16[256,512]{1,0:T(8,128)(2,1)S(1)}, bf16[256,512]{1,0:T(8,128)(2,1)S(1)}, u32[]{:S(2)}, u32[]{:S(2)}) collective-permute-start(bf16[256,512]{1,0:T(8,128)(2,1)S(1)} %collective-permute-done.7.refs_7_), channel_id=1, source_target_pairs={{0,5},{1,2},{2,7},{3,0},{4,1},{5,8},{6,3},{7,10},{8,13},{9,4},{10,... | collective-permute-start | bytes 786440 | tf_op jit(solution)/shard_map/ppermute | solution.py:314
  19.9 1.2 %collective-permute-done.9.refs_7_ = bf16[256,512]{1,0:T(8,128)(2,1)S(1)} collective-permute-done((bf16[256,512]{1,0:T(8,128)(2,1)S(1)}, bf16[256,512]{1,0:T(8,128)(2,1)S(1)}, u32[]{:S(2)}, u32[]{:S(2)}) %collective-permute-start.9) | collective-permute-done | bytes 262176 | tf_op jit(solution)/shard_map/ppermute | solution.py:314
  21.1 2.1 %collective-permute-start.13 = (bf16[256,512]{1,0:T(8,128)(2,1)S(1)}, bf16[256,512]{1,0:T(8,128)(2,1)S(1)}, u32[]{:S(2)}, u32[]{:S(2)}) collective-permute-start(bf16[256,512]{1,0:T(8,128)(2,1)S(1)} %collective-permute-done.9.refs_7_), channel_id=1, source_target_pairs={{0,5},{1,2},{2,7},{3,0},{4,1},{5,8},{6,3},{7,10},{8,13},{9,4},{10,... | collective-permute-start | bytes 786440 | tf_op jit(solution)/shard_map/ppermute | solution.py:314
  23.1 0.0 collective-permute-start.6
  23.1 0.0 collective-permute-done.2.refs_8_
  23.2 0.5 %collective-permute-start.8 = (bf16[256,512]{1,0:T(8,128)(2,1)S(1)}, bf16[256,512]{1,0:T(8,128)(2,1)S(1)}, u32[]{:S(2)}, u32[]{:S(2)}) collective-permute-start(bf16[256,512]{1,0:T(8,128)(2,1)S(1)} %collective-permute-done.7.refs_7_), channel_id=1, source_target_pairs={{0,1},{1,0},{2,3},{3,2},{4,5},{5,4},{6,7},{7,6},{8,9},{9,8},{10,11... | collective-permute-start | bytes 786440 | tf_op jit(solution)/shard_map/ppermute | solution.py:314
  23.7 0.0 collective-permute-done.4.refs_8_
  23.7 0.1 collective-permute-start.10
  23.7 0.1 collective-permute-done.11.refs_9_
  23.9 0.3 collective-permute-start.12
  24.2 3.0 %collective-permute-done.13.refs_8_ = bf16[256,512]{1,0:T(8,128)(2,1)S(1)} collective-permute-done((bf16[256,512]{1,0:T(8,128)(2,1)S(1)}, bf16[256,512]{1,0:T(8,128)(2,1)S(1)}, u32[]{:S(2)}, u32[]{:S(2)}) %collective-permute-start.13) | collective-permute-done | bytes 262176 | tf_op jit(solution)/shard_map/ppermute | solution.py:314
  27.1 0.1 collective-permute-start.14
  28.6 1.9 %shard_map.123 = (bf16[640,512]{1,0:T(8,128)(2,1)S(1)}, bf16[512,64]{1,0:T(8,128)(2,1)S(1)}, f32[1,64]{1,0:T(1,128)S(1)}, f32[144,64]{1,0:T(8,128)S(1)}) custom-call(s32[2]{0:T(128)} %length_hbm.1, bf16[64,4096]{1,0:T(8,128)(2,1)} %query_hbm.1, bf16[2,4096]{1,0:T(2,128)(2,1)} %cont_hbm.1, bf16[2,128,512]{2,1,0:T(8,128)(2,1)} %key_hbm.1, ...), custom_call_target="tpu_custom_call" | custom-call | flops 67108864 | bytes 1048576 | tf_op jit(solution)/shard_map/pallas_call | solution.py:333
  30.5 1.0 %shard_map.125 = (f32[1,64]{1,0:T(1,128)S(1)}, f32[144,64]{1,0:T(8,128)S(1)}, f32[4,1,512]{2,1,0:T(1,128)S(1)}, f32[4,144,512]{2,1,0:T(8,128)S(1)}) custom-call(s32[2,128]{1,0:T(2,128)S(1)} %shard_map.122.refs_0_, bf16[640,512]{1,0:T(8,128)(2,1)S(1)} %get-tuple-element.34.refs_1_, ...), custom_call_target="tpu_custom_call", output_to_operand_aliasing={{0}: (3, {}), {1}: (4, {})} | custom-call | flops 134217728 | bytes 1048576 | tf_op jit(solution)/shard_map/pallas_call | solution.py:373
  31.6 1.2 %shard_map.126 = (f32[1,64]{1,0:T(1,128)S(1)}, f32[144,64]{1,0:T(8,128)S(1)}, f32[4,1,512]{2,1,0:T(1,128)S(1)}, f32[4,144,512]{2,1,0:T(8,128)S(1)}) custom-call(s32[2,128]{1,0:T(2,128)S(1)} %shard_map.122.refs_0_, bf16[640,512]{1,0:T(8,128)(2,1)S(1)} %get-tuple-element.34.refs_1_, ...), custom_call_target="tpu_custom_call", output_to_operand_aliasing={{0}: (3, {}), {1}: (4, {}), {2}: (5, {}), {3}: (6, {})} | custom-call | flops 134217728 | bytes 1048576 | tf_op jit(solution)/shard_map/pallas_call | solution.py:373
  32.7 1.2 %shard_map.127 = (f32[1,64]{1,0:T(1,128)S(1)}, f32[144,64]{1,0:T(8,128)S(1)}, f32[4,1,512]{2,1,0:T(1,128)S(1)}, f32[4,144,512]{2,1,0:T(8,128)S(1)}) custom-call(s32[2,128]{1,0:T(2,128)S(1)} %shard_map.122.refs_0_, bf16[640,512]{1,0:T(8,128)(2,1)S(1)} %get-tuple-element.34.refs_1_, ...), custom_call_target="tpu_custom_call", output_to_operand_aliasing={{0}: (3, {}), {1}: (4, {}), {2}: (5, {}), {3}: (6, {})} | custom-call | flops 134217728 | bytes 1048576 | tf_op jit(solution)/shard_map/pallas_call | solution.py:373
  33.9 0.0 collective-permute-done.6.refs_8_
  33.9 1.2 %shard_map.128 = (f32[1,64]{1,0:T(1,128)S(1)}, f32[144,64]{1,0:T(8,128)S(1)}, f32[4,1,512]{2,1,0:T(1,128)S(1)}, f32[4,144,512]{2,1,0:T(8,128)S(1)}) custom-call(s32[2,128]{1,0:T(2,128)S(1)} %shard_map.122.refs_0_, bf16[640,512]{1,0:T(8,128)(2,1)S(1)} %get-tuple-element.34.refs_1_, ...), custom_call_target="tpu_custom_call", output_to_operand_aliasing={{0}: (3, {}), {1}: (4, {}), {2}: (5, {}), {3}: (6, {})} | custom-call | flops 134217728 | bytes 1048576 | tf_op jit(solution)/shard_map/pallas_call | solution.py:373
  35.1 0.0 collective-permute-done.8.refs_8_
  35.1 1.2 %shard_map.129 = (f32[1,64]{1,0:T(1,128)S(1)}, f32[144,64]{1,0:T(8,128)S(1)}, f32[4,1,512]{2,1,0:T(1,128)S(1)}, f32[4,144,512]{2,1,0:T(8,128)S(1)}) custom-call(s32[2,128]{1,0:T(2,128)S(1)} %shard_map.122.refs_0_, bf16[640,512]{1,0:T(8,128)(2,1)S(1)} %get-tuple-element.34.refs_1_, ...), custom_call_target="tpu_custom_call", output_to_operand_aliasing={{0}: (3, {}), {1}: (4, {}), {2}: (5, {}), {3}: (6, {})} | custom-call | flops 134217728 | bytes 1048576 | tf_op jit(solution)/shard_map/pallas_call | solution.py:373
  36.3 0.0 collective-permute-done.10.refs_8_
  36.3 1.7 %shard_map.130 = (f32[1,64]{1,0:T(1,128)S(1)}, f32[144,64]{1,0:T(8,128)S(1)}, f32[4,1,512]{2,1,0:T(1,128)S(1)}, f32[4,144,512]{2,1,0:T(8,128)S(1)}) custom-call(s32[2,128]{1,0:T(2,128)S(1)} %shard_map.122.refs_0_, bf16[640,512]{1,0:T(8,128)(2,1)S(1)} %get-tuple-element.34.refs_1_, ...), custom_call_target="tpu_custom_call", output_to_operand_aliasing={{0}: (3, {}), {1}: (4, {}), {2}: (5, {}), {3}: (6, {})} | custom-call | flops 201326592 | bytes 1048576 | tf_op jit(solution)/shard_map/pallas_call | solution.py:373
  38.0 0.0 collective-permute-done.12.refs_7_
  38.0 1.2 %shard_map.131 = (f32[1,64]{1,0:T(1,128)S(1)}, f32[144,64]{1,0:T(8,128)S(1)}, f32[4,1,512]{2,1,0:T(1,128)S(1)}, f32[4,144,512]{2,1,0:T(8,128)S(1)}) custom-call(s32[2,128]{1,0:T(2,128)S(1)} %shard_map.122.refs_0_, bf16[640,512]{1,0:T(8,128)(2,1)S(1)} %get-tuple-element.34.refs_1_, ...), custom_call_target="tpu_custom_call", output_to_operand_aliasing={{0}: (3, {}), {1}: (4, {}), {2}: (5, {}), {3}: (6, {})} | custom-call | flops 134217728 | bytes 1048576 | tf_op jit(solution)/shard_map/pallas_call | solution.py:373
  39.2 0.0 collective-permute-done.14.refs_7_
  39.2 1.5 %shard_map.132 = (bf16[64,4096]{1,0:T(8,128)(2,1)}, bf16[2,4096]{1,0:T(2,128)(2,1)}) custom-call(s32[2,128]{1,0:T(2,128)S(1)} %shard_map.122.refs_0_, bf16[640,512]{1,0:T(8,128)(2,1)S(1)} %get-tuple-element.34.refs_1_, bf16[512,64]{1,0:T(8,128)(2,1)S(1)} %get-tuple-element.35.refs_2_, f32[1,64]{1,0:T(1,128)S(1)} %get-tuple-element.62.refs_3_, ...), custom_call_target="tpu_custom_call" | custom-call | flops 67108864 | bytes 1048576 | tf_op jit(solution)/shard_map/pallas_call | solution.py:373
  (1 shorter events, 0.0 us)
Async XLA Ops:
  1.6 3.2 %collective-permute-start = (bf16[256,512]{1,0:T(8,128)(2,1)S(1)}, bf16[256,512]{1,0:T(8,128)(2,1)S(1)}, u32[]{:S(2)}, u32[]{:S(2)}) collective-permute-start(bf16[256,512]{1,0:T(8,128)(2,1)S(1)} %shard_map.124.refs_5_), channel_id=1, source_target_pairs={{0,1},{1,0},{2,3},{3,2},{4,5},{5,4},{6,7},{7,6},{8,9},{9,8},{10,11... | collective-permute-start | bytes 786440 | tf_op jit(solution)/shard_map/ppermute | solution.py:314
  2.2 6.7 %collective-permute-start.1 = (bf16[256,512]{1,0:T(8,128)(2,1)S(1)}, bf16[256,512]{1,0:T(8,128)(2,1)S(1)}, u32[]{:S(2)}, u32[]{:S(2)}) collective-permute-start(bf16[256,512]{1,0:T(8,128)(2,1)S(1)} %shard_map.124.refs_5_), channel_id=1, source_target_pairs={{0,5},{1,2},{2,7},{3,0},{4,1},{5,8},{6,3},{7,10},{8,13},{9,4},{10,... | collective-permute-start | bytes 786440 | tf_op jit(solution)/shard_map/ppermute | solution.py:314
  4.9 6.8 %collective-permute-start.3 = (bf16[256,512]{1,0:T(8,128)(2,1)S(1)}, bf16[256,512]{1,0:T(8,128)(2,1)S(1)}, u32[]{:S(2)}, u32[]{:S(2)}) collective-permute-start(bf16[256,512]{1,0:T(8,128)(2,1)S(1)} %collective-permute-done.refs_6_), channel_id=1, source_target_pairs={{0,5},{1,2},{2,7},{3,0},{4,1},{5,8},{6,3},{7,10},{8,13},{9,4},{10,... | collective-permute-start | bytes 786440 | tf_op jit(solution)/shard_map/ppermute | solution.py:314
  8.9 6.1 %collective-permute-start.5 = (bf16[256,512]{1,0:T(8,128)(2,1)S(1)}, bf16[256,512]{1,0:T(8,128)(2,1)S(1)}, u32[]{:S(2)}, u32[]{:S(2)}) collective-permute-start(bf16[256,512]{1,0:T(8,128)(2,1)S(1)} %collective-permute-done.1.refs_7_), channel_id=1, source_target_pairs={{0,5},{1,2},{2,7},{3,0},{4,1},{5,8},{6,3},{7,10},{8,13},{9,4},{10,... | collective-permute-start | bytes 786440 | tf_op jit(solution)/shard_map/ppermute | solution.py:314
  11.7 6.1 %collective-permute-start.7 = (bf16[256,512]{1,0:T(8,128)(2,1)S(1)}, bf16[256,512]{1,0:T(8,128)(2,1)S(1)}, u32[]{:S(2)}, u32[]{:S(2)}) collective-permute-start(bf16[256,512]{1,0:T(8,128)(2,1)S(1)} %collective-permute-done.3.refs_7_), channel_id=1, source_target_pairs={{0,5},{1,2},{2,7},{3,0},{4,1},{5,8},{6,3},{7,10},{8,13},{9,4},{10,... | collective-permute-start | bytes 786440 | tf_op jit(solution)/shard_map/ppermute | solution.py:314
  15.0 6.1 %collective-permute-start.9 = (bf16[256,512]{1,0:T(8,128)(2,1)S(1)}, bf16[256,512]{1,0:T(8,128)(2,1)S(1)}, u32[]{:S(2)}, u32[]{:S(2)}) collective-permute-start(bf16[256,512]{1,0:T(8,128)(2,1)S(1)} %collective-permute-done.5.refs_7_), channel_id=1, source_target_pairs={{0,5},{1,2},{2,7},{3,0},{4,1},{5,8},{6,3},{7,10},{8,13},{9,4},{10,... | collective-permute-start | bytes 786440 | tf_op jit(solution)/shard_map/ppermute | solution.py:314
  17.1 6.1 %collective-permute-start.2 = (bf16[256,512]{1,0:T(8,128)(2,1)S(1)}, bf16[256,512]{1,0:T(8,128)(2,1)S(1)}, u32[]{:S(2)}, u32[]{:S(2)}) collective-permute-start(bf16[256,512]{1,0:T(8,128)(2,1)S(1)} %collective-permute-done.1.refs_7_), channel_id=1, source_target_pairs={{0,1},{1,0},{2,3},{3,2},{4,5},{5,4},{6,7},{7,6},{8,9},{9,8},{10,11... | collective-permute-start | bytes 786440 | tf_op jit(solution)/shard_map/ppermute | solution.py:314
  17.1 6.6 %collective-permute-start.4 = (bf16[256,512]{1,0:T(8,128)(2,1)S(1)}, bf16[256,512]{1,0:T(8,128)(2,1)S(1)}, u32[]{:S(2)}, u32[]{:S(2)}) collective-permute-start(bf16[256,512]{1,0:T(8,128)(2,1)S(1)} %collective-permute-done.3.refs_7_), channel_id=1, source_target_pairs={{0,1},{1,0},{2,3},{3,2},{4,5},{5,4},{6,7},{7,6},{8,9},{9,8},{10,11... | collective-permute-start | bytes 786440 | tf_op jit(solution)/shard_map/ppermute | solution.py:314
  17.8 6.1 %collective-permute-start.11 = (bf16[256,512]{1,0:T(8,128)(2,1)S(1)}, bf16[256,512]{1,0:T(8,128)(2,1)S(1)}, u32[]{:S(2)}, u32[]{:S(2)}) collective-permute-start(bf16[256,512]{1,0:T(8,128)(2,1)S(1)} %collective-permute-done.7.refs_7_), channel_id=1, source_target_pairs={{0,5},{1,2},{2,7},{3,0},{4,1},{5,8},{6,3},{7,10},{8,13},{9,4},{10,... | collective-permute-start | bytes 786440 | tf_op jit(solution)/shard_map/ppermute | solution.py:314
  21.1 6.1 %collective-permute-start.13 = (bf16[256,512]{1,0:T(8,128)(2,1)S(1)}, bf16[256,512]{1,0:T(8,128)(2,1)S(1)}, u32[]{:S(2)}, u32[]{:S(2)}) collective-permute-start(bf16[256,512]{1,0:T(8,128)(2,1)S(1)} %collective-permute-done.9.refs_7_), channel_id=1, source_target_pairs={{0,5},{1,2},{2,7},{3,0},{4,1},{5,8},{6,3},{7,10},{8,13},{9,4},{10,... | collective-permute-start | bytes 786440 | tf_op jit(solution)/shard_map/ppermute | solution.py:314
  23.1 10.8 %collective-permute-start.6 = (bf16[256,512]{1,0:T(8,128)(2,1)S(1)}, bf16[256,512]{1,0:T(8,128)(2,1)S(1)}, u32[]{:S(2)}, u32[]{:S(2)}) collective-permute-start(bf16[256,512]{1,0:T(8,128)(2,1)S(1)} %collective-permute-done.5.refs_7_), channel_id=1, source_target_pairs={{0,1},{1,0},{2,3},{3,2},{4,5},{5,4},{6,7},{7,6},{8,9},{9,8},{10,11... | collective-permute-start | bytes 786440 | tf_op jit(solution)/shard_map/ppermute | solution.py:314
  23.2 11.9 %collective-permute-start.8 = (bf16[256,512]{1,0:T(8,128)(2,1)S(1)}, bf16[256,512]{1,0:T(8,128)(2,1)S(1)}, u32[]{:S(2)}, u32[]{:S(2)}) collective-permute-start(bf16[256,512]{1,0:T(8,128)(2,1)S(1)} %collective-permute-done.7.refs_7_), channel_id=1, source_target_pairs={{0,1},{1,0},{2,3},{3,2},{4,5},{5,4},{6,7},{7,6},{8,9},{9,8},{10,11... | collective-permute-start | bytes 786440 | tf_op jit(solution)/shard_map/ppermute | solution.py:314
  23.7 12.6 %collective-permute-start.10 = (bf16[256,512]{1,0:T(8,128)(2,1)S(1)}, bf16[256,512]{1,0:T(8,128)(2,1)S(1)}, u32[]{:S(2)}, u32[]{:S(2)}) collective-permute-start(bf16[256,512]{1,0:T(8,128)(2,1)S(1)} %collective-permute-done.9.refs_7_), channel_id=1, source_target_pairs={{0,1},{1,0},{2,3},{3,2},{4,5},{5,4},{6,7},{7,6},{8,9},{9,8},{10,11... | collective-permute-start | bytes 786440 | tf_op jit(solution)/shard_map/ppermute | solution.py:314
  23.9 14.2 %collective-permute-start.12 = (bf16[256,512]{1,0:T(8,128)(2,1)S(1)}, bf16[256,512]{1,0:T(8,128)(2,1)S(1)}, u32[]{:S(2)}, u32[]{:S(2)}) collective-permute-start(bf16[256,512]{1,0:T(8,128)(2,1)S(1)} %collective-permute-done.11.refs_9_), channel_id=1, source_target_pairs={{0,1},{1,0},{2,3},{3,2},{4,5},{5,4},{6,7},{7,6},{8,9},{9,8},{10,11... | collective-permute-start | bytes 786440 | tf_op jit(solution)/shard_map/ppermute | solution.py:314
  27.1 12.0 %collective-permute-start.14 = (bf16[256,512]{1,0:T(8,128)(2,1)S(1)}, bf16[256,512]{1,0:T(8,128)(2,1)S(1)}, u32[]{:S(2)}, u32[]{:S(2)}) collective-permute-start(bf16[256,512]{1,0:T(8,128)(2,1)S(1)} %collective-permute-done.13.refs_8_), channel_id=1, source_target_pairs={{0,1},{1,0},{2,3},{3,2},{4,5},{5,4},{6,7},{7,6},{8,9},{9,8},{10,11... | collective-permute-start | bytes 786440 | tf_op jit(solution)/shard_map/ppermute | solution.py:314
